TPU v7x, 512 devices: a whole 4x4x16 slice. The times are simulated.
512 devices in a mesh: trainer: 32 (over z_hi, x, y), depth: 16 (over z_lo, core).
Axes of the slice: x: 4, y: 4, z: 16 (z_hi: 2, z_lo: 8; z = z_hi * 8 + z_lo), core: 2. Of those that a mesh axis runs over, the one named last changes fastest.
Arguments:
- noise: bfloat16 [32, 64, 64, 256], P('trainer', 'depth'), may hold values from -6 to 6
- gen_weight: float32 [32, 331776], P('trainer', 'depth'), may hold values from -0.15625 to 0.15625
- gen_momentum: float32 [32, 331776], P('trainer', 'depth'), may hold values from -6 to 6
- disc_weight: bfloat16 [32, 8, 128, 64], P('trainer'), may hold values from -0.25 to 0.25
- score_weight: float32 [32, 128], P('trainer'), may hold values from -0.5 to 0.5
- pairing: int32 [32], replicated, may hold values from 0 to 31, as said below
- flags: int32 [32], replicated, may hold values from 0 to 1, as said below
Outputs:
- generated: bfloat16 [32, 64, 64, 256], P('trainer', 'depth')
- new_weight: float32 [32, 331776], P('trainer', 'depth')
- new_momentum: float32 [32, 331776], P('trainer', 'depth')
Inputs may be any that keep to these rules, and one draw needn't show every extreme that they name: pairing is a perfect matching: pairing[pairing[i]] == i and pairing[i] != i for every trainer. `flags`: in every matched pair exactly one trainer has flag 1.
All inputs are finite; a program needn't handle non-finite values.
Results may differ from a plain program's by a relative error of at most 0.013.
Values may be sent and summed in bfloat16 or wider, within the bound.
No kernel may reach another device: no remote copies, remote signals or barrier semaphores. Data moves between devices by JAX's collectives and lax.ppermute only.
A program may use at most 64 MiB of HBM per device.

v0:
```python
import jax
import jax.numpy as jnp
from jax import lax
from jax.sharding import PartitionSpec as P

Y = 2
X = 128


momentum_decay = 0.9
step_length = 0.01


def extended(block, sides, width):
    for axis, dim in sides:
        count = lax.axis_size(axis)
        forward = [(i, i + 1) for i in range(count - 1)]
        backward = [(target, source) for source, target in forward]
        low = lax.ppermute(
            lax.slice_in_dim(block, block.shape[dim] - width, None, axis=dim), axis, forward
        )
        high = lax.ppermute(lax.slice_in_dim(block, 0, width, axis=dim), axis, backward)
        block = jnp.concatenate([low, block, high], axis=dim)
    return block


def framed_copies(padded):
    breadth = X
    cells = padded.shape[2]
    framed = jnp.pad(padded, ((0, 0), (0, 0), (breadth + 1, breadth + 1)))
    column = (jnp.arange(cells + 2 * breadth + 2, dtype=jnp.int32) - breadth - 1) % breadth
    left_copy = jnp.where(
        (column == breadth - 1)[None, None, :], jnp.zeros((), framed.dtype), framed
    )
    right_copy = jnp.where((column == 0)[None, None, :], jnp.zeros((), framed.dtype), framed)
    return (left_copy, framed, right_copy)


def stacked_window(copies, read_y, cells):
    breadth = X
    parts_list = []
    for read_x in range(3):
        begin = read_y * breadth + read_x
        parts_list.append(copies[read_x][:, :, begin : begin + cells])
    return jnp.concatenate(parts_list, axis=1)


def group_kernel(layer):
    channels = layer.shape[-1]
    cube = layer.reshape(3, 3, 3, channels, channels)
    return cube.transpose(0, 1, 3, 2, 4).reshape(3, 3, channels, 3 * channels)


def flip_kernel(layer):
    channels = layer.shape[-1]
    cube = layer.reshape(3, 3, 3, channels, channels)[::-1, ::-1, ::-1].swapaxes(3, 4)
    return cube.transpose(0, 1, 3, 2, 4).reshape(3, 3, channels, 3 * channels)


def convolve_grouped(padded, grouped):
    planes, cells = (padded.shape[0] - 2, padded.shape[2])
    copies = framed_copies(padded)
    summed = jnp.zeros((planes, grouped.shape[2], cells), jnp.float32)
    for read_y in range(3):
        window = stacked_window(copies, read_y, cells)
        for read_z in range(3):
            summed = summed + jnp.einsum(
                "oj,zjs->zos",
                grouped[read_z, read_y],
                window[read_z : read_z + planes],
                preferred_element_type=jnp.float32,
            )
    return summed


def convolve(padded, layer):
    return convolve_grouped(padded, group_kernel(layer))


def convolve_back(padded, layer):
    return convolve_grouped(padded, flip_kernel(layer))


def kernel_grad(gradient, padded):
    planes, channels_out, cells = gradient.shape
    channels_in = padded.shape[1]
    copies = framed_copies(padded)
    rows_list = []
    for read_z in range(3):
        row_list = []
        for read_y in range(3):
            window = stacked_window(copies, read_y, cells)
            row_list.append(
                jnp.einsum(
                    "zos,zjs->oj",
                    gradient,
                    window[read_z : read_z + planes],
                    preferred_element_type=jnp.float32,
                )
            )
        rows_list.append(jnp.stack(row_list))
    grouped = jnp.stack(rows_list)
    return (
        grouped.reshape(3, 3, channels_out, 3, channels_in)
        .transpose(0, 1, 3, 2, 4)
        .reshape(27, channels_out, channels_in)
    )


def gelu_back(inputs, upstream):
    return jax.vjp(jax.nn.gelu, inputs)[1](upstream)[0]


def widen_back(gradient):
    return extended(gradient, (("depth", 0),), 1)


def widen_forward(volume):
    return extended(volume, (("depth", 0),), 1)


def critic_grad(generated, disc_kernel, score_vector):
    planes, channels, cells = generated.shape
    blocks = generated.reshape(planes // 2, 2, channels, Y // 2, 2, X // 2, 2)
    kernel_cube = disc_kernel.reshape(2, 2, 2, disc_kernel.shape[1], channels)
    response = jnp.einsum(
        "abdoc,zacybxd->zoyx", kernel_cube, blocks, preferred_element_type=jnp.float32
    )
    features = jax.nn.gelu(response)
    scores = jnp.sum(score_vector[None, :, None, None] * features, axis=1)
    slope = -jax.nn.sigmoid(-scores)
    upstream = gelu_back(response, slope[:, None] * score_vector[None, :, None, None]).astype(
        jnp.bfloat16
    )
    spread = jnp.einsum(
        "abdoc,zoyx->zacybxd", kernel_cube, upstream, preferred_element_type=jnp.float32
    )
    return spread.reshape(planes, channels, cells)


def on_device(noise, gen_weight, gen_momentum, disc_weight, score_weight, pairing, flags):
    trainer_rank = lax.axis_index("trainer")
    partner = pairing[trainer_rank]
    keeper = flags[trainer_rank] == 1
    pieces_in = (
        lax.all_gather(gen_weight.astype(jnp.bfloat16), "trainer", axis=0, tiled=True).astype(
            jnp.float32
        ),
        lax.all_gather(gen_momentum.astype(jnp.bfloat16), "trainer", axis=0, tiled=True).astype(
            jnp.float32
        ),
    )
    row_ids = jnp.arange(pieces_in[0].shape[0], dtype=jnp.int32)
    matched = (row_ids == partner)[:, None]
    weight_part = jnp.sum(jnp.where(matched, pieces_in[0], 0.0), axis=0, keepdims=True)
    moment_part = jnp.sum(jnp.where(matched, pieces_in[1], 0.0), axis=0, keepdims=True)
    other_weight = jnp.zeros_like(gen_weight) + weight_part
    other_moment = jnp.zeros_like(gen_momentum) + moment_part
    chosen_weight = jnp.where(keeper, gen_weight, other_weight)
    chosen_momentum = jnp.where(keeper, gen_momentum, other_moment)
    channels = noise.shape[2]
    all_kernels = lax.all_gather(chosen_weight.astype(jnp.bfloat16), "depth", axis=1, tiled=True)
    layers = all_kernels.reshape(3, 27, channels, channels)
    latent = noise[0]
    latent_pad = widen_forward(latent)
    first_pre = convolve(latent_pad, layers[0])
    first_act_pad = widen_forward(jax.nn.gelu(first_pre).astype(jnp.bfloat16))
    second_pre = convolve(first_act_pad, layers[1])
    second_act_pad = widen_forward(jax.nn.gelu(second_pre).astype(jnp.bfloat16))
    third_pre = convolve(second_act_pad, layers[2])
    output_f = jnp.tanh(third_pre)
    generated = output_f.astype(jnp.bfloat16)
    gen_grad = critic_grad(generated, disc_weight[0], score_weight[0])
    third_grad = (gen_grad * (1.0 - output_f * output_f)).astype(jnp.bfloat16)
    grad_three = kernel_grad(third_grad, second_act_pad)
    second_back = convolve_back(widen_back(third_grad), layers[2])
    second_grad = gelu_back(second_pre, second_back).astype(jnp.bfloat16)
    grad_two = kernel_grad(second_grad, first_act_pad)
    first_back = convolve_back(widen_back(second_grad), layers[1])
    first_grad = gelu_back(first_pre, first_back).astype(jnp.bfloat16)
    grad_one = kernel_grad(first_grad, latent_pad)
    local_grad = jnp.concatenate(
        [grad_one.reshape(-1), grad_two.reshape(-1), grad_three.reshape(-1)]
    )
    share_len = gen_weight.shape[1]
    grad_whole = lax.psum(local_grad.astype(jnp.bfloat16), "depth").astype(jnp.float32)
    grad_share = lax.dynamic_slice_in_dim(
        grad_whole, lax.axis_index("depth") * share_len, share_len, 0
    )
    new_momentum = momentum_decay * chosen_momentum + grad_share[None, :]
    new_weight = chosen_weight - step_length * new_momentum
    return (generated[None], new_weight, new_momentum)


def solution(mesh):
    placed = (
        P("trainer", "depth", None, None),
        P("trainer", "depth"),
        P("trainer", "depth"),
        P("trainer", None, None, None),
        P("trainer", None),
        P(),
        P(),
    )
    return jax.shard_map(
        on_device,
        mesh=mesh,
        in_specs=placed,
        out_specs=(P("trainer", "depth", None, None), P("trainer", "depth"), P("trainer", "depth")),
        check_vma=False,
    )
```

profile of v0, /device:TPU:1, one launch (start us, length us, event | category | flops | bytes accessed | tf_op | source)
XLA Modules:
  0.0 621.0 jit_solution(14482769151043284614)
XLA Ops:
  7.2 1.6 convert_bitcast_fusion.1
  8.9 1.6 convert_bitcast_fusion
  10.6 0.8 slice_bitcast_fusion.91
  11.4 4.9 collective-permute-start
  16.3 5.1 collective-permute-start.1
  21.4 1.2 dynamic_slice.10
  22.7 0.7 iota_compare_fusion.2
  23.4 1.2 dynamic_slice.9
  25.3 1.1 broadcast_select_fusion.9
  27.0 0.9 pad_maximum_fusion.3
  27.9 0.9 pad_maximum_fusion.2
  28.7 124.7 %all-gather.5.cloned.1.call-done = bf16[32,1,20736]{2,1,0:T(2,128)(2,1)} async-done(((bf16[1,1,20736]{2,1,0:T(2,128)(2,1)}), bf16[32,1,20736]{2,1,0:T(2,128)(2,1)}) %all-gather.5.cloned.1.call-update) | async-done | bytes 1327120 | tf_op jit(solution)/shard_map/all_gather | solution.py:146
  153.4 4.5 convert_element_type.63
  157.9 131.5 %all-gather.7.cloned.1.call-done = bf16[32,1,20736]{2,1,0:T(2,128)(2,1)} async-done(((bf16[1,1,20736]{2,1,0:T(2,128)(2,1)}), bf16[32,1,20736]{2,1,0:T(2,128)(2,1)}) %all-gather.7.cloned.1.call-update) | async-done | bytes 1327120 | tf_op jit(solution)/shard_map/all_gather | solution.py:149
  289.4 3.2 fusion.1
  293.2 39.0 %all_gather.10 = bf16[1,331776]{1,0:T(2,128)(2,1)S(1)} all-gather(bf16[1,20736]{1,0:T(2,128)(2,1)S(1)} %fusion.167), channel_id=1, replica_groups=mesh['trainer'=32,'depth'=16] {'depth'}, dimensions={1}, use_global_device_ids=true | all-gather | bytes 705024 | tf_op jit(solution)/shard_map/all_gather | solution.py:162
  332.2 4.4 slice_reduce_fusion.2
  339.9 1.0 multiply_convert_fusion.1
  340.9 1.9 collective-permute-start.2
  342.8 2.6 collective-permute-start.3
  345.6 1.0 copy.109
  346.6 1.4 collective-permute-done.3
  348.9 0.7 copy-done.12
  351.5 1.0 multiply_convert_fusion
  352.5 1.9 collective-permute-start.4
  354.4 2.4 collective-permute-start.5
  356.8 1.8 rev.7
  358.6 1.9 reshape_squeeze.16
  360.5 1.8 rev.6
  362.4 2.0 copy.119
  365.3 0.7 copy-done.13
  368.6 0.7 convert_bitcast_fusion.3
  369.3 0.8 copy.130
  370.1 1.3 multiply_reduce_fusion
  371.7 1.2 copy.132
  373.0 1.9 copy.133
  374.9 1.1 fusion.136
  376.0 1.2 fusion.33
  378.3 0.9 fusion.29
  379.4 0.9 fusion.28
  380.3 0.9 fusion.25
  381.1 0.6 fusion.193
  382.5 0.9 copy.176
  383.3 1.5 copy.172
  384.8 1.5 copy.175
  386.3 3.1 collective-permute-start.6
  389.5 1.9 collective-permute-start.7
  391.4 1.8 maximum_bitcast_fusion.2
  393.2 2.0 copy.181
  395.1 2.0 reshape_reshape.14
  397.1 1.1 broadcast_select_fusion.6
  398.8 0.7 copy-done.15
  400.1 0.8 pad_maximum_fusion.11
  406.4 3.6 collective-permute-start.8
  410.0 2.1 collective-permute-start.9
  412.6 0.9 reshape_reshape.13
  413.5 1.9 collective-permute-done.9
  415.4 1.1 broadcast_select_fusion.5
  417.0 0.7 copy-done.14
  418.4 0.8 pad_maximum_fusion.14
  425.6 0.9 pad_maximum_fusion
  426.5 186.2 %all-reduce.7.cloned.1.call-done = bf16[331776]{0:T(1024)(128)(2,1)} async-done(((bf16[331776]{0:T(1024)(128)(2,1)}), bf16[331776]{0:T(1024)(128)(2,1)}) %all-reduce.7.cloned.1.call-update) | async-done | bytes 663568 | tf_op jit(solution)/shard_map/psum | solution.py:186
  612.6 0.9 dynamic-slice_convert_fusion
  613.6 0.9 multiply_subtract_fusion
  (209 shorter events, 27.5 us)
Async XLA Ops:
  7.2 363.0 %copy-start = (bf16[1,8,128,64]{2,3,1,0:T(8,128)(2,1)S(1)}, bf16[1,8,128,64]{2,3,1,0:T(8,128)(2,1)}, u32[]{:S(2)}) copy-start(bf16[1,8,128,64]{2,3,1,0:T(8,128)(2,1)} %param.10) | copy-start | bytes 393220
  7.2 146.2 %all-gather.5.cloned.1.call-start = ((), (), s32[]{:S(2)}) async-start(), calls=%async_computation.1 | async-start | bytes 2737152 | tf_op jit(solution)/shard_map/all_gather | solution.py:146
  8.9 280.5 %all-gather.7.cloned.1.call-start = ((), (), s32[]{:S(2)}) async-start(), calls=%async_computation.2 | async-start | bytes 2737152 | tf_op jit(solution)/shard_map/all_gather | solution.py:149
  10.5 602.1 %all-reduce.7.cloned.1.call-start = ((), (), s32[]{:S(2)}) async-start(), calls=%async_computation | async-start | bytes 1327104 | tf_op jit(solution)/shard_map/psum | solution.py:186
  11.4 13.9 %collective-permute-start = (bf16[1,64,256]{2,1,0:T(8,128)(2,1)S(1)}, bf16[1,64,256]{2,1,0:T(8,128)(2,1)S(1)}, u32[]{:S(2)}, u32[]{:S(2)}) collective-permute-start(bf16[1,64,256]{2,1,0:T(8,128)(2,1)S(1)} %get-tuple-element.73), channel_id=1, source_target_pairs={{0,1},{1,2},{2,3},{3,4},{4,5},{5,6},{6,7},{7,8},{8,9},{9,10},{10,1... | collective-permute-start | bytes 98312 | tf_op jit(solution)/shard_map/ppermute | solution.py:19
  16.3 9.0 %collective-permute-start.1 = (bf16[1,64,256]{2,1,0:T(8,128)(2,1)S(1)}, bf16[1,64,256]{2,1,0:T(8,128)(2,1)S(1)}, u32[]{:S(2)}, u32[]{:S(2)}) collective-permute-start(bf16[1,64,256]{2,1,0:T(8,128)(2,1)S(1)} %get-tuple-element.74), channel_id=1, source_target_pairs={{1,0},{2,1},{3,2},{4,3},{5,4},{6,5},{7,6},{8,7},{9,8},{10,9},{11,1... | collective-permute-start | bytes 98312 | tf_op jit(solution)/shard_map/ppermute | solution.py:22
  22.7 341.7 %copy-start.27 = (pred[514]{0:T(1024)(128)(4,1)}, pred[514]{0:T(1024)(128)(4,1)S(1)}, u32[]{:S(2)}) copy-start(pred[514]{0:T(1024)(128)(4,1)S(1)} %broadcast_compare_fusion.1) | copy-start | bytes 1546
  22.7 341.7 %copy-start.29 = (pred[514]{0:T(1024)(128)(4,1)}, pred[514]{0:T(1024)(128)(4,1)S(1)}, u32[]{:S(2)}) copy-start(pred[514]{0:T(1024)(128)(4,1)S(1)} %broadcast_compare_fusion) | copy-start | bytes 1546
  26.9 0.9 copy-start.18
  157.9 134.7 %copy-start.21 = (f32[1,20736]{1,0:T(1,128)S(1)}, f32[1,20736]{1,0:T(1,128)}, u32[]{:S(2)}) copy-start(f32[1,20736]{1,0:T(1,128)} %param.8) | copy-start | bytes 248836
  292.6 0.6 copy-start.19
  337.1 1.1 copy-start.2
  338.4 1.1 copy-start.1
  340.9 5.7 collective-permute-start.2
  342.8 5.2 collective-permute-start.3
  345.6 3.3 copy-start.11
  348.6 1.0 copy-start.12
  351.0 1.4 copy-start.3
  352.5 11.8 %collective-permute-start.4 = (bf16[1,64,256]{2,1,0:T(8,128)(2,1)S(1)}, bf16[1,64,256]{2,1,0:T(8,128)(2,1)S(1)}, u32[]{:S(2)}, u32[]{:S(2)}) collective-permute-start(bf16[1,64,256]{2,1,0:T(8,128)(2,1)S(1)} %get-tuple-element.69), channel_id=1, source_target_pairs={{0,1},{1,2},{2,3},{3,4},{4,5},{5,6},{6,7},{7,8},{8,9},{9,10},{10,1... | collective-permute-start | bytes 98312 | tf_op jit(solution)/shard_map/ppermute | solution.py:19
  354.4 9.9 %collective-permute-start.5 = (bf16[1,64,256]{2,1,0:T(8,128)(2,1)S(1)}, bf16[1,64,256]{2,1,0:T(8,128)(2,1)S(1)}, u32[]{:S(2)}, u32[]{:S(2)}) collective-permute-start(bf16[1,64,256]{2,1,0:T(8,128)(2,1)S(1)} %get-tuple-element.70), channel_id=1, source_target_pairs={{1,0},{2,1},{3,2},{4,3},{5,4},{6,5},{7,6},{8,7},{9,8},{10,9},{11,1... | collective-permute-start | bytes 98312 | tf_op jit(solution)/shard_map/ppermute | solution.py:22
  364.9 1.0 copy-start.13
  365.3 1.4 copy-start.5
  366.7 0.8 copy-start.7
  367.5 0.8 copy-start.9
  368.4 1.8 copy-start.31
  374.9 2.4 copy-start.8
  374.9 2.6 copy-start.6
  374.9 2.9 copy-start.10
  386.3 10.8 %collective-permute-start.6 = (bf16[1,64,256]{2,1,0:T(8,128)(2,1)}, bf16[1,64,256]{2,1,0:T(8,128)(2,1)}, u32[]{:S(2)}, u32[]{:S(2)}) collective-permute-start(bf16[1,64,256]{2,1,0:T(8,128)(2,1)} %get-tuple-element.67), channel_id=1, source_target_pairs={{0,1},{1,2},{2,3},{3,4},{4,5},{5,6},{6,7},{7,8},{8,9},{9,10},{10,1... | collective-permute-start | bytes 98312 | tf_op jit(solution)/shard_map/ppermute | solution.py:19
  389.5 7.6 %collective-permute-start.7 = (bf16[1,64,256]{2,1,0:T(8,128)(2,1)}, bf16[1,64,256]{2,1,0:T(8,128)(2,1)}, u32[]{:S(2)}, u32[]{:S(2)}) collective-permute-start(bf16[1,64,256]{2,1,0:T(8,128)(2,1)} %get-tuple-element.68), channel_id=1, source_target_pairs={{1,0},{2,1},{3,2},{4,3},{5,4},{6,5},{7,6},{8,7},{9,8},{10,9},{11,1... | collective-permute-start | bytes 98312 | tf_op jit(solution)/shard_map/ppermute | solution.py:22
  393.2 4.0 copy-start.28
  393.2 4.0 copy-start.30
  398.5 1.0 copy-start.15
  401.7 1.0 copy-start.26
  401.9 1.1 copy-start.4
  406.4 7.1 %collective-permute-start.8 = (bf16[1,64,256]{2,1,0:T(8,128)(2,1)S(1)}, bf16[1,64,256]{2,1,0:T(8,128)(2,1)S(1)}, u32[]{:S(2)}, u32[]{:S(2)}) collective-permute-start(bf16[1,64,256]{2,1,0:T(8,128)(2,1)S(1)} %get-tuple-element.65), channel_id=1, source_target_pairs={{0,1},{1,2},{2,3},{3,4},{4,5},{5,6},{6,7},{7,8},{8,9},{9,10},{10,1... | collective-permute-start | bytes 98312 | tf_op jit(solution)/shard_map/ppermute | solution.py:19
  410.0 5.3 collective-permute-start.9
  416.7 1.0 copy-start.14
  419.9 1.0 copy-start.25
  424.5 0.9 copy-start.16
  424.5 1.0 copy-start.17
  425.5 188.0 %copy-start.20 = (f32[20736]{0:T(1024)S(1)}, f32[20736]{0:T(1024)}, u32[]{:S(2)}) copy-start(f32[20736]{0:T(1024)} %copy-done.19) | copy-start | bytes 248836
  425.5 188.0 %copy-start.22 = (f32[1,20736]{1,0:T(1,128)S(1)}, f32[1,20736]{1,0:T(1,128)}, u32[]{:S(2)}) copy-start(f32[1,20736]{1,0:T(1,128)} %param.8) | copy-start | bytes 248836
  425.6 188.0 %copy-start.23 = (f32[20736]{0:T(1024)S(1)}, f32[20736]{0:T(1024)}, u32[]{:S(2)}) copy-start(f32[20736]{0:T(1024)} %get-tuple-element.6) | copy-start | bytes 248836
  425.6 188.0 %copy-start.24 = (f32[1,20736]{1,0:T(1,128)S(1)}, f32[1,20736]{1,0:T(1,128)}, u32[]{:S(2)}) copy-start(f32[1,20736]{1,0:T(1,128)} %param.9) | copy-start | bytes 248836
Sparse Core Ops, SparseCore 0:
  12.8 140.5 all-gather.4
  158.2 131.0 all-gather.6
  426.6 186.0 all-reduce.6
where the time goes:
time: 623 us; the launch traced here: 621 us
  waiting for transfers between devices  446 us (72%)
  local copies, waits for them, and re-layouts  42.4 us (7%)
  blocking collectives  39 us (6%)
  starting transfers between devices  29.8 us (5%)
  other arithmetic  25.9 us (4%)
  matrix products  22.7 us (4%)
  between operations  15.6 us (3%)
    psum x1, waiting for transfers between devices, on_device(): lax.psum(local_grad.astype(jnp.bfloat16), 'depth').astype(jnp.float32)  186 us
    all_gather x1, waiting for transfers between devices, on_device(): lax.all_gather(gen_momentum.astype(jnp.bfloat16), 'trainer', axis=0, tile...  131 us
    all_gather x1, waiting for transfers between devices, on_device(): lax.all_gather(gen_weight.astype(jnp.bfloat16), 'trainer', axis=0, tiled=...  125 us
    all_gather x1, blocking collectives, on_device(): lax.all_gather(chosen_weight.astype(jnp.bfloat16), 'depth', axis=1, tiled...  39 us
    ppermute x5, starting transfers between devices, extended(): lax.ppermute(lax.slice_in_dim(block, block.shape[dim] - width, None, axis...  15.5 us
    ppermute x5, starting transfers between devices, extended(): lax.ppermute(lax.slice_in_dim(block, 0, width, axis=dim), axis, backward)  14.2 us
  transfers between devices with their start and end apart: 13, of which 5 were waited for; matrix products, arithmetic and copies ran while one was open for 5% of the time, Pallas kernels for 0%

commit v1 on v0

--- a/solution.py
+++ b/solution.py
@@ -138,29 +138,73 @@
     return spread.reshape(planes, channels, cells)
 
 
+def move(value, axis, target_of):
+    count = lax.axis_size(axis)
+    return lax.ppermute(value, axis, [(i, target_of(i)) for i in range(count)])
+
+
+def fetch_partner(value, pairing):
+    rank = lax.axis_index("trainer")
+    half, row, col = rank // 16, (rank // 4) % 4, rank % 4
+    across = move(value, "trainer", lambda i: i ^ 16)
+    low = half == 0
+    both = jnp.stack([jnp.where(low, value, across), jnp.where(low, across, value)])
+    held = [both]
+    for shift in range(1, 4):
+        held.append(move(both, "trainer", lambda i: (i // 4) * 4 + (i + shift) % 4))
+    held = jnp.concatenate(held)
+    fetched = value
+    own_source = pairing[rank]
+    for shift in range(4):
+        target = half * 16 + ((row + shift) % 4) * 4 + col
+        source = pairing[target]
+        slot = ((col - source % 4) % 4) * 2 + source // 16
+        message = lax.dynamic_index_in_dim(held, slot, 0, keepdims=False)
+        if shift:
+            message = move(
+                message, "trainer", lambda i: (i // 16) * 16 + (i + 4 * shift) % 16
+            )
+        here = (row - (own_source // 4) % 4) % 4 == shift
+        fetched = jnp.where(here, message, fetched)
+    return fetched
+
+
+def gather_depth(block):
+    rank = lax.axis_index("depth")
+    shape = block.shape
+    for mask in (8, 4, 2, 1):
+        got = move(block, "depth", lambda i: i ^ mask)
+        low = (rank & mask) == 0
+        block = jnp.stack([jnp.where(low, block, got), jnp.where(low, got, block)])
+    return block.transpose(3, 2, 1, 0, 4, 5).reshape(-1)
+
+
+def scatter_depth(whole, share):
+    rank = lax.axis_index("depth")
+    held = whole.reshape((2, 2, 2, 2) + share)
+    for axis, mask in ((3, 1), (2, 2), (1, 4), (0, 8)):
+        bit = (rank // mask) % 2
+        sent = lax.dynamic_index_in_dim(held, 1 - bit, axis, keepdims=False)
+        kept = lax.dynamic_index_in_dim(held, bit, axis, keepdims=False)
+        got = move(sent.astype(jnp.bfloat16), "depth", lambda i: i ^ mask)
+        held = kept + got.astype(jnp.float32)
+    return held
+
+
 def on_device(noise, gen_weight, gen_momentum, disc_weight, score_weight, pairing, flags):
-    trainer_rank = lax.axis_index("trainer")
-    partner = pairing[trainer_rank]
-    keeper = flags[trainer_rank] == 1
-    pieces_in = (
-        lax.all_gather(gen_weight.astype(jnp.bfloat16), "trainer", axis=0, tiled=True).astype(
-            jnp.float32
-        ),
-        lax.all_gather(gen_momentum.astype(jnp.bfloat16), "trainer", axis=0, tiled=True).astype(
-            jnp.float32
-        ),
-    )
-    row_ids = jnp.arange(pieces_in[0].shape[0], dtype=jnp.int32)
-    matched = (row_ids == partner)[:, None]
-    weight_part = jnp.sum(jnp.where(matched, pieces_in[0], 0.0), axis=0, keepdims=True)
-    moment_part = jnp.sum(jnp.where(matched, pieces_in[1], 0.0), axis=0, keepdims=True)
-    other_weight = jnp.zeros_like(gen_weight) + weight_part
-    other_moment = jnp.zeros_like(gen_momentum) + moment_part
-    chosen_weight = jnp.where(keeper, gen_weight, other_weight)
-    chosen_momentum = jnp.where(keeper, gen_momentum, other_moment)
+    share = (gen_weight.shape[1] // 128, 128)
+    keeper = flags[lax.axis_index("trainer")] == 1
+    own_weight = gen_weight.reshape(share)
+    own_moment = gen_momentum.reshape(share)
+    other_weight = fetch_partner(own_weight.astype(jnp.bfloat16), pairing)
+    chosen_weight = jnp.where(keeper, own_weight, other_weight.astype(jnp.float32))
+    sent_moment, chosen_weight = lax.optimization_barrier(
+        (own_moment.astype(jnp.bfloat16), chosen_weight)
+    )
+    other_moment = fetch_partner(sent_moment, pairing)
+    chosen_momentum = jnp.where(keeper, own_moment, other_moment.astype(jnp.float32))
     channels = noise.shape[2]
-    all_kernels = lax.all_gather(chosen_weight.astype(jnp.bfloat16), "depth", axis=1, tiled=True)
-    layers = all_kernels.reshape(3, 27, channels, channels)
+    layers = gather_depth(chosen_weight.astype(jnp.bfloat16)).reshape(3, 27, channels, channels)
     latent = noise[0]
     latent_pad = widen_forward(latent)
     first_pre = convolve(latent_pad, layers[0])
@@ -182,13 +226,11 @@
     local_grad = jnp.concatenate(
         [grad_one.reshape(-1), grad_two.reshape(-1), grad_three.reshape(-1)]
     )
-    share_len = gen_weight.shape[1]
-    grad_whole = lax.psum(local_grad.astype(jnp.bfloat16), "depth").astype(jnp.float32)
-    grad_share = lax.dynamic_slice_in_dim(
-        grad_whole, lax.axis_index("depth") * share_len, share_len, 0
-    )
-    new_momentum = momentum_decay * chosen_momentum + grad_share[None, :]
+    grad_share = scatter_depth(local_grad, share)
+    new_momentum = momentum_decay * chosen_momentum + grad_share
     new_weight = chosen_weight - step_length * new_momentum
+    new_momentum = new_momentum.reshape(gen_weight.shape)
+    new_weight = new_weight.reshape(gen_weight.shape)
     return (generated[None], new_weight, new_momentum)
 
 

time: 623 us -> 241 us (0.39)
  the two profiles are of different devices: /device:TPU:1 before, /device:TPU:4 now
where the time goes in v1:
time: 241 us; the launch traced here: 239 us
  starting transfers between devices  115 us (48%)
  local copies, waits for them, and re-layouts  38.7 us (16%)
  waiting for transfers between devices  33.5 us (14%)
  matrix products  20.6 us (9%)
  between operations  16.5 us (7%)
  other arithmetic  14.9 us (6%)
    ppermute x22, starting transfers between devices, move(): return lax.ppermute(value, axis, [(i, target_of(i)) for i in range(count)])  89.8 us
    ppermute x22, waiting for transfers between devices, move(): return lax.ppermute(value, axis, [(i, target_of(i)) for i in range(count)])  33.5 us
    ppermute x5, starting transfers between devices, extended(): lax.ppermute(lax.slice_in_dim(block, block.shape[dim] - width, None, axis...  18.3 us
    dot_general x45, matrix products, convolve_grouped(): jnp.einsum('oj,zjs->zos', grouped[read_z, read_y], window[read_z:read_z +...  11.4 us
    unnamed x90, local copies, waits for them, and re-layouts  8.96 us
    dot_general x27, matrix products, kernel_grad(): jnp.einsum('zos,zjs->oj', gradient, window[read_z:read_z + planes], prefe...  7.62 us
    ppermute x5, starting transfers between devices, extended(): lax.ppermute(lax.slice_in_dim(block, 0, width, axis=dim), axis, backward)  6.41 us
    unnamed x7, other arithmetic  5.35 us
  transfers between devices with their start and end apart: 32, of which 12 were waited for; matrix products, arithmetic and copies ran while one was open for 11% of the time, Pallas kernels for 0%

profile of v1, /device:TPU:4, one launch (start us, length us, event | category | flops | bytes accessed | tf_op | source)
XLA Modules:
  0.0 238.9 jit_solution(13195210693332246994)
XLA Ops:
  1.5 1.3 collective-permute-start.1
  2.8 3.0 %collective-permute-start = (bf16[1,64,256]{2,1,0:T(8,128)(2,1)S(1)}, bf16[1,64,256]{2,1,0:T(8,128)(2,1)S(1)}, u32[]{:S(2)}, u32[]{:S(2)}) collective-permute-start(bf16[1,64,256]{2,1,0:T(8,128)(2,1)S(1)} %get-tuple-element.95), channel_id=1, source_target_pairs={{0,1},{1,2},{2,3},{3,4},{4,5},{5,6},{6,7},{7,8},{8,9},{9,10},{10,1... | collective-permute-start | bytes 98312 | tf_op jit(solution)/shard_map/ppermute | solution.py:19
  5.8 1.1 reduce.2
  6.9 15.7 %collective-permute-start.2 = (bf16[162,128]{1,0:T(8,128)(2,1)S(1)}, bf16[162,128]{1,0:T(8,128)(2,1)S(1)}, u32[]{:S(2)}, u32[]{:S(2)}) collective-permute-start(bf16[162,128]{1,0:T(8,128)(2,1)S(1)} %bitcast_convert_fusion), channel_id=1, source_target_pairs={{0,256},{16,272},{32,288},{48,304},{64,320},{80,336},{96,352},{112... | collective-permute-start | bytes 124424 | tf_op jit(solution)/shard_map/ppermute | solution.py:143
  22.7 1.1 reduce.1
  24.6 1.5 fusion.204
  40.6 3.5 %collective-permute-start.3 = (bf16[2,162,128]{2,1,0:T(8,128)(2,1)S(1)}, bf16[2,162,128]{2,1,0:T(8,128)(2,1)S(1)}, u32[]{:S(2)}, u32[]{:S(2)}) collective-permute-start(bf16[2,162,128]{2,1,0:T(8,128)(2,1)S(1)} %pad_maximum_fusion.18), channel_id=1, source_target_pairs={{0,16},{16,32},{32,48},{48,0},{64,80},{80,96},{96,112},{112,64},{1... | collective-permute-start | bytes 248840 | tf_op jit(solution)/shard_map/ppermute | solution.py:143
  44.4 4.8 %collective-permute-start.4 = (bf16[2,162,128]{2,1,0:T(8,128)(2,1)S(1)}, bf16[2,162,128]{2,1,0:T(8,128)(2,1)S(1)}, u32[]{:S(2)}, u32[]{:S(2)}) collective-permute-start(bf16[2,162,128]{2,1,0:T(8,128)(2,1)S(1)} %pad_maximum_fusion.18), channel_id=1, source_target_pairs={{0,32},{16,48},{32,0},{48,16},{64,96},{80,112},{96,64},{112,80},{1... | collective-permute-start | bytes 248840 | tf_op jit(solution)/shard_map/ppermute | solution.py:143
  49.2 3.3 %collective-permute-start.5 = (bf16[2,162,128]{2,1,0:T(8,128)(2,1)S(1)}, bf16[2,162,128]{2,1,0:T(8,128)(2,1)S(1)}, u32[]{:S(2)}, u32[]{:S(2)}) collective-permute-start(bf16[2,162,128]{2,1,0:T(8,128)(2,1)S(1)} %pad_maximum_fusion.18), channel_id=1, source_target_pairs={{0,48},{16,0},{32,16},{48,32},{64,112},{80,64},{96,80},{112,96},{1... | collective-permute-start | bytes 248840 | tf_op jit(solution)/shard_map/ppermute | solution.py:143
  52.8 3.0 %collective-permute-done.5 = bf16[2,162,128]{2,1,0:T(8,128)(2,1)S(1)} collective-permute-done((bf16[2,162,128]{2,1,0:T(8,128)(2,1)S(1)}, bf16[2,162,128]{2,1,0:T(8,128)(2,1)S(1)}, u32[]{:S(2)}, u32[]{:S(2)}) %collective-permute-start.5) | collective-permute-done | bytes 82976 | tf_op jit(solution)/shard_map/ppermute | solution.py:143
  55.8 2.4 %collective-permute-start.6 = (bf16[162,128]{1,0:T(8,128)(2,1)S(1)}, bf16[162,128]{1,0:T(8,128)(2,1)S(1)}, u32[]{:S(2)}, u32[]{:S(2)}) collective-permute-start(bf16[162,128]{1,0:T(8,128)(2,1)S(1)} %get-tuple-element.73), channel_id=1, source_target_pairs={{0,192},{16,208},{32,224},{48,240},{64,0},{80,16},{96,32},{112,48}... | collective-permute-start | bytes 124424 | tf_op jit(solution)/shard_map/ppermute | solution.py:143
  58.3 4.6 %collective-permute-start.7 = (bf16[162,128]{1,0:T(8,128)(2,1)S(1)}, bf16[162,128]{1,0:T(8,128)(2,1)S(1)}, u32[]{:S(2)}, u32[]{:S(2)}) collective-permute-start(bf16[162,128]{1,0:T(8,128)(2,1)S(1)} %get-tuple-element.72), channel_id=1, source_target_pairs={{0,128},{16,144},{32,160},{48,176},{64,192},{80,208},{96,224},{112... | collective-permute-start | bytes 124424 | tf_op jit(solution)/shard_map/ppermute | solution.py:143
  62.9 1.9 collective-permute-start.8
  65.7 3.1 %collective-permute-done.8 = bf16[162,128]{1,0:T(8,128)(2,1)S(1)} collective-permute-done((bf16[162,128]{1,0:T(8,128)(2,1)S(1)}, bf16[162,128]{1,0:T(8,128)(2,1)S(1)}, u32[]{:S(2)}, u32[]{:S(2)}) %collective-permute-start.8) | collective-permute-done | bytes 41504 | tf_op jit(solution)/shard_map/ppermute | solution.py:143
  68.9 5.3 %collective-permute-start.9 = (bf16[162,128]{1,0:T(8,128)(2,1)S(1)}, bf16[162,128]{1,0:T(8,128)(2,1)S(1)}, u32[]{:S(2)}, u32[]{:S(2)}) collective-permute-start(bf16[162,128]{1,0:T(8,128)(2,1)S(1)} %convert_element_type.84), channel_id=1, source_target_pairs={{0,8},{1,9},{2,10},{3,11},{4,12},{5,13},{6,14},{7,15},{8,0},{9,1},... | collective-permute-start | bytes 124424 | tf_op jit(solution)/shard_map/ppermute | solution.py:143
  74.5 4.3 %collective-permute-done.9 = bf16[162,128]{1,0:T(8,128)(2,1)S(1)} collective-permute-done((bf16[162,128]{1,0:T(8,128)(2,1)S(1)}, bf16[162,128]{1,0:T(8,128)(2,1)S(1)}, u32[]{:S(2)}, u32[]{:S(2)}) %collective-permute-start.9) | collective-permute-done | bytes 41504 | tf_op jit(solution)/shard_map/ppermute | solution.py:143
  78.8 3.4 %collective-permute-start.10 = (bf16[2,162,128]{2,1,0:T(8,128)(2,1)S(1)}, bf16[2,162,128]{2,1,0:T(8,128)(2,1)S(1)}, u32[]{:S(2)}, u32[]{:S(2)}) collective-permute-start(bf16[2,162,128]{2,1,0:T(8,128)(2,1)S(1)} %pad_maximum_fusion.19), channel_id=1, source_target_pairs={{0,4},{1,5},{2,6},{3,7},{4,0},{5,1},{6,2},{7,3},{8,12},{9,13},{10,... | collective-permute-start | bytes 248840 | tf_op jit(solution)/shard_map/ppermute | solution.py:143
  82.2 4.7 %collective-permute-done.10 = bf16[2,162,128]{2,1,0:T(8,128)(2,1)S(1)} collective-permute-done((bf16[2,162,128]{2,1,0:T(8,128)(2,1)S(1)}, bf16[2,162,128]{2,1,0:T(8,128)(2,1)S(1)}, u32[]{:S(2)}, u32[]{:S(2)}) %collective-permute-start.10) | collective-permute-done | bytes 82976 | tf_op jit(solution)/shard_map/ppermute | solution.py:143
  87.0 2.1 collective-permute-start.11
  89.4 5.0 %collective-permute-done.11 = bf16[2,2,162,128]{3,2,1,0:T(8,128)(2,1)S(1)} collective-permute-done((bf16[2,2,162,128]{3,2,1,0:T(8,128)(2,1)S(1)}, bf16[2,2,162,128]{3,2,1,0:T(8,128)(2,1)S(1)}, u32[]{:S(2)}, u32[]{:S(2)}) %collective-permute-start.11) | collective-permute-done | bytes 165920 | tf_op jit(solution)/shard_map/ppermute | solution.py:143
  94.4 1.9 collective-permute-start.12
  96.5 1.5 collective-permute-done.12
  99.0 1.8 reshape_reshape.12
  100.8 1.1 fusion.184
  101.9 1.3 copy.15
  105.0 1.0 multiply_convert_fusion.1
  105.9 1.3 collective-permute-start.14
  107.2 3.0 %collective-permute-start.13 = (bf16[1,64,256]{2,1,0:T(8,128)(2,1)S(1)}, bf16[1,64,256]{2,1,0:T(8,128)(2,1)S(1)}, u32[]{:S(2)}, u32[]{:S(2)}) collective-permute-start(bf16[1,64,256]{2,1,0:T(8,128)(2,1)S(1)} %get-tuple-element.93), channel_id=1, source_target_pairs={{0,1},{1,2},{2,3},{3,4},{4,5},{5,6},{6,7},{7,8},{8,9},{9,10},{10,1... | collective-permute-start | bytes 98312 | tf_op jit(solution)/shard_map/ppermute | solution.py:19
  110.3 2.7 %collective-permute-start.17 = (bf16[162,128]{1,0:T(8,128)(2,1)}, bf16[162,128]{1,0:T(8,128)(2,1)}, u32[]{:S(2)}, u32[]{:S(2)}) collective-permute-start(bf16[162,128]{1,0:T(8,128)(2,1)} %bitcast_convert_fusion.1), channel_id=1, source_target_pairs={{0,256},{16,272},{32,288},{48,304},{64,320},{80,336},{96,352},{112... | collective-permute-start | bytes 124424 | tf_op jit(solution)/shard_map/ppermute | solution.py:143
  113.0 1.0 copy.25
  120.4 1.3 collective-permute-start.16
  121.7 4.2 %collective-permute-start.15 = (bf16[1,64,256]{2,1,0:T(8,128)(2,1)}, bf16[1,64,256]{2,1,0:T(8,128)(2,1)}, u32[]{:S(2)}, u32[]{:S(2)}) collective-permute-start(bf16[1,64,256]{2,1,0:T(8,128)(2,1)} %get-tuple-element.91), channel_id=1, source_target_pairs={{0,1},{1,2},{2,3},{3,4},{4,5},{5,6},{6,7},{7,8},{8,9},{9,10},{10,1... | collective-permute-start | bytes 98312 | tf_op jit(solution)/shard_map/ppermute | solution.py:19
  126.1 1.4 constant_dynamic-update-slice_fusion.9
  127.5 2.0 copy.35
  129.5 1.8 rev.6
  132.1 1.2 broadcast_select_fusion.7
  139.7 1.3 multiply_reduce_fusion
  141.3 1.2 copy.47
  142.5 1.9 copy.48
  144.4 1.1 fusion.135
  145.5 1.3 fusion.36
  149.5 1.3 collective-permute-start.25
  150.8 4.4 %collective-permute-start.24 = (bf16[1,64,256]{2,1,0:T(8,128)(2,1)}, bf16[1,64,256]{2,1,0:T(8,128)(2,1)}, u32[]{:S(2)}, u32[]{:S(2)}) collective-permute-start(bf16[1,64,256]{2,1,0:T(8,128)(2,1)} %get-tuple-element.89), channel_id=1, source_target_pairs={{0,1},{1,2},{2,3},{3,4},{4,5},{5,6},{6,7},{7,8},{8,9},{9,10},{10,1... | collective-permute-start | bytes 98312 | tf_op jit(solution)/shard_map/ppermute | solution.py:19
  155.2 1.0 maximum_bitcast_fusion.2
  156.1 2.4 %copy.96 = f32[3,3,3,64,64]{4,3,2,1,0:T(8,128)} copy(f32[3,3,3,64,64]{3,4,2,1,0:T(8,128)} %maximum_bitcast_fusion.2) | data formatting | bytes 884736 | tf_op jit(solution)/shard_map/transpose | solution.py:105
  158.6 1.3 reshape_reshape.15
  159.9 1.2 broadcast_select_fusion.6
  169.3 1.3 collective-permute-start.27
  170.6 3.7 %collective-permute-start.26 = (bf16[1,64,256]{2,1,0:T(8,128)(2,1)S(1)}, bf16[1,64,256]{2,1,0:T(8,128)(2,1)S(1)}, u32[]{:S(2)}, u32[]{:S(2)}) collective-permute-start(bf16[1,64,256]{2,1,0:T(8,128)(2,1)S(1)} %get-tuple-element.87), channel_id=1, source_target_pairs={{0,1},{1,2},{2,3},{3,4},{4,5},{5,6},{6,7},{7,8},{8,9},{9,10},{10,1... | collective-permute-start | bytes 98312 | tf_op jit(solution)/shard_map/ppermute | solution.py:19
  174.4 1.2 copy.86
  175.6 2.1 reshape_reshape.14
  186.2 3.6 %collective-permute-start.28 = (bf16[2,2,2,162,128]{4,3,2,1,0:T(8,128)(2,1)S(1)}, bf16[2,2,2,162,128]{4,3,2,1,0:T(8,128)(2,1)S(1)}, u32[]{:S(2)}, u32[]{:S(2)}) collective-permute-start(bf16[2,2,2,162,128]{4,3,2,1,0:T(8,128)(2,1)S(1)} %fusion.120), channel_id=1, source_target_pairs={{0,1},{1,0},{2,3},{3,2},{4,5},{5,4},{6,7},{7,6},{8,9},{9,8},{10,11... | collective-permute-start | bytes 995336 | tf_op jit(solution)/shard_map/ppermute | solution.py:143
  190.7 2.3 collective-permute-start.18
  193.1 5.6 %collective-permute-start.19 = (bf16[2,162,128]{2,1,0:T(8,128)(2,1)S(1)}, bf16[2,162,128]{2,1,0:T(8,128)(2,1)S(1)}, u32[]{:S(2)}, u32[]{:S(2)}) collective-permute-start(bf16[2,162,128]{2,1,0:T(8,128)(2,1)S(1)} %pad_maximum_fusion.20), channel_id=1, source_target_pairs={{0,32},{16,48},{32,0},{48,16},{64,96},{80,112},{96,64},{112,80},{1... | collective-permute-start | bytes 248840 | tf_op jit(solution)/shard_map/ppermute | solution.py:143
  198.7 1.9 collective-permute-start.20
  200.8 2.8 %collective-permute-start.29 = (bf16[2,2,162,128]{3,2,1,0:T(8,128)(2,1)S(1)}, bf16[2,2,162,128]{3,2,1,0:T(8,128)(2,1)S(1)}, u32[]{:S(2)}, u32[]{:S(2)}) collective-permute-start(bf16[2,2,162,128]{3,2,1,0:T(8,128)(2,1)S(1)} %fusion.141), channel_id=1, source_target_pairs={{0,2},{1,3},{2,0},{3,1},{4,6},{5,7},{6,4},{7,5},{8,10},{9,11},{10,... | collective-permute-start | bytes 497672 | tf_op jit(solution)/shard_map/ppermute | solution.py:143
  203.7 1.4 collective-permute-done.20
  205.1 3.5 %collective-permute-done.29 = bf16[2,2,162,128]{3,2,1,0:T(8,128)(2,1)S(1)} collective-permute-done((bf16[2,2,162,128]{3,2,1,0:T(8,128)(2,1)S(1)}, bf16[2,2,162,128]{3,2,1,0:T(8,128)(2,1)S(1)}, u32[]{:S(2)}, u32[]{:S(2)}) %collective-permute-start.29) | collective-permute-done | bytes 165920 | tf_op jit(solution)/shard_map/ppermute | solution.py:143
  208.6 7.6 %collective-permute-start.30 = (bf16[2,162,128]{2,1,0:T(8,128)(2,1)S(1)}, bf16[2,162,128]{2,1,0:T(8,128)(2,1)S(1)}, u32[]{:S(2)}, u32[]{:S(2)}) collective-permute-start(bf16[2,162,128]{2,1,0:T(8,128)(2,1)S(1)} %fusion.142), channel_id=1, source_target_pairs={{0,4},{1,5},{2,6},{3,7},{4,0},{5,1},{6,2},{7,3},{8,12},{9,13},{10,... | collective-permute-start | bytes 248840 | tf_op jit(solution)/shard_map/ppermute | solution.py:143
  216.3 2.1 collective-permute-start.21
  218.4 3.8 %collective-permute-start.22 = (bf16[162,128]{1,0:T(8,128)(2,1)S(1)}, bf16[162,128]{1,0:T(8,128)(2,1)S(1)}, u32[]{:S(2)}, u32[]{:S(2)}) collective-permute-start(bf16[162,128]{1,0:T(8,128)(2,1)S(1)} %get-tuple-element.67), channel_id=1, source_target_pairs={{0,128},{16,144},{32,160},{48,176},{64,192},{80,208},{96,224},{112... | collective-permute-start | bytes 124424 | tf_op jit(solution)/shard_map/ppermute | solution.py:143
  222.2 4.5 %collective-permute-start.23 = (bf16[162,128]{1,0:T(8,128)(2,1)S(1)}, bf16[162,128]{1,0:T(8,128)(2,1)S(1)}, u32[]{:S(2)}, u32[]{:S(2)}) collective-permute-start(bf16[162,128]{1,0:T(8,128)(2,1)S(1)} %get-tuple-element.66), channel_id=1, source_target_pairs={{0,64},{16,80},{32,96},{48,112},{64,128},{80,144},{96,160},{112,17... | collective-permute-start | bytes 124424 | tf_op jit(solution)/shard_map/ppermute | solution.py:143
  226.7 4.0 %collective-permute-start.31 = (bf16[162,128]{1,0:T(8,128)(2,1)S(1)}, bf16[162,128]{1,0:T(8,128)(2,1)S(1)}, u32[]{:S(2)}, u32[]{:S(2)}) collective-permute-start(bf16[162,128]{1,0:T(8,128)(2,1)S(1)} %fusion.155), channel_id=1, source_target_pairs={{0,8},{1,9},{2,10},{3,11},{4,12},{5,13},{6,14},{7,15},{8,0},{9,1},... | collective-permute-start | bytes 124424 | tf_op jit(solution)/shard_map/ppermute | solution.py:143
  230.7 5.8 %collective-permute-done.31 = bf16[162,128]{1,0:T(8,128)(2,1)S(1)} collective-permute-done((bf16[162,128]{1,0:T(8,128)(2,1)S(1)}, bf16[162,128]{1,0:T(8,128)(2,1)S(1)}, u32[]{:S(2)}, u32[]{:S(2)}) %collective-permute-start.31) | collective-permute-done | bytes 41504 | tf_op jit(solution)/shard_map/ppermute | solution.py:143
  (266 shorter events, 43.1 us)
Async XLA Ops:
  0.6 139.1 %copy-start = (bf16[1,8,128,64]{2,3,1,0:T(8,128)(2,1)S(1)}, bf16[1,8,128,64]{2,3,1,0:T(8,128)(2,1)}, u32[]{:S(2)}) copy-start(bf16[1,8,128,64]{2,3,1,0:T(8,128)(2,1)} %param.10) | copy-start | bytes 393220
  0.6 43.5 %copy-start.25 = (bf16[1,4,64,256]{3,2,1,0:T(8,128)(2,1)S(1)}, bf16[1,4,64,256]{3,2,1,0:T(8,128)(2,1)}, u32[]{:S(2)}) copy-start(bf16[1,4,64,256]{3,2,1,0:T(8,128)(2,1)} %param.7) | copy-start | bytes 393220
  0.7 38.6 %copy-start.41 = (s32[32]{0:T(128)S(1)}, s32[32]{0:T(128)}, u32[]{:S(2)}) copy-start(s32[32]{0:T(128)} %param.13) | copy-start | bytes 388
  1.5 42.6 %collective-permute-start.1 = (bf16[1,64,256]{2,1,0:T(8,128)(2,1)S(1)}, bf16[1,64,256]{2,1,0:T(8,128)(2,1)S(1)}, u32[]{:S(2)}, u32[]{:S(2)}) collective-permute-start(bf16[1,64,256]{2,1,0:T(8,128)(2,1)S(1)} %get-tuple-element.96), channel_id=1, source_target_pairs={{1,0},{2,1},{3,2},{4,3},{5,4},{6,5},{7,6},{8,7},{9,8},{10,9},{11,1... | collective-permute-start | bytes 98312 | tf_op jit(solution)/shard_map/ppermute | solution.py:22
  2.8 41.3 %collective-permute-start = (bf16[1,64,256]{2,1,0:T(8,128)(2,1)S(1)}, bf16[1,64,256]{2,1,0:T(8,128)(2,1)S(1)}, u32[]{:S(2)}, u32[]{:S(2)}) collective-permute-start(bf16[1,64,256]{2,1,0:T(8,128)(2,1)S(1)} %get-tuple-element.95), channel_id=1, source_target_pairs={{0,1},{1,2},{2,3},{3,4},{4,5},{5,6},{6,7},{7,8},{8,9},{9,10},{10,1... | collective-permute-start | bytes 98312 | tf_op jit(solution)/shard_map/ppermute | solution.py:19
  6.9 33.6 %collective-permute-start.2 = (bf16[162,128]{1,0:T(8,128)(2,1)S(1)}, bf16[162,128]{1,0:T(8,128)(2,1)S(1)}, u32[]{:S(2)}, u32[]{:S(2)}) collective-permute-start(bf16[162,128]{1,0:T(8,128)(2,1)S(1)} %bitcast_convert_fusion), channel_id=1, source_target_pairs={{0,256},{16,272},{32,288},{48,304},{64,320},{80,336},{96,352},{112... | collective-permute-start | bytes 124424 | tf_op jit(solution)/shard_map/ppermute | solution.py:143
  23.8 20.6 %copy-start.26 = (f32[20736]{0:T(1024)}, f32[20736]{0:T(1024)S(1)}, u32[]{:S(2)}) copy-start(f32[20736]{0:T(1024)S(1)} %reduce.1) | copy-start | bytes 248836
  24.4 19.7 %copy-start.37 = (pred[514]{0:T(1024)(128)(4,1)}, pred[514]{0:T(1024)(128)(4,1)S(1)}, u32[]{:S(2)}) copy-start(pred[514]{0:T(1024)(128)(4,1)S(1)} %get-tuple-element.110) | copy-start | bytes 1546
  24.4 40.4 %copy-start.34 = (pred[514]{0:T(1024)(128)(4,1)}, pred[514]{0:T(1024)(128)(4,1)S(1)}, u32[]{:S(2)}) copy-start(pred[514]{0:T(1024)(128)(4,1)S(1)} %get-tuple-element.111) | copy-start | bytes 1546
  40.6 11.9 %collective-permute-start.3 = (bf16[2,162,128]{2,1,0:T(8,128)(2,1)S(1)}, bf16[2,162,128]{2,1,0:T(8,128)(2,1)S(1)}, u32[]{:S(2)}, u32[]{:S(2)}) collective-permute-start(bf16[2,162,128]{2,1,0:T(8,128)(2,1)S(1)} %pad_maximum_fusion.18), channel_id=1, source_target_pairs={{0,16},{16,32},{32,48},{48,0},{64,80},{80,96},{96,112},{112,64},{1... | collective-permute-start | bytes 248840 | tf_op jit(solution)/shard_map/ppermute | solution.py:143
  44.4 8.3 %collective-permute-start.4 = (bf16[2,162,128]{2,1,0:T(8,128)(2,1)S(1)}, bf16[2,162,128]{2,1,0:T(8,128)(2,1)S(1)}, u32[]{:S(2)}, u32[]{:S(2)}) collective-permute-start(bf16[2,162,128]{2,1,0:T(8,128)(2,1)S(1)} %pad_maximum_fusion.18), channel_id=1, source_target_pairs={{0,32},{16,48},{32,0},{48,16},{64,96},{80,112},{96,64},{112,80},{1... | collective-permute-start | bytes 248840 | tf_op jit(solution)/shard_map/ppermute | solution.py:143
  49.2 6.6 %collective-permute-start.5 = (bf16[2,162,128]{2,1,0:T(8,128)(2,1)S(1)}, bf16[2,162,128]{2,1,0:T(8,128)(2,1)S(1)}, u32[]{:S(2)}, u32[]{:S(2)}) collective-permute-start(bf16[2,162,128]{2,1,0:T(8,128)(2,1)S(1)} %pad_maximum_fusion.18), channel_id=1, source_target_pairs={{0,48},{16,0},{32,16},{48,32},{64,112},{80,64},{96,80},{112,96},{1... | collective-permute-start | bytes 248840 | tf_op jit(solution)/shard_map/ppermute | solution.py:143
  55.8 9.1 %collective-permute-start.6 = (bf16[162,128]{1,0:T(8,128)(2,1)S(1)}, bf16[162,128]{1,0:T(8,128)(2,1)S(1)}, u32[]{:S(2)}, u32[]{:S(2)}) collective-permute-start(bf16[162,128]{1,0:T(8,128)(2,1)S(1)} %get-tuple-element.73), channel_id=1, source_target_pairs={{0,192},{16,208},{32,224},{48,240},{64,0},{80,16},{96,32},{112,48}... | collective-permute-start | bytes 124424 | tf_op jit(solution)/shard_map/ppermute | solution.py:143
  58.3 7.4 %collective-permute-start.7 = (bf16[162,128]{1,0:T(8,128)(2,1)S(1)}, bf16[162,128]{1,0:T(8,128)(2,1)S(1)}, u32[]{:S(2)}, u32[]{:S(2)}) collective-permute-start(bf16[162,128]{1,0:T(8,128)(2,1)S(1)} %get-tuple-element.72), channel_id=1, source_target_pairs={{0,128},{16,144},{32,160},{48,176},{64,192},{80,208},{96,224},{112... | collective-permute-start | bytes 124424 | tf_op jit(solution)/shard_map/ppermute | solution.py:143
  62.9 5.9 %collective-permute-start.8 = (bf16[162,128]{1,0:T(8,128)(2,1)S(1)}, bf16[162,128]{1,0:T(8,128)(2,1)S(1)}, u32[]{:S(2)}, u32[]{:S(2)}) collective-permute-start(bf16[162,128]{1,0:T(8,128)(2,1)S(1)} %get-tuple-element.71), channel_id=1, source_target_pairs={{0,64},{16,80},{32,96},{48,112},{64,128},{80,144},{96,160},{112,17... | collective-permute-start | bytes 124424 | tf_op jit(solution)/shard_map/ppermute | solution.py:143
  68.9 13.4 %copy-start.21 = (f32[162,128]{1,0:T(8,128)}, f32[162,128]{1,0:T(8,128)S(1)}, u32[]{:S(2)}) copy-start(f32[162,128]{1,0:T(8,128)S(1)} %bitcast_select_fusion) | copy-start | bytes 248836
  68.9 9.8 %collective-permute-start.9 = (bf16[162,128]{1,0:T(8,128)(2,1)S(1)}, bf16[162,128]{1,0:T(8,128)(2,1)S(1)}, u32[]{:S(2)}, u32[]{:S(2)}) collective-permute-start(bf16[162,128]{1,0:T(8,128)(2,1)S(1)} %convert_element_type.84), channel_id=1, source_target_pairs={{0,8},{1,9},{2,10},{3,11},{4,12},{5,13},{6,14},{7,15},{8,0},{9,1},... | collective-permute-start | bytes 124424 | tf_op jit(solution)/shard_map/ppermute | solution.py:143
  78.8 8.2 %collective-permute-start.10 = (bf16[2,162,128]{2,1,0:T(8,128)(2,1)S(1)}, bf16[2,162,128]{2,1,0:T(8,128)(2,1)S(1)}, u32[]{:S(2)}, u32[]{:S(2)}) collective-permute-start(bf16[2,162,128]{2,1,0:T(8,128)(2,1)S(1)} %pad_maximum_fusion.19), channel_id=1, source_target_pairs={{0,4},{1,5},{2,6},{3,7},{4,0},{5,1},{6,2},{7,3},{8,12},{9,13},{10,... | collective-permute-start | bytes 248840 | tf_op jit(solution)/shard_map/ppermute | solution.py:143
  87.0 7.3 %collective-permute-start.11 = (bf16[2,2,162,128]{3,2,1,0:T(8,128)(2,1)S(1)}, bf16[2,2,162,128]{3,2,1,0:T(8,128)(2,1)S(1)}, u32[]{:S(2)}, u32[]{:S(2)}) collective-permute-start(bf16[2,2,162,128]{3,2,1,0:T(8,128)(2,1)S(1)} %pad_maximum_fusion.17), channel_id=1, source_target_pairs={{0,2},{1,3},{2,0},{3,1},{4,6},{5,7},{6,4},{7,5},{8,10},{9,11},{10,... | collective-permute-start | bytes 497672 | tf_op jit(solution)/shard_map/ppermute | solution.py:143
  94.4 3.5 %collective-permute-start.12 = (bf16[2,2,2,162,128]{4,3,2,1,0:T(8,128)(2,1)S(1)}, bf16[2,2,2,162,128]{4,3,2,1,0:T(8,128)(2,1)S(1)}, u32[]{:S(2)}, u32[]{:S(2)}) collective-permute-start(bf16[2,2,2,162,128]{4,3,2,1,0:T(8,128)(2,1)S(1)} %pad_maximum_fusion.16), channel_id=1, source_target_pairs={{0,1},{1,0},{2,3},{3,2},{4,5},{5,4},{6,7},{7,6},{8,9},{9,8},{10,11... | collective-permute-start | bytes 995336 | tf_op jit(solution)/shard_map/ppermute | solution.py:143
  104.7 8.2 %copy-start.9 = (bf16[1,27,64,64]{3,2,1,0:T(8,128)(2,1)S(1)}, bf16[1,27,64,64]{3,2,1,0:T(8,128)(2,1)}, u32[]{:S(2)}) copy-start(bf16[1,27,64,64]{3,2,1,0:T(8,128)(2,1)} %get-tuple-element.22) | copy-start | bytes 663556
  104.9 9.0 %copy-start.38 = (pred[514]{0:T(1024)(128)(4,1)S(1)}, pred[514]{0:T(1024)(128)(4,1)}, u32[]{:S(2)}) copy-start(pred[514]{0:T(1024)(128)(4,1)} %copy-done.37) | copy-start | bytes 1546
  105.9 8.4 %copy-start.17 = (bf16[4,64,256]{2,1,0:T(8,128)(2,1)}, bf16[4,64,256]{2,1,0:T(8,128)(2,1)S(1)}, u32[]{:S(2)}) copy-start(bf16[4,64,256]{2,1,0:T(8,128)(2,1)S(1)} %get-tuple-element.104) | copy-start | bytes 393220
  105.9 8.3 %copy-start.35 = (pred[514]{0:T(1024)(128)(4,1)S(1)}, pred[514]{0:T(1024)(128)(4,1)}, u32[]{:S(2)}) copy-start(pred[514]{0:T(1024)(128)(4,1)} %copy-done.34) | copy-start | bytes 1546
  105.9 8.0 %collective-permute-start.14 = (bf16[1,64,256]{2,1,0:T(8,128)(2,1)S(1)}, bf16[1,64,256]{2,1,0:T(8,128)(2,1)S(1)}, u32[]{:S(2)}, u32[]{:S(2)}) collective-permute-start(bf16[1,64,256]{2,1,0:T(8,128)(2,1)S(1)} %get-tuple-element.94), channel_id=1, source_target_pairs={{1,0},{2,1},{3,2},{4,3},{5,4},{6,5},{7,6},{8,7},{9,8},{10,9},{11,1... | collective-permute-start | bytes 98312 | tf_op jit(solution)/shard_map/ppermute | solution.py:22
  107.2 6.7 %collective-permute-start.13 = (bf16[1,64,256]{2,1,0:T(8,128)(2,1)S(1)}, bf16[1,64,256]{2,1,0:T(8,128)(2,1)S(1)}, u32[]{:S(2)}, u32[]{:S(2)}) collective-permute-start(bf16[1,64,256]{2,1,0:T(8,128)(2,1)S(1)} %get-tuple-element.93), channel_id=1, source_target_pairs={{0,1},{1,2},{2,3},{3,4},{4,5},{5,6},{6,7},{7,8},{8,9},{9,10},{10,1... | collective-permute-start | bytes 98312 | tf_op jit(solution)/shard_map/ppermute | solution.py:19
  110.3 15.8 %collective-permute-start.17 = (bf16[162,128]{1,0:T(8,128)(2,1)}, bf16[162,128]{1,0:T(8,128)(2,1)}, u32[]{:S(2)}, u32[]{:S(2)}) collective-permute-start(bf16[162,128]{1,0:T(8,128)(2,1)} %bitcast_convert_fusion.1), channel_id=1, source_target_pairs={{0,256},{16,272},{32,288},{48,304},{64,320},{80,336},{96,352},{112... | collective-permute-start | bytes 124424 | tf_op jit(solution)/shard_map/ppermute | solution.py:143
  115.0 1.0 copy-start.11
  117.7 1.4 copy-start.1
  120.4 11.7 %collective-permute-start.16 = (bf16[1,64,256]{2,1,0:T(8,128)(2,1)}, bf16[1,64,256]{2,1,0:T(8,128)(2,1)S(1)}, u32[]{:S(2)}, u32[]{:S(2)}) collective-permute-start(bf16[1,64,256]{2,1,0:T(8,128)(2,1)} %get-tuple-element.92), channel_id=1, source_target_pairs={{1,0},{2,1},{3,2},{4,3},{5,4},{6,5},{7,6},{8,7},{9,8},{10,9},{11,1... | collective-permute-start | bytes 98312 | tf_op jit(solution)/shard_map/ppermute | solution.py:22
  121.7 10.4 %collective-permute-start.15 = (bf16[1,64,256]{2,1,0:T(8,128)(2,1)}, bf16[1,64,256]{2,1,0:T(8,128)(2,1)}, u32[]{:S(2)}, u32[]{:S(2)}) collective-permute-start(bf16[1,64,256]{2,1,0:T(8,128)(2,1)} %get-tuple-element.91), channel_id=1, source_target_pairs={{0,1},{1,2},{2,3},{3,4},{4,5},{5,6},{6,7},{7,8},{8,9},{9,10},{10,1... | collective-permute-start | bytes 98312 | tf_op jit(solution)/shard_map/ppermute | solution.py:19
  133.8 1.0 copy-start.12
  133.9 1.6 copy-start.3
  137.8 1.9 copy-start.40
  144.4 2.4 %copy-start.6 = (bf16[6,192,256]{2,1,0:T(8,128)(2,1)S(1)}, bf16[6,192,256]{2,1,0:T(8,128)(2,1)}, u32[]{:S(2)}) copy-start(bf16[6,192,256]{2,1,0:T(8,128)(2,1)} %copy-done.5) | copy-start | bytes 1769476
  144.4 2.7 %copy-start.4 = (bf16[6,192,256]{2,1,0:T(8,128)(2,1)S(1)}, bf16[6,192,256]{2,1,0:T(8,128)(2,1)}, u32[]{:S(2)}) copy-start(bf16[6,192,256]{2,1,0:T(8,128)(2,1)} %copy-done.3) | copy-start | bytes 1769476
  144.4 3.0 %copy-start.8 = (bf16[6,192,256]{2,1,0:T(8,128)(2,1)S(1)}, bf16[6,192,256]{2,1,0:T(8,128)(2,1)}, u32[]{:S(2)}) copy-start(bf16[6,192,256]{2,1,0:T(8,128)(2,1)} %copy-done.7) | copy-start | bytes 1769476
  145.5 3.3 %copy-start.13 = (bf16[4,64,256]{2,1,0:T(8,128)(2,1)}, bf16[4,64,256]{2,1,0:T(8,128)(2,1)S(1)}, u32[]{:S(2)}) copy-start(bf16[4,64,256]{2,1,0:T(8,128)(2,1)S(1)} %fusion.135) | copy-start | bytes 393220
  149.5 10.4 %collective-permute-start.25 = (bf16[1,64,256]{2,1,0:T(8,128)(2,1)}, bf16[1,64,256]{2,1,0:T(8,128)(2,1)S(1)}, u32[]{:S(2)}, u32[]{:S(2)}) collective-permute-start(bf16[1,64,256]{2,1,0:T(8,128)(2,1)} %get-tuple-element.90), channel_id=1, source_target_pairs={{1,0},{2,1},{3,2},{4,3},{5,4},{6,5},{7,6},{8,7},{9,8},{10,9},{11,1... | collective-permute-start | bytes 98312 | tf_op jit(solution)/shard_map/ppermute | solution.py:22
  150.8 9.1 %collective-permute-start.24 = (bf16[1,64,256]{2,1,0:T(8,128)(2,1)}, bf16[1,64,256]{2,1,0:T(8,128)(2,1)}, u32[]{:S(2)}, u32[]{:S(2)}) collective-permute-start(bf16[1,64,256]{2,1,0:T(8,128)(2,1)} %get-tuple-element.89), channel_id=1, source_target_pairs={{0,1},{1,2},{2,3},{3,4},{4,5},{5,6},{6,7},{7,8},{8,9},{9,10},{10,1... | collective-permute-start | bytes 98312 | tf_op jit(solution)/shard_map/ppermute | solution.py:19
  161.6 1.0 copy-start.20
  165.3 1.1 copy-start.2
  166.4 2.3 copy-start.23
  169.3 8.4 %collective-permute-start.27 = (bf16[1,64,256]{2,1,0:T(8,128)(2,1)}, bf16[1,64,256]{2,1,0:T(8,128)(2,1)S(1)}, u32[]{:S(2)}, u32[]{:S(2)}) collective-permute-start(bf16[1,64,256]{2,1,0:T(8,128)(2,1)} %get-tuple-element.88), channel_id=1, source_target_pairs={{1,0},{2,1},{3,2},{4,3},{5,4},{6,5},{7,6},{8,7},{9,8},{10,9},{11,1... | collective-permute-start | bytes 98312 | tf_op jit(solution)/shard_map/ppermute | solution.py:22
  170.6 7.2 %collective-permute-start.26 = (bf16[1,64,256]{2,1,0:T(8,128)(2,1)S(1)}, bf16[1,64,256]{2,1,0:T(8,128)(2,1)S(1)}, u32[]{:S(2)}, u32[]{:S(2)}) collective-permute-start(bf16[1,64,256]{2,1,0:T(8,128)(2,1)S(1)} %get-tuple-element.87), channel_id=1, source_target_pairs={{0,1},{1,2},{2,3},{3,4},{4,5},{5,6},{6,7},{7,8},{8,9},{9,10},{10,1... | collective-permute-start | bytes 98312 | tf_op jit(solution)/shard_map/ppermute | solution.py:19
  174.3 3.4 %copy-start.24 = (bf16[4,64,256]{2,1,0:T(8,128)(2,1)S(1)}, bf16[4,64,256]{2,1,0:T(8,128)(2,1)}, u32[]{:S(2)}) copy-start(bf16[4,64,256]{2,1,0:T(8,128)(2,1)} %copy-done.23) | copy-start | bytes 393220
  174.4 3.4 %copy-start.36 = (pred[514]{0:T(1024)(128)(4,1)S(1)}, pred[514]{0:T(1024)(128)(4,1)}, u32[]{:S(2)}) copy-start(pred[514]{0:T(1024)(128)(4,1)} %copy-done.34) | copy-start | bytes 1546
  174.4 3.4 %copy-start.39 = (pred[514]{0:T(1024)(128)(4,1)S(1)}, pred[514]{0:T(1024)(128)(4,1)}, u32[]{:S(2)}) copy-start(pred[514]{0:T(1024)(128)(4,1)} %copy-done.37) | copy-start | bytes 1546
  178.6 1.0 copy-start.19
  184.9 1.0 copy-start.10
  186.0 3.8 %copy-start.31 = (bf16[8,162,128]{2,1,0:T(8,128)(2,1)S(1)}, bf16[8,162,128]{2,1,0:T(8,128)(2,1)}, u32[]{:S(2)}) copy-start(bf16[8,162,128]{2,1,0:T(8,128)(2,1)} %get-tuple-element.11) | copy-start | bytes 995332
  186.0 4.7 %copy-start.30 = (bf16[1,162,128]{2,1,0:T(8,128)(2,1)S(1)}, bf16[1,162,128]{2,1,0:T(8,128)(2,1)}, u32[]{:S(2)}) copy-start(bf16[1,162,128]{2,1,0:T(8,128)(2,1)} %get-tuple-element.12) | copy-start | bytes 124420
  186.2 14.4 %collective-permute-start.28 = (bf16[2,2,2,162,128]{4,3,2,1,0:T(8,128)(2,1)S(1)}, bf16[2,2,2,162,128]{4,3,2,1,0:T(8,128)(2,1)S(1)}, u32[]{:S(2)}, u32[]{:S(2)}) collective-permute-start(bf16[2,2,2,162,128]{4,3,2,1,0:T(8,128)(2,1)S(1)} %fusion.120), channel_id=1, source_target_pairs={{0,1},{1,0},{2,3},{3,2},{4,5},{5,4},{6,7},{7,6},{8,9},{9,8},{10,11... | collective-permute-start | bytes 995336 | tf_op jit(solution)/shard_map/ppermute | solution.py:143
  190.7 9.9 %collective-permute-start.18 = (bf16[2,162,128]{2,1,0:T(8,128)(2,1)S(1)}, bf16[2,162,128]{2,1,0:T(8,128)(2,1)S(1)}, u32[]{:S(2)}, u32[]{:S(2)}) collective-permute-start(bf16[2,162,128]{2,1,0:T(8,128)(2,1)S(1)} %pad_maximum_fusion.20), channel_id=1, source_target_pairs={{0,16},{16,32},{32,48},{48,0},{64,80},{80,96},{96,112},{112,64},{1... | collective-permute-start | bytes 248840 | tf_op jit(solution)/shard_map/ppermute | solution.py:143
  193.1 10.5 %collective-permute-start.19 = (bf16[2,162,128]{2,1,0:T(8,128)(2,1)S(1)}, bf16[2,162,128]{2,1,0:T(8,128)(2,1)S(1)}, u32[]{:S(2)}, u32[]{:S(2)}) collective-permute-start(bf16[2,162,128]{2,1,0:T(8,128)(2,1)S(1)} %pad_maximum_fusion.20), channel_id=1, source_target_pairs={{0,32},{16,48},{32,0},{48,16},{64,96},{80,112},{96,64},{112,80},{1... | collective-permute-start | bytes 248840 | tf_op jit(solution)/shard_map/ppermute | solution.py:143
  198.7 6.4 %collective-permute-start.20 = (bf16[2,162,128]{2,1,0:T(8,128)(2,1)S(1)}, bf16[2,162,128]{2,1,0:T(8,128)(2,1)S(1)}, u32[]{:S(2)}, u32[]{:S(2)}) collective-permute-start(bf16[2,162,128]{2,1,0:T(8,128)(2,1)S(1)} %pad_maximum_fusion.20), channel_id=1, source_target_pairs={{0,48},{16,0},{32,16},{48,32},{64,112},{80,64},{96,80},{112,96},{1... | collective-permute-start | bytes 248840 | tf_op jit(solution)/shard_map/ppermute | solution.py:143
  200.7 35.8 %copy-start.22 = (f32[162,128]{1,0:T(8,128)S(1)}, f32[162,128]{1,0:T(8,128)}, u32[]{:S(2)}) copy-start(f32[162,128]{1,0:T(8,128)} %copy-done.21) | copy-start | bytes 248836
  200.7 35.8 %copy-start.27 = (f32[20736]{0:T(1024)S(1)}, f32[20736]{0:T(1024)}, u32[]{:S(2)}) copy-start(f32[20736]{0:T(1024)} %copy-done.26) | copy-start | bytes 248836
  200.8 7.8 %collective-permute-start.29 = (bf16[2,2,162,128]{3,2,1,0:T(8,128)(2,1)S(1)}, bf16[2,2,162,128]{3,2,1,0:T(8,128)(2,1)S(1)}, u32[]{:S(2)}, u32[]{:S(2)}) collective-permute-start(bf16[2,2,162,128]{3,2,1,0:T(8,128)(2,1)S(1)} %fusion.141), channel_id=1, source_target_pairs={{0,2},{1,3},{2,0},{3,1},{4,6},{5,7},{6,4},{7,5},{8,10},{9,11},{10,... | collective-permute-start | bytes 497672 | tf_op jit(solution)/shard_map/ppermute | solution.py:143
  208.6 18.1 %collective-permute-start.30 = (bf16[2,162,128]{2,1,0:T(8,128)(2,1)S(1)}, bf16[2,162,128]{2,1,0:T(8,128)(2,1)S(1)}, u32[]{:S(2)}, u32[]{:S(2)}) collective-permute-start(bf16[2,162,128]{2,1,0:T(8,128)(2,1)S(1)} %fusion.142), channel_id=1, source_target_pairs={{0,4},{1,5},{2,6},{3,7},{4,0},{5,1},{6,2},{7,3},{8,12},{9,13},{10,... | collective-permute-start | bytes 248840 | tf_op jit(solution)/shard_map/ppermute | solution.py:143
  216.3 14.4 %collective-permute-start.21 = (bf16[162,128]{1,0:T(8,128)(2,1)S(1)}, bf16[162,128]{1,0:T(8,128)(2,1)S(1)}, u32[]{:S(2)}, u32[]{:S(2)}) collective-permute-start(bf16[162,128]{1,0:T(8,128)(2,1)S(1)} %get-tuple-element.68), channel_id=1, source_target_pairs={{0,192},{16,208},{32,224},{48,240},{64,0},{80,16},{96,32},{112,48}... | collective-permute-start | bytes 124424 | tf_op jit(solution)/shard_map/ppermute | solution.py:143
  218.4 12.3 %collective-permute-start.22 = (bf16[162,128]{1,0:T(8,128)(2,1)S(1)}, bf16[162,128]{1,0:T(8,128)(2,1)S(1)}, u32[]{:S(2)}, u32[]{:S(2)}) collective-permute-start(bf16[162,128]{1,0:T(8,128)(2,1)S(1)} %get-tuple-element.67), channel_id=1, source_target_pairs={{0,128},{16,144},{32,160},{48,176},{64,192},{80,208},{96,224},{112... | collective-permute-start | bytes 124424 | tf_op jit(solution)/shard_map/ppermute | solution.py:143
  222.2 8.5 %collective-permute-start.23 = (bf16[162,128]{1,0:T(8,128)(2,1)S(1)}, bf16[162,128]{1,0:T(8,128)(2,1)S(1)}, u32[]{:S(2)}, u32[]{:S(2)}) collective-permute-start(bf16[162,128]{1,0:T(8,128)(2,1)S(1)} %get-tuple-element.66), channel_id=1, source_target_pairs={{0,64},{16,80},{32,96},{48,112},{64,128},{80,144},{96,160},{112,17... | collective-permute-start | bytes 124424 | tf_op jit(solution)/shard_map/ppermute | solution.py:143
  226.7 9.8 %collective-permute-start.31 = (bf16[162,128]{1,0:T(8,128)(2,1)S(1)}, bf16[162,128]{1,0:T(8,128)(2,1)S(1)}, u32[]{:S(2)}, u32[]{:S(2)}) collective-permute-start(bf16[162,128]{1,0:T(8,128)(2,1)S(1)} %fusion.155), channel_id=1, source_target_pairs={{0,8},{1,9},{2,10},{3,11},{4,12},{5,13},{6,14},{7,15},{8,0},{9,1},... | collective-permute-start | bytes 124424 | tf_op jit(solution)/shard_map/ppermute | solution.py:143
  (10 other events, 8.4 us)

commit v2 on v0

v2 whole, which is shorter than its diff:
```python
import math

import jax
import jax.numpy as jnp
from jax import lax
from jax.experimental import pallas as pl
from jax.experimental.pallas import tpu as pltpu
from jax.sharding import PartitionSpec as P

CH = 64
ROW = 128
ROWS = 162
SLABS = 16
PLANES = 4
DEPTH = 64
K_ROWS = 27 * CH // 2
FLAT_ROWS = 3 * K_ROWS
momentum_decay = 0.9
step_length = 0.01


def gelu_parts(x):
    c = math.sqrt(2.0 / math.pi)
    square = x * x
    t = jnp.tanh(c * (x + 0.044715 * (x * square)))
    half = 0.5 * (1.0 + t)
    slope = half + 0.5 * x * (1.0 - t * t) * (c * (1.0 + 3.0 * 0.044715 * square))
    return x * half, slope


def local_kernel(
    slab_ref,
    far_low,
    low,
    own,
    high,
    far_high,
    held_ref,
    got_ref,
    critic_ref,
    critic_back_ref,
    score_ref,
    out_ref,
    keep_ref,
    send_ref,
    raw,
    natural,
    forward_w,
    backward_w,
    win0,
    win1,
    win2,
    wing3,
    wing2,
    grad1,
    slope1,
    slope2,
    flat_k,
    flat,
):
    slab = slab_ref[0]
    lane = lax.broadcasted_iota(jnp.int32, (2 * CH, ROW), 1)
    lane_half = lax.broadcasted_iota(jnp.int32, (CH, ROW), 1)

    def store_window(target, index, value):
        target[index, 0:ROW, :] = jnp.where(lane == 0, 0.0, pltpu.roll(value, 1, 1)).astype(
            jnp.bfloat16
        )
        target[index, ROW : 2 * ROW, :] = value.astype(jnp.bfloat16)
        target[index, 2 * ROW : 3 * ROW, :] = jnp.where(
            lane == ROW - 1, 0.0, pltpu.roll(value, ROW - 1, 1)
        ).astype(jnp.bfloat16)

    def inside(plane, value):
        z = slab * PLANES + plane
        return jnp.where(jnp.logical_and(z >= 0, z < DEPTH), value, 0.0)

    sources = (
        [far_low[0]]
        + [low[i] for i in range(PLANES)]
        + [own[i] for i in range(PLANES)]
        + [high[i] for i in range(PLANES)]
        + [far_high[0]]
    )
    for index, plane in enumerate(sources):
        value = jnp.concatenate([plane[:, :ROW], plane[:, ROW:]], axis=0).astype(jnp.float32)
        store_window(win0, index, value)

    for block in range(SLABS):
        apart = block ^ slab
        slot = ((apart >> 1) & 1) * 4 + ((apart >> 2) & 1) * 2 + ((apart >> 3) & 1)
        piece = jnp.where(
            (apart & 1) == 1,
            got_ref[slot].astype(jnp.float32),
            held_ref[slot].astype(jnp.float32),
        )
        raw[block * ROWS : (block + 1) * ROWS, :] = piece

    for layer in range(3):
        rows = raw[layer * K_ROWS : (layer + 1) * K_ROWS, :]
        natural[pl.ds(layer * 2 * K_ROWS, K_ROWS, stride=2), :] = rows
        natural[pl.ds(layer * 2 * K_ROWS + 1, K_ROWS, stride=2), :] = pltpu.roll(rows, CH, 1)

    def kernel_at(layer, a, b, c):
        start = (layer * 27 + 9 * a + 3 * b + c) * CH
        return natural[start : start + CH, :]

    left = lane_half < CH
    for layer in range(3):
        for a in range(3):
            for c in range(3):
                middle = kernel_at(layer, a, 1, c)
                top = jnp.where(left, middle, pltpu.roll(kernel_at(layer, a, 2, c), CH, 1))
                bottom = jnp.where(left, kernel_at(layer, a, 0, c), pltpu.roll(middle, CH, 1))
                block = jnp.concatenate([top, bottom], axis=0)
                spot = (3 * a + c) * ROW
                forward_w[layer, :, spot : spot + ROW] = block.astype(jnp.bfloat16)
                if layer:
                    spot = (3 * (2 - a) + 2 - c) * ROW
                    backward_w[layer - 1, :, spot : spot + ROW] = block.T.astype(jnp.bfloat16)

    def pair_product(weights, windows, index):
        first = windows[index : index + 3].reshape(9 * ROW, ROW)
        second = windows[index + 1 : index + 4].reshape(9 * ROW, ROW)
        return jnp.dot(
            weights,
            jnp.concatenate([first, second], axis=1),
            preferred_element_type=jnp.float32,
        )

    for pair in range(6):
        pre = pair_product(forward_w[0], win0, 2 * pair)
        for side in range(2):
            plane = 2 * pair + side - 4
            value, slope = gelu_parts(pre[:, side * ROW : (side + 1) * ROW])
            if 0 <= plane < PLANES:
                slope1[plane] = slope
            store_window(win1, plane + 4, inside(plane, value))

    for pair in range(5):
        pre = pair_product(forward_w[1], win1, 2 * pair)
        for side in range(2):
            plane = 2 * pair + side - 3
            value, slope = gelu_parts(pre[:, side * ROW : (side + 1) * ROW])
            if -1 <= plane < PLANES + 1:
                slope2[plane + 1] = slope
            store_window(win2, plane + 3, inside(plane, value))

    even = (lane % 2) == 0
    for pair in range(4):
        pre = pair_product(forward_w[2], win2, 2 * pair)
        made = jnp.tanh(pre)
        parts = []
        for side in range(2):
            plane = 2 * pair + side - 2
            shown = made[:, side * ROW : (side + 1) * ROW].astype(jnp.bfloat16)
            if 0 <= plane < PLANES:
                out_ref[plane] = jnp.concatenate([shown[:CH], shown[CH:]], axis=1)
            parts.append(shown)
            parts.append(pltpu.roll(shown.astype(jnp.float32), ROW - 1, 1).astype(jnp.bfloat16))
        response = jnp.dot(
            critic_ref[...], jnp.concatenate(parts, axis=0), preferred_element_type=jnp.float32
        )
        features, slope = gelu_parts(response)
        score = jnp.sum(score_ref[...] * features, axis=0, keepdims=True)
        push = -jax.nn.sigmoid(-score)
        upstream = (slope * (push * score_ref[...])).astype(jnp.bfloat16).astype(jnp.float32)
        upstream = jnp.where(even, upstream, 0.0)
        both = jnp.concatenate(
            [upstream.astype(jnp.bfloat16), pltpu.roll(upstream, 1, 1).astype(jnp.bfloat16)],
            axis=0,
        )
        spread = jnp.dot(critic_back_ref[...], both, preferred_element_type=jnp.float32)
        for side in range(2):
            plane = 2 * pair + side - 2
            t = made[:, side * ROW : (side + 1) * ROW]
            grad = spread[side * ROW : (side + 1) * ROW] * (1.0 - t * t)
            grad = grad.astype(jnp.bfloat16).astype(jnp.float32)
            store_window(wing3, plane + 2, inside(plane, grad))

    def kernel_grad(layer, gradient, windows, offset):
        for a in range(3):
            moved = jnp.concatenate([windows[z + a + offset] for z in range(PLANES)], axis=1)
            product = lax.dot_general(
                gradient, moved, (((1,), (1,)), ((), ())), preferred_element_type=jnp.float32
            )
            for c in range(3):
                block = product[:, c * ROW : (c + 1) * ROW]
                top, bottom = block[:CH], block[CH:]
                values = (bottom, top + pltpu.roll(bottom, CH, 1), pltpu.roll(top, CH, 1))
                for b in range(3):
                    spot = 9 * a + 3 * b + c
                    flat_k[spot * CH : (spot + 1) * CH, :] = values[b]
        evens = flat_k[pl.ds(0, K_ROWS, stride=2), :]
        odds = flat_k[pl.ds(1, K_ROWS, stride=2), :]
        wide = lax.broadcasted_iota(jnp.int32, (K_ROWS, ROW), 1)
        flat[layer * K_ROWS : (layer + 1) * K_ROWS, :] = jnp.where(
            wide < CH, evens, pltpu.roll(odds, CH, 1)
        )

    def centre(windows, offset):
        return jnp.concatenate(
            [windows[z + offset, ROW : 2 * ROW, :] for z in range(PLANES)], axis=1
        )

    kernel_grad(2, centre(wing3, 2), win2, 2)
    for pair in range(3):
        back = pair_product(backward_w[1], wing3, 2 * pair)
        for side in range(2):
            plane = 2 * pair + side - 1
            grad = slope2[plane + 1] * back[:, side * ROW : (side + 1) * ROW]
            grad = grad.astype(jnp.bfloat16).astype(jnp.float32)
            store_window(wing2, plane + 1, inside(plane, grad))
    kernel_grad(1, centre(wing2, 1), win1, 3)
    for pair in range(2):
        back = pair_product(backward_w[0], wing2, 2 * pair)
        for side in range(2):
            plane = 2 * pair + side
            grad = slope1[plane] * back[:, side * ROW : (side + 1) * ROW]
            grad1[:, plane * ROW : (plane + 1) * ROW] = grad.astype(jnp.bfloat16)
    kernel_grad(0, grad1[...], win0, 4)

    for block in range(SLABS):
        apart = block ^ slab
        slot = ((apart >> 1) & 1) * 4 + ((apart >> 2) & 1) * 2 + ((apart >> 3) & 1)
        piece = flat[block * ROWS : (block + 1) * ROWS, :]

        @pl.when((apart & 1) == 1)
        def _():
            send_ref[slot] = piece.astype(jnp.bfloat16)

        @pl.when((apart & 1) == 0)
        def _():
            keep_ref[slot] = piece


def local_step(slab, pieces, held, got, critic, critic_back, score):
    bf16, f32 = jnp.bfloat16, jnp.float32
    vmem = pl.BlockSpec(memory_space=pltpu.VMEM)
    return pl.pallas_call(
        local_kernel,
        out_shape=(
            jax.ShapeDtypeStruct((PLANES, CH, 2 * ROW), bf16),
            jax.ShapeDtypeStruct((SLABS // 2, ROWS, ROW), f32),
            jax.ShapeDtypeStruct((SLABS // 2, ROWS, ROW), bf16),
        ),
        in_specs=[pl.BlockSpec(memory_space=pltpu.SMEM)] + [vmem] * 10,
        out_specs=(vmem, vmem, vmem),
        scratch_shapes=[
            pltpu.VMEM((FLAT_ROWS, ROW), f32),
            pltpu.VMEM((2 * FLAT_ROWS, ROW), f32),
            pltpu.VMEM((3, ROW, 9 * ROW), bf16),
            pltpu.VMEM((2, ROW, 9 * ROW), bf16),
            pltpu.VMEM((14, 3 * ROW, ROW), bf16),
            pltpu.VMEM((12, 3 * ROW, ROW), bf16),
            pltpu.VMEM((10, 3 * ROW, ROW), bf16),
            pltpu.VMEM((8, 3 * ROW, ROW), bf16),
            pltpu.VMEM((6, 3 * ROW, ROW), bf16),
            pltpu.VMEM((ROW, PLANES * ROW), bf16),
            pltpu.VMEM((PLANES, ROW, ROW), f32),
            pltpu.VMEM((PLANES + 2, ROW, ROW), f32),
            pltpu.VMEM((2 * K_ROWS, ROW), f32),
            pltpu.VMEM((FLAT_ROWS, ROW), f32),
        ],
        compiler_params=pltpu.CompilerParams(vmem_limit_bytes=48 << 20),
        cost_estimate=pl.CostEstimate(
            flops=6_000_000_000, bytes_accessed=4_000_000, transcendentals=1_000_000
        ),
        name="local_step",
    )(slab, *pieces, held, got, critic, critic_back, score)


def move(value, axis, target_of):
    count = lax.axis_size(axis)
    return lax.ppermute(value, axis, [(i, target_of(i)) for i in range(count)])


def fetch_partner(value, pairing):
    rank = lax.axis_index("trainer")
    half = rank // 16
    across = move(value, "trainer", lambda i: i ^ 16)
    wanted = lax.dynamic_slice_in_dim(pairing, half * 16, 16) // 16 == half
    slots = jnp.where(wanted.reshape((16,) + (1,) * value.ndim), value[None], across[None])
    groups = [list(range(16)), list(range(16, 32))]
    heard = lax.all_to_all(slots, "trainer", 0, 0, axis_index_groups=groups)
    return lax.dynamic_index_in_dim(heard, pairing[rank] % 16, 0, keepdims=False)


def gather_depth(block):
    held = block[None]
    for mask in (8, 4, 2):
        held = jnp.concatenate([held, move(held, "depth", lambda i: i ^ mask)])
    return held, move(held, "depth", lambda i: i ^ 1)


def scatter_depth(keep, send):
    keep = keep + move(send, "depth", lambda i: i ^ 1).astype(jnp.float32)
    for mask in (2, 4, 8):
        size = keep.shape[0] // 2
        send = keep[size:].astype(jnp.bfloat16)
        keep = keep[:size] + move(send, "depth", lambda i: i ^ mask).astype(jnp.float32)
    return keep[0]


def shifted(value, by):
    count = lax.axis_size("depth")
    links = [(i, i + by) for i in range(count) if 0 <= i + by < count]
    return lax.ppermute(value, "depth", links)


def critic_forms(disc):
    cube = disc.reshape(2, 2, 2, disc.shape[1], disc.shape[2])
    forward = cube.transpose(3, 0, 2, 1, 4).reshape(ROW, 8 * CH)
    backward = cube.transpose(0, 1, 4, 2, 3).reshape(4 * CH, 2 * ROW)
    return forward, backward


def on_device(noise, gen_weight, gen_momentum, disc_weight, score_weight, pairing, flags):
    keeper = flags[lax.axis_index("trainer")] == 1
    own_weight = gen_weight.reshape(ROWS, ROW)
    own_moment = gen_momentum.reshape(ROWS, ROW)
    sent = jnp.stack([own_weight, own_moment]).astype(jnp.bfloat16)
    other = fetch_partner(sent, pairing).astype(jnp.float32)
    chosen_weight = jnp.where(keeper, own_weight, other[0])
    chosen_momentum = jnp.where(keeper, own_moment, other[1])
    latent = noise[0]
    pieces = (
        shifted(latent[PLANES - 1 :], 2),
        shifted(latent, 1),
        latent,
        shifted(latent, -1),
        shifted(latent[:1], -2),
    )
    critic, critic_back = critic_forms(disc_weight[0])
    score = jnp.broadcast_to(score_weight[0][:, None], (ROW, ROW))
    held, got = gather_depth(chosen_weight.astype(jnp.bfloat16))
    slab = lax.axis_index("depth").astype(jnp.int32).reshape(1)
    generated, keep, send = local_step(slab, pieces, held, got, critic, critic_back, score)
    grad_share = scatter_depth(keep, send)
    new_momentum = momentum_decay * chosen_momentum + grad_share
    new_weight = chosen_weight - step_length * new_momentum
    return (
        generated[None],
        new_weight.reshape(gen_weight.shape),
        new_momentum.reshape(gen_weight.shape),
    )


def solution(mesh):
    placed = (
        P("trainer", "depth", None, None),
        P("trainer", "depth"),
        P("trainer", "depth"),
        P("trainer", None, None, None),
        P("trainer", None),
        P(),
        P(),
    )
    return jax.shard_map(
        on_device,
        mesh=mesh,
        in_specs=placed,
        out_specs=(P("trainer", "depth", None, None), P("trainer", "depth"), P("trainer", "depth")),
        check_vma=False,
    )
```

time: 623 us -> 140 us (0.22)
  the two profiles are of different devices: /device:TPU:1 before, /device:TPU:8 now
where the time goes in v2:
time: 140 us; the launch traced here: 139 us
  starting transfers between devices  70.3 us (50%)
  waiting for transfers between devices  49.6 us (35%)
  Pallas kernels  7.16 us (5%)
  other arithmetic  6.48 us (5%)
  between operations  3.61 us (3%)
  local copies, waits for them, and re-layouts  1.83 us (1%)
    ppermute x9, starting transfers between devices, move(): return lax.ppermute(value, axis, [(i, target_of(i)) for i in range(count)])  53.6 us
    ppermute x9, waiting for transfers between devices, move(): return lax.ppermute(value, axis, [(i, target_of(i)) for i in range(count)])  29.1 us
    all_to_all x1, waiting for transfers between devices, fetch_partner(): heard = lax.all_to_all(slots, 'trainer', 0, 0, axis_index_groups=groups)  14.7 us
    ppermute x4, starting transfers between devices, shifted(): return lax.ppermute(value, 'depth', links)  9.16 us
    all_to_all x1, starting transfers between devices, fetch_partner(): heard = lax.all_to_all(slots, 'trainer', 0, 0, axis_index_groups=groups)  7.52 us
    pallas_call x1, Pallas kernels, local_step(): pl.pallas_call(local_kernel, out_shape=(jax.ShapeDtypeStruct((PLANES, CH,...  7.16 us
    ppermute x4, waiting for transfers between devices, shifted(): return lax.ppermute(value, 'depth', links)  5.72 us
  transfers between devices with their start and end apart: 14, of which 10 were waited for; matrix products, arithmetic and copies ran while one was open for 2% of the time, Pallas kernels for 0%

profile of v2, /device:TPU:8, one launch (start us, length us, event | category | flops | bytes accessed | tf_op | source)
XLA Modules:
  0.0 139.0 jit_solution(13672037003820178461)
XLA Ops:
  0.6 1.1 convert_reduce_fusion
  1.7 1.1 reduce
  2.9 15.7 %collective-permute-start.4 = (bf16[2,162,128]{2,1,0:T(8,128)(2,1)S(1)}, bf16[2,162,128]{2,1,0:T(8,128)(2,1)S(1)}, u32[]{:S(2)}, u32[]{:S(2)}) collective-permute-start(bf16[2,162,128]{2,1,0:T(8,128)(2,1)S(1)} %pad_maximum_fusion.2), channel_id=1, source_target_pairs={{0,256},{16,272},{32,288},{48,304},{64,320},{80,336},{96,352},{112... | collective-permute-start | bytes 248840 | tf_op jit(solution)/shard_map/ppermute | solution.py:275
  18.6 0.1 copy.17
  18.7 0.7 fusion.5
  19.4 2.0 %collective-permute-done.4 = bf16[2,162,128]{2,1,0:T(8,128)(2,1)S(1)} collective-permute-done((bf16[2,162,128]{2,1,0:T(8,128)(2,1)S(1)}, bf16[2,162,128]{2,1,0:T(8,128)(2,1)S(1)}, u32[]{:S(2)}, u32[]{:S(2)}) %collective-permute-start.4) | collective-permute-done | bytes 82976 | tf_op jit(solution)/shard_map/ppermute | solution.py:275
  21.4 0.1 copy.18
  21.5 2.3 %broadcast_select_fusion = bf16[16,2,162,128]{3,1,2,0:T(2,128)(2,1)} fusion(pred[16]{0:T(512)(128)(4,1)S(1)} %fusion.5, bf16[2,162,128]{2,0,1:T(2,128)(2,1)S(1)} %copy.18, bf16[2,162,128]{2,0,1:T(2,128)(2,1)S(1)} %copy.17), kind=kLoop, calls=%fused_computation | loop fusion | flops 663552 | bytes 1493008 | tf_op jit(solution)/shard_map/jit(_where)/select_n | solution.py:283
  23.7 0.0 copy-start.5
  23.8 0.0 copy-start.6
  23.8 7.5 %all-to-all-start = ((bf16[16,2,162,128]{3,1,2,0:T(2,128)(2,1)}), bf16[16,2,162,128]{3,1,2,0:T(2,128)(2,1)S(1)}, u32[]{:S(2)}, u32[]{:S(2)}) async-start(bf16[16,2,162,128]{3,1,2,0:T(2,128)(2,1)} %broadcast_select_fusion), calls=%async_computation | async-start | bytes 2654208 | tf_op jit(solution)/shard_map/all_to_all | solution.py:285
  31.3 0.0 copy-start
  31.3 0.0 copy-start.1
  31.3 0.0 copy-done.5
  31.3 0.6 dynamic_slice.15
  33.9 0.0 copy-done.6
  33.9 0.6 dynamic_slice.13
  35.1 14.7 %all-to-all-done = bf16[16,2,162,128]{3,1,2,0:T(2,128)(2,1)S(1)} async-done(((bf16[16,2,162,128]{3,1,2,0:T(2,128)(2,1)}), bf16[16,2,162,128]{3,1,2,0:T(2,128)(2,1)S(1)}, u32[]{:S(2)}, u32[]{:S(2)}) %all-to-all-start) | async-done | bytes 1327136 | tf_op jit(solution)/shard_map/all_to_all | solution.py:285
  49.8 0.1 constant_dynamic-slice_fusion
  49.9 0.0 copy-start.4
  50.0 9.6 %collective-permute-start.5 = (bf16[1,162,128]{2,1,0:T(8,128)(2,1)S(1)}, bf16[1,162,128]{2,1,0:T(8,128)(2,1)S(1)}, u32[]{:S(2)}, u32[]{:S(2)}) collective-permute-start(bf16[1,162,128]{2,1,0:T(8,128)(2,1)S(1)} %fusion.1), channel_id=1, source_target_pairs={{0,8},{1,9},{2,10},{3,11},{4,12},{5,13},{6,14},{7,15},{8,0},{9,1},... | collective-permute-start | bytes 124424 | tf_op jit(solution)/shard_map/ppermute | solution.py:275
  59.6 2.7 %collective-permute-done.5 = bf16[1,162,128]{2,1,0:T(8,128)(2,1)S(1)} collective-permute-done((bf16[1,162,128]{2,1,0:T(8,128)(2,1)S(1)}, bf16[1,162,128]{2,1,0:T(8,128)(2,1)S(1)}, u32[]{:S(2)}, u32[]{:S(2)}) %collective-permute-start.5) | collective-permute-done | bytes 41504 | tf_op jit(solution)/shard_map/ppermute | solution.py:275
  62.3 7.2 %collective-permute-start.6 = (bf16[2,162,128]{2,1,0:T(8,128)(2,1)S(1)}, bf16[2,162,128]{2,1,0:T(8,128)(2,1)S(1)}, u32[]{:S(2)}, u32[]{:S(2)}) collective-permute-start(bf16[2,162,128]{2,1,0:T(8,128)(2,1)S(1)} %pad_maximum_fusion.3), channel_id=1, source_target_pairs={{0,4},{1,5},{2,6},{3,7},{4,0},{5,1},{6,2},{7,3},{8,12},{9,13},{10,... | collective-permute-start | bytes 248840 | tf_op jit(solution)/shard_map/ppermute | solution.py:275
  69.5 2.9 %collective-permute-done.6 = bf16[2,162,128]{2,1,0:T(8,128)(2,1)S(1)} collective-permute-done((bf16[2,162,128]{2,1,0:T(8,128)(2,1)S(1)}, bf16[2,162,128]{2,1,0:T(8,128)(2,1)S(1)}, u32[]{:S(2)}, u32[]{:S(2)}) %collective-permute-start.6) | collective-permute-done | bytes 82976 | tf_op jit(solution)/shard_map/ppermute | solution.py:275
  72.4 1.9 %collective-permute-start.7 = (bf16[4,162,128]{2,1,0:T(8,128)(2,1)S(1)}, bf16[4,162,128]{2,1,0:T(8,128)(2,1)S(1)}, u32[]{:S(2)}, u32[]{:S(2)}) collective-permute-start(bf16[4,162,128]{2,1,0:T(8,128)(2,1)S(1)} %pad_maximum_fusion.1), channel_id=1, source_target_pairs={{0,2},{1,3},{2,0},{3,1},{4,6},{5,7},{6,4},{7,5},{8,10},{9,11},{10,... | collective-permute-start | bytes 497672 | tf_op jit(solution)/shard_map/ppermute | solution.py:275
  74.3 5.4 %collective-permute-done.7 = bf16[4,162,128]{2,1,0:T(8,128)(2,1)S(1)} collective-permute-done((bf16[4,162,128]{2,1,0:T(8,128)(2,1)S(1)}, bf16[4,162,128]{2,1,0:T(8,128)(2,1)S(1)}, u32[]{:S(2)}, u32[]{:S(2)}) %collective-permute-start.7) | collective-permute-done | bytes 165920 | tf_op jit(solution)/shard_map/ppermute | solution.py:275
  79.7 1.9 %collective-permute-start.8 = (bf16[8,162,128]{2,1,0:T(8,128)(2,1)S(1)}, bf16[8,162,128]{2,1,0:T(8,128)(2,1)S(1)}, u32[]{:S(2)}, u32[]{:S(2)}) collective-permute-start(bf16[8,162,128]{2,1,0:T(8,128)(2,1)S(1)} %pad_maximum_fusion.held_ref), channel_id=1, source_target_pairs={{0,1},{1,0},{2,3},{3,2},{4,5},{5,4},{6,7},{7,6},{8,9},{9,8},{10,11... | collective-permute-start | bytes 995336 | tf_op jit(solution)/shard_map/ppermute | solution.py:275
  81.7 0.0 copy-done
  81.7 2.4 %collective-permute-start.1 = (bf16[4,64,256]{2,1,0:T(8,128)(2,1)S(1)}, bf16[4,64,256]{2,1,0:T(8,128)(2,1)S(1)}, u32[]{:S(2)}, u32[]{:S(2)}) collective-permute-start(bf16[4,64,256]{2,1,0:T(8,128)(2,1)S(1)} %bitcast.47), channel_id=1, source_target_pairs={{0,1},{1,2},{2,3},{3,4},{4,5},{5,6},{6,7},{7,8},{8,9},{9,10},{10,1... | collective-permute-start | bytes 393224 | tf_op jit(solution)/shard_map/ppermute | solution.py:308
  84.1 1.3 collective-permute-start.2
  85.4 4.2 %collective-permute-start = (bf16[1,64,256]{2,1,0:T(8,128)(2,1)S(1)}, bf16[1,64,256]{2,1,0:T(8,128)(2,1)S(1)}, u32[]{:S(2)}, u32[]{:S(2)}) collective-permute-start(bf16[1,64,256]{2,1,0:T(8,128)(2,1)S(1)} %get-tuple-element.14), channel_id=1, source_target_pairs={{0,2},{1,3},{2,4},{3,5},{4,6},{5,7},{6,8},{7,9},{8,10},{9,11},{10,... | collective-permute-start | bytes 98312 | tf_op jit(solution)/shard_map/ppermute | solution.py:308
  89.6 1.3 collective-permute-start.3
  90.9 0.0 copy-done.1
  90.9 0.1 copy.21
  91.1 0.1 copy.22.critic_ref
  91.2 0.0 collective-permute-done.far_low
  91.2 5.7 %collective-permute-done.3.far_high = bf16[1,64,256]{2,1,0:T(8,128)(2,1)S(1)} collective-permute-done((bf16[1,64,256]{2,1,0:T(8,128)(2,1)S(1)}, bf16[1,64,256]{2,1,0:T(8,128)(2,1)S(1)}, u32[]{:S(2)}, u32[]{:S(2)}) %collective-permute-start.3) | collective-permute-done | bytes 32800 | tf_op jit(solution)/shard_map/ppermute | solution.py:308
  96.9 0.0 collective-permute-done.1.low
  96.9 0.0 collective-permute-done.2.high
  96.9 0.0 collective-permute-done.8.got_ref
  96.9 0.0 copy-done.4
  96.9 0.1 broadcast_in_dim.41.score_ref
  97.0 7.2 %local_step.1 = (bf16[4,64,256]{2,1,0:T(8,128)(2,1)}, f32[8,162,128]{2,1,0:T(8,128)S(1)}, bf16[8,162,128]{2,1,0:T(8,128)(2,1)S(1)}) custom-call(s32[1]{0:T(128)} %bitcast.slab_ref, bf16[1,64,256]{2,1,0:T(8,128)(2,1)S(1)} %collective-permute-done.far_low, bf16[4,64,256]{2,1,0:T(8,128)(2,1)S(1)} %collective-permute-done.1.low, ...), custom_call_target="tpu_custom_call" | custom-call | flops 6000000000 | bytes 4000000 | tf_op jit(solution)/shard_map/local_step/pallas_call | solution.py:240
  104.2 1.9 %collective-permute-start.9 = (bf16[8,162,128]{2,1,0:T(8,128)(2,1)S(1)}, bf16[8,162,128]{2,1,0:T(8,128)(2,1)S(1)}, u32[]{:S(2)}, u32[]{:S(2)}) collective-permute-start(bf16[8,162,128]{2,1,0:T(8,128)(2,1)S(1)} %get-tuple-element.8), channel_id=1, source_target_pairs={{0,1},{1,0},{2,3},{3,2},{4,5},{5,4},{6,7},{7,6},{8,9},{9,8},{10,11... | collective-permute-start | bytes 995336 | tf_op jit(solution)/shard_map/ppermute | solution.py:275
  106.1 1.6 %collective-permute-done.9 = bf16[8,162,128]{2,1,0:T(8,128)(2,1)S(1)} collective-permute-done((bf16[8,162,128]{2,1,0:T(8,128)(2,1)S(1)}, bf16[8,162,128]{2,1,0:T(8,128)(2,1)S(1)}, u32[]{:S(2)}, u32[]{:S(2)}) %collective-permute-start.9) | collective-permute-done | bytes 331808 | tf_op jit(solution)/shard_map/ppermute | solution.py:275
  107.7 0.1 convert_add_fusion
  107.8 0.0 copy-start.2
  107.8 0.0 copy-start.3
  107.8 4.1 %collective-permute-start.10 = (bf16[4,162,128]{2,1,0:T(8,128)(2,1)S(1)}, bf16[4,162,128]{2,1,0:T(8,128)(2,1)S(1)}, u32[]{:S(2)}, u32[]{:S(2)}) collective-permute-start(bf16[4,162,128]{2,1,0:T(8,128)(2,1)S(1)} %slice.77), channel_id=1, source_target_pairs={{0,2},{1,3},{2,0},{3,1},{4,6},{5,7},{6,4},{7,5},{8,10},{9,11},{10,... | collective-permute-start | bytes 497672 | tf_op jit(solution)/shard_map/ppermute | solution.py:275
  111.9 4.7 %collective-permute-done.10 = bf16[4,162,128]{2,1,0:T(8,128)(2,1)S(1)} collective-permute-done((bf16[4,162,128]{2,1,0:T(8,128)(2,1)S(1)}, bf16[4,162,128]{2,1,0:T(8,128)(2,1)S(1)}, u32[]{:S(2)}, u32[]{:S(2)}) %collective-permute-start.10) | collective-permute-done | bytes 165920 | tf_op jit(solution)/shard_map/ppermute | solution.py:275
  116.6 6.4 %collective-permute-start.11 = (bf16[2,162,128]{2,1,0:T(8,128)(2,1)S(1)}, bf16[2,162,128]{2,1,0:T(8,128)(2,1)S(1)}, u32[]{:S(2)}, u32[]{:S(2)}) collective-permute-start(bf16[2,162,128]{2,1,0:T(8,128)(2,1)S(1)} %slice.78), channel_id=1, source_target_pairs={{0,4},{1,5},{2,6},{3,7},{4,0},{5,1},{6,2},{7,3},{8,12},{9,13},{10,... | collective-permute-start | bytes 248840 | tf_op jit(solution)/shard_map/ppermute | solution.py:275
  123.0 4.1 %collective-permute-done.11 = bf16[2,162,128]{2,1,0:T(8,128)(2,1)S(1)} collective-permute-done((bf16[2,162,128]{2,1,0:T(8,128)(2,1)S(1)}, bf16[2,162,128]{2,1,0:T(8,128)(2,1)S(1)}, u32[]{:S(2)}, u32[]{:S(2)}) %collective-permute-start.11) | collective-permute-done | bytes 82976 | tf_op jit(solution)/shard_map/ppermute | solution.py:275
  127.2 4.9 %collective-permute-start.12 = (bf16[1,162,128]{2,1,0:T(8,128)(2,1)S(1)}, bf16[1,162,128]{2,1,0:T(8,128)(2,1)S(1)}, u32[]{:S(2)}, u32[]{:S(2)}) collective-permute-start(bf16[1,162,128]{2,1,0:T(8,128)(2,1)S(1)} %slice.79), channel_id=1, source_target_pairs={{0,8},{1,9},{2,10},{3,11},{4,12},{5,13},{6,14},{7,15},{8,0},{9,1},... | collective-permute-start | bytes 124424 | tf_op jit(solution)/shard_map/ppermute | solution.py:275
  132.1 5.8 %collective-permute-done.12 = bf16[1,162,128]{2,1,0:T(8,128)(2,1)S(1)} collective-permute-done((bf16[1,162,128]{2,1,0:T(8,128)(2,1)S(1)}, bf16[1,162,128]{2,1,0:T(8,128)(2,1)S(1)}, u32[]{:S(2)}, u32[]{:S(2)}) %collective-permute-start.12) | collective-permute-done | bytes 41504 | tf_op jit(solution)/shard_map/ppermute | solution.py:275
  137.9 0.0 copy-done.2
  137.9 0.0 copy-done.3
  137.9 1.0 fusion.2
  (16 shorter events, 0.3 us)
Async XLA Ops:
  2.9 18.5 %collective-permute-start.4 = (bf16[2,162,128]{2,1,0:T(8,128)(2,1)S(1)}, bf16[2,162,128]{2,1,0:T(8,128)(2,1)S(1)}, u32[]{:S(2)}, u32[]{:S(2)}) collective-permute-start(bf16[2,162,128]{2,1,0:T(8,128)(2,1)S(1)} %pad_maximum_fusion.2), channel_id=1, source_target_pairs={{0,256},{16,272},{32,288},{48,304},{64,320},{80,336},{96,352},{112... | collective-permute-start | bytes 248840 | tf_op jit(solution)/shard_map/ppermute | solution.py:275
  23.7 7.5 %copy-start.5 = (s32[32]{0:T(128)S(1)}, s32[32]{0:T(128)}, u32[]{:S(2)}) copy-start(s32[32]{0:T(128)} %param.12) | copy-start | bytes 388
  23.8 10.1 %copy-start.6 = (s32[32]{0:T(128)S(1)}, s32[32]{0:T(128)}, u32[]{:S(2)}) copy-start(s32[32]{0:T(128)} %param.13) | copy-start | bytes 388
  23.8 26.1 %all-to-all-start = ((bf16[16,2,162,128]{3,1,2,0:T(2,128)(2,1)}), bf16[16,2,162,128]{3,1,2,0:T(2,128)(2,1)S(1)}, u32[]{:S(2)}, u32[]{:S(2)}) async-start(bf16[16,2,162,128]{3,1,2,0:T(2,128)(2,1)} %broadcast_select_fusion), calls=%async_computation | async-start | bytes 2654208 | tf_op jit(solution)/shard_map/all_to_all | solution.py:285
  31.3 50.4 %copy-start = (bf16[1,4,64,256]{3,2,1,0:T(8,128)(2,1)S(1)}, bf16[1,4,64,256]{3,2,1,0:T(8,128)(2,1)}, u32[]{:S(2)}) copy-start(bf16[1,4,64,256]{3,2,1,0:T(8,128)(2,1)} %param.7) | copy-start | bytes 393220
  31.3 59.6 %copy-start.1 = (bf16[1,8,128,64]{2,3,1,0:T(8,128)(2,1)S(1)}, bf16[1,8,128,64]{2,3,1,0:T(8,128)(2,1)}, u32[]{:S(2)}) copy-start(bf16[1,8,128,64]{2,3,1,0:T(8,128)(2,1)} %param.10) | copy-start | bytes 393220
  49.9 47.0 %copy-start.4 = (f32[1,128]{1,0:T(1,128)S(1)}, f32[1,128]{1,0:T(1,128)}, u32[]{:S(2)}) copy-start(f32[1,128]{1,0:T(1,128)} %param.11) | copy-start | bytes 1540
  50.0 12.3 %collective-permute-start.5 = (bf16[1,162,128]{2,1,0:T(8,128)(2,1)S(1)}, bf16[1,162,128]{2,1,0:T(8,128)(2,1)S(1)}, u32[]{:S(2)}, u32[]{:S(2)}) collective-permute-start(bf16[1,162,128]{2,1,0:T(8,128)(2,1)S(1)} %fusion.1), channel_id=1, source_target_pairs={{0,8},{1,9},{2,10},{3,11},{4,12},{5,13},{6,14},{7,15},{8,0},{9,1},... | collective-permute-start | bytes 124424 | tf_op jit(solution)/shard_map/ppermute | solution.py:275
  62.3 10.1 %collective-permute-start.6 = (bf16[2,162,128]{2,1,0:T(8,128)(2,1)S(1)}, bf16[2,162,128]{2,1,0:T(8,128)(2,1)S(1)}, u32[]{:S(2)}, u32[]{:S(2)}) collective-permute-start(bf16[2,162,128]{2,1,0:T(8,128)(2,1)S(1)} %pad_maximum_fusion.3), channel_id=1, source_target_pairs={{0,4},{1,5},{2,6},{3,7},{4,0},{5,1},{6,2},{7,3},{8,12},{9,13},{10,... | collective-permute-start | bytes 248840 | tf_op jit(solution)/shard_map/ppermute | solution.py:275
  72.4 7.3 %collective-permute-start.7 = (bf16[4,162,128]{2,1,0:T(8,128)(2,1)S(1)}, bf16[4,162,128]{2,1,0:T(8,128)(2,1)S(1)}, u32[]{:S(2)}, u32[]{:S(2)}) collective-permute-start(bf16[4,162,128]{2,1,0:T(8,128)(2,1)S(1)} %pad_maximum_fusion.1), channel_id=1, source_target_pairs={{0,2},{1,3},{2,0},{3,1},{4,6},{5,7},{6,4},{7,5},{8,10},{9,11},{10,... | collective-permute-start | bytes 497672 | tf_op jit(solution)/shard_map/ppermute | solution.py:275
  79.7 17.2 %collective-permute-start.8 = (bf16[8,162,128]{2,1,0:T(8,128)(2,1)S(1)}, bf16[8,162,128]{2,1,0:T(8,128)(2,1)S(1)}, u32[]{:S(2)}, u32[]{:S(2)}) collective-permute-start(bf16[8,162,128]{2,1,0:T(8,128)(2,1)S(1)} %pad_maximum_fusion.held_ref), channel_id=1, source_target_pairs={{0,1},{1,0},{2,3},{3,2},{4,5},{5,4},{6,7},{7,6},{8,9},{9,8},{10,11... | collective-permute-start | bytes 995336 | tf_op jit(solution)/shard_map/ppermute | solution.py:275
  81.7 15.3 %collective-permute-start.1 = (bf16[4,64,256]{2,1,0:T(8,128)(2,1)S(1)}, bf16[4,64,256]{2,1,0:T(8,128)(2,1)S(1)}, u32[]{:S(2)}, u32[]{:S(2)}) collective-permute-start(bf16[4,64,256]{2,1,0:T(8,128)(2,1)S(1)} %bitcast.47), channel_id=1, source_target_pairs={{0,1},{1,2},{2,3},{3,4},{4,5},{5,6},{6,7},{7,8},{8,9},{9,10},{10,1... | collective-permute-start | bytes 393224 | tf_op jit(solution)/shard_map/ppermute | solution.py:308
  84.1 12.8 %collective-permute-start.2 = (bf16[4,64,256]{2,1,0:T(8,128)(2,1)S(1)}, bf16[4,64,256]{2,1,0:T(8,128)(2,1)S(1)}, u32[]{:S(2)}, u32[]{:S(2)}) collective-permute-start(bf16[4,64,256]{2,1,0:T(8,128)(2,1)S(1)} %bitcast.48), channel_id=1, source_target_pairs={{1,0},{2,1},{3,2},{4,3},{5,4},{6,5},{7,6},{8,7},{9,8},{10,9},{11,1... | collective-permute-start | bytes 393224 | tf_op jit(solution)/shard_map/ppermute | solution.py:308
  85.4 5.8 %collective-permute-start = (bf16[1,64,256]{2,1,0:T(8,128)(2,1)S(1)}, bf16[1,64,256]{2,1,0:T(8,128)(2,1)S(1)}, u32[]{:S(2)}, u32[]{:S(2)}) collective-permute-start(bf16[1,64,256]{2,1,0:T(8,128)(2,1)S(1)} %get-tuple-element.14), channel_id=1, source_target_pairs={{0,2},{1,3},{2,4},{3,5},{4,6},{5,7},{6,8},{7,9},{8,10},{9,11},{10,... | collective-permute-start | bytes 98312 | tf_op jit(solution)/shard_map/ppermute | solution.py:308
  89.6 7.3 %collective-permute-start.3 = (bf16[1,64,256]{2,1,0:T(8,128)(2,1)S(1)}, bf16[1,64,256]{2,1,0:T(8,128)(2,1)S(1)}, u32[]{:S(2)}, u32[]{:S(2)}) collective-permute-start(bf16[1,64,256]{2,1,0:T(8,128)(2,1)S(1)} %get-tuple-element.13), channel_id=1, source_target_pairs={{2,0},{3,1},{4,2},{5,3},{6,4},{7,5},{8,6},{9,7},{10,8},{11,9},{12,... | collective-permute-start | bytes 98312 | tf_op jit(solution)/shard_map/ppermute | solution.py:308
  104.2 3.5 %collective-permute-start.9 = (bf16[8,162,128]{2,1,0:T(8,128)(2,1)S(1)}, bf16[8,162,128]{2,1,0:T(8,128)(2,1)S(1)}, u32[]{:S(2)}, u32[]{:S(2)}) collective-permute-start(bf16[8,162,128]{2,1,0:T(8,128)(2,1)S(1)} %get-tuple-element.8), channel_id=1, source_target_pairs={{0,1},{1,0},{2,3},{3,2},{4,5},{5,4},{6,7},{7,6},{8,9},{9,8},{10,11... | collective-permute-start | bytes 995336 | tf_op jit(solution)/shard_map/ppermute | solution.py:275
  107.8 30.1 %copy-start.2 = (f32[1,20736]{1,0:T(1,128)S(1)}, f32[1,20736]{1,0:T(1,128)}, u32[]{:S(2)}) copy-start(f32[1,20736]{1,0:T(1,128)} %param.8) | copy-start | bytes 248836
  107.8 30.1 %copy-start.3 = (f32[1,20736]{1,0:T(1,128)S(1)}, f32[1,20736]{1,0:T(1,128)}, u32[]{:S(2)}) copy-start(f32[1,20736]{1,0:T(1,128)} %param.9) | copy-start | bytes 248836
  107.8 8.7 %collective-permute-start.10 = (bf16[4,162,128]{2,1,0:T(8,128)(2,1)S(1)}, bf16[4,162,128]{2,1,0:T(8,128)(2,1)S(1)}, u32[]{:S(2)}, u32[]{:S(2)}) collective-permute-start(bf16[4,162,128]{2,1,0:T(8,128)(2,1)S(1)} %slice.77), channel_id=1, source_target_pairs={{0,2},{1,3},{2,0},{3,1},{4,6},{5,7},{6,4},{7,5},{8,10},{9,11},{10,... | collective-permute-start | bytes 497672 | tf_op jit(solution)/shard_map/ppermute | solution.py:275
  116.6 10.5 %collective-permute-start.11 = (bf16[2,162,128]{2,1,0:T(8,128)(2,1)S(1)}, bf16[2,162,128]{2,1,0:T(8,128)(2,1)S(1)}, u32[]{:S(2)}, u32[]{:S(2)}) collective-permute-start(bf16[2,162,128]{2,1,0:T(8,128)(2,1)S(1)} %slice.78), channel_id=1, source_target_pairs={{0,4},{1,5},{2,6},{3,7},{4,0},{5,1},{6,2},{7,3},{8,12},{9,13},{10,... | collective-permute-start | bytes 248840 | tf_op jit(solution)/shard_map/ppermute | solution.py:275
  127.2 10.7 %collective-permute-start.12 = (bf16[1,162,128]{2,1,0:T(8,128)(2,1)S(1)}, bf16[1,162,128]{2,1,0:T(8,128)(2,1)S(1)}, u32[]{:S(2)}, u32[]{:S(2)}) collective-permute-start(bf16[1,162,128]{2,1,0:T(8,128)(2,1)S(1)} %slice.79), channel_id=1, source_target_pairs={{0,8},{1,9},{2,10},{3,11},{4,12},{5,13},{6,14},{7,15},{8,0},{9,1},... | collective-permute-start | bytes 124424 | tf_op jit(solution)/shard_map/ppermute | solution.py:275

commit v3 on v2

--- a/solution.py
+++ b/solution.py
@@ -88,7 +88,7 @@
 
     for block in range(SLABS):
         apart = block ^ slab
-        slot = ((apart >> 1) & 1) * 4 + ((apart >> 2) & 1) * 2 + ((apart >> 3) & 1)
+        slot = ((apart >> 1) & 1) * 4 + ((apart >> 2) & 1) * 2 + block // 8
         piece = jnp.where(
             (apart & 1) == 1,
             got_ref[slot].astype(jnp.float32),
@@ -222,16 +222,15 @@
 
     for block in range(SLABS):
         apart = block ^ slab
-        slot = ((apart >> 1) & 1) * 4 + ((apart >> 2) & 1) * 2 + ((apart >> 3) & 1)
         piece = flat[block * ROWS : (block + 1) * ROWS, :]
 
         @pl.when((apart & 1) == 1)
         def _():
-            send_ref[slot] = piece.astype(jnp.bfloat16)
+            send_ref[block // 2] = piece.astype(jnp.bfloat16)
 
         @pl.when((apart & 1) == 0)
         def _():
-            keep_ref[slot] = piece
+            keep_ref[block // 2] = piece
 
 
 def local_step(slab, pieces, held, got, critic, critic_back, score):
@@ -275,31 +274,32 @@
     return lax.ppermute(value, axis, [(i, target_of(i)) for i in range(count)])
 
 
-def fetch_partner(value, pairing):
-    rank = lax.axis_index("trainer")
-    half = rank // 16
-    across = move(value, "trainer", lambda i: i ^ 16)
-    wanted = lax.dynamic_slice_in_dim(pairing, half * 16, 16) // 16 == half
-    slots = jnp.where(wanted.reshape((16,) + (1,) * value.ndim), value[None], across[None])
+def plane_exchange(slots):
     groups = [list(range(16)), list(range(16, 32))]
-    heard = lax.all_to_all(slots, "trainer", 0, 0, axis_index_groups=groups)
-    return lax.dynamic_index_in_dim(heard, pairing[rank] % 16, 0, keepdims=False)
-
-
-def gather_depth(block):
-    held = block[None]
-    for mask in (8, 4, 2):
-        held = jnp.concatenate([held, move(held, "depth", lambda i: i ^ mask)])
-    return held, move(held, "depth", lambda i: i ^ 1)
-
-
-def scatter_depth(keep, send):
-    keep = keep + move(send, "depth", lambda i: i ^ 1).astype(jnp.float32)
-    for mask in (2, 4, 8):
-        size = keep.shape[0] // 2
-        send = keep[size:].astype(jnp.bfloat16)
-        keep = keep[:size] + move(send, "depth", lambda i: i ^ mask).astype(jnp.float32)
-    return keep[0]
+    return lax.all_to_all(slots, "trainer", 0, 0, axis_index_groups=groups)
+
+
+def source_of(trainer, pairing, flags):
+    return jnp.where(flags[trainer] == 1, trainer, pairing[trainer])
+
+
+def far_exchange(slots):
+    depth = lax.axis_size("depth")
+    groups = [
+        [(t + s) * depth + d + e for s in (0, 16) for e in (0, 8)]
+        for t in range(16)
+        for d in range(8)
+    ]
+    return lax.all_to_all(slots, ("trainer", "depth"), 0, 0, axis_index_groups=groups)
+
+
+def sum_depth(keep, send):
+    groups = [list(range(core, 16, 2)) for core in range(2)]
+    mine = keep + move(send, "depth", lambda i: i ^ 1).astype(jnp.float32)
+    heard = lax.all_to_all(
+        mine.astype(jnp.bfloat16), "depth", 0, 0, axis_index_groups=groups
+    )
+    return jnp.sum(heard.astype(jnp.float32), axis=0)
 
 
 def shifted(value, by):
@@ -316,14 +316,24 @@
 
 
 def on_device(noise, gen_weight, gen_momentum, disc_weight, score_weight, pairing, flags):
-    keeper = flags[lax.axis_index("trainer")] == 1
+    together = lax.optimization_barrier
+    rank = lax.axis_index("trainer")
+    slab = lax.axis_index("depth").astype(jnp.int32)
+    half = rank // 16
     own_weight = gen_weight.reshape(ROWS, ROW)
     own_moment = gen_momentum.reshape(ROWS, ROW)
-    sent = jnp.stack([own_weight, own_moment]).astype(jnp.bfloat16)
-    other = fetch_partner(sent, pairing).astype(jnp.float32)
-    chosen_weight = jnp.where(keeper, own_weight, other[0])
-    chosen_momentum = jnp.where(keeper, own_moment, other[1])
-    latent = noise[0]
+    sent_moment = own_moment.astype(jnp.bfloat16)
+    heard = plane_exchange(
+        jnp.broadcast_to(own_weight.astype(jnp.bfloat16)[None], (16, ROWS, ROW))
+    )
+    across = move(sent_moment, "trainer", lambda i: i ^ 16)
+    latent, heard, across = together((noise[0], heard, across))
+    source = source_of(rank, pairing, flags)
+    other_source = source_of(rank ^ 16, pairing, flags)
+    for_own = lax.dynamic_index_in_dim(heard, source % 16, 0)
+    for_other = lax.dynamic_index_in_dim(heard, other_source % 16, 0)
+    to_own = (jnp.arange(4) // 2 == half)[:, None, None]
+    got = far_exchange(jnp.where(to_own, for_own, for_other))
     pieces = (
         shifted(latent[PLANES - 1 :], 2),
         shifted(latent, 1),
@@ -333,10 +343,27 @@
     )
     critic, critic_back = critic_forms(disc_weight[0])
     score = jnp.broadcast_to(score_weight[0][:, None], (ROW, ROW))
-    held, got = gather_depth(chosen_weight.astype(jnp.bfloat16))
-    slab = lax.axis_index("depth").astype(jnp.int32).reshape(1)
-    generated, keep, send = local_step(slab, pieces, held, got, critic, critic_back, score)
-    grad_share = scatter_depth(keep, send)
+    got, pieces, critic, critic_back, score, across = together(
+        (got, pieces, critic, critic_back, score, across)
+    )
+    held = lax.dynamic_slice_in_dim(got, 2 * (source // 16), 2, 0)
+    other_weight = lax.dynamic_index_in_dim(held, slab // 8, 0, keepdims=False)
+    wanted = lax.dynamic_slice_in_dim(pairing, half * 16, 16) // 16 == half
+    heard_moment = plane_exchange(
+        jnp.where(wanted[:, None, None], sent_moment[None], across[None])
+    )
+    for mask in (4, 2):
+        held = jnp.concatenate([held, move(held, "depth", lambda i: i ^ mask)])
+    near = move(held, "depth", lambda i: i ^ 1)
+    generated, keep, send = local_step(
+        slab.reshape(1), pieces, held, near, critic, critic_back, score
+    )
+    keep, send, heard_moment = together((keep, send, heard_moment))
+    grad_share = sum_depth(keep, send)
+    other_moment = lax.dynamic_index_in_dim(heard_moment, pairing[rank] % 16, 0, keepdims=False)
+    keeper = flags[rank] == 1
+    chosen_weight = jnp.where(keeper, own_weight, other_weight.astype(jnp.float32))
+    chosen_momentum = jnp.where(keeper, own_moment, other_moment.astype(jnp.float32))
     new_momentum = momentum_decay * chosen_momentum + grad_share
     new_weight = chosen_weight - step_length * new_momentum
     return (

time: 140 us -> 131 us (0.936)
  waiting for transfers between devices: 49.6 us -> 39.7 us
  between operations: 3.61 us -> 5.6 us
    ppermute x9 -> x5, starting transfers between devices: 53.6 us -> 24.2 us  [move(): return lax.ppermute(value, axis, [(i, target_of(i)) for i in range(count)])]
    all_to_all x1 -> x4, starting transfers between devices: 7.52 us -> 34.9 us  [the longest x2 16.5 us: plane_exchange(): return lax.all_to_all(slots, 'trainer', 0, 0, axis_index_groups=groups)]
    ppermute x9 -> x5, waiting for transfers between devices: 29.1 us -> 9.81 us  [move(): return lax.ppermute(value, axis, [(i, target_of(i)) for i in range(count)])]
    all_to_all x1 -> x4, waiting for transfers between devices: 14.7 us -> 28.5 us  [the longest x1 19.3 us: sum_depth(): lax.all_to_all(mine.astype(jnp.bfloat16), 'depth', 0, 0, axis_index_group...]
    ppermute x4, waiting for transfers between devices: 5.72 us -> 1.33 us  [shifted(): return lax.ppermute(value, 'depth', links)]
    convert_element_type x2 -> x3, other arithmetic: 0.03 us -> 2.13 us  [the longest x1 1.11 us: on_device(): own_weight.astype(jnp.bfloat16)[None]]
    ppermute x4, starting transfers between devices: 9.16 us -> 10.9 us  [shifted(): return lax.ppermute(value, 'depth', links)]
  transfers between devices with their start and end apart: 14 -> 13, of which waited for: 10 -> 7; matrix products, arithmetic and copies ran while one was open for 2% -> 2% of each run, Pallas kernels for 0% -> 5%
where the time goes in v3:
time: 131 us; the launch traced here: 130 us
  starting transfers between devices  69.9 us (53%)
  waiting for transfers between devices  39.7 us (30%)
  Pallas kernels  7.1 us (5%)
  between operations  5.6 us (4%)
  other arithmetic  5.12 us (4%)
  local copies, waits for them, and re-layouts  2.71 us (2%)
    ppermute x5, starting transfers between devices, move(): return lax.ppermute(value, axis, [(i, target_of(i)) for i in range(count)])  24.2 us
    all_to_all x1, waiting for transfers between devices, sum_depth(): lax.all_to_all(mine.astype(jnp.bfloat16), 'depth', 0, 0, axis_index_group...  19.3 us
    all_to_all x2, starting transfers between devices, plane_exchange(): return lax.all_to_all(slots, 'trainer', 0, 0, axis_index_groups=groups)  16.5 us
    ppermute x4, starting transfers between devices, shifted(): return lax.ppermute(value, 'depth', links)  10.9 us
    all_to_all x1, starting transfers between devices, far_exchange(): lax.all_to_all(slots, ('trainer', 'depth'), 0, 0, axis_index_groups=groups)  10.4 us
    ppermute x5, waiting for transfers between devices, move(): return lax.ppermute(value, axis, [(i, target_of(i)) for i in range(count)])  9.81 us
    all_to_all x1, starting transfers between devices, sum_depth(): lax.all_to_all(mine.astype(jnp.bfloat16), 'depth', 0, 0, axis_index_group...  7.92 us
    pallas_call x1, Pallas kernels, local_step(): pl.pallas_call(local_kernel, out_shape=(jax.ShapeDtypeStruct((PLANES, CH,...  7.1 us
  transfers between devices with their start and end apart: 13, of which 7 were waited for; matrix products, arithmetic and copies ran while one was open for 2% of the time, Pallas kernels for 5%

profile of v3, /device:TPU:8, one launch (start us, length us, event | category | flops | bytes accessed | tf_op | source)
XLA Modules:
  0.0 130.1 jit_solution(1836483240121317568)
XLA Ops:
  0.6 1.1 convert_reduce_fusion.2
  1.7 1.0 broadcast_in_dim.73
  2.7 0.0 copy-start.3
  2.7 9.3 %all-to-all-start = ((bf16[16,162,128]{2,1,0:T(8,128)(2,1)}), bf16[16,162,128]{2,1,0:T(8,128)(2,1)S(1)}, u32[]{:S(2)}, u32[]{:S(2)}) async-start(bf16[16,162,128]{2,1,0:T(8,128)(2,1)} %broadcast_in_dim.73), calls=%async_computation | async-start | bytes 1376256 | tf_op jit(solution)/shard_map/all_to_all | solution.py:279
  12.0 0.0 copy-done.3
  12.0 0.2 convert_reduce_fusion.1
  12.2 13.9 %collective-permute-start = (bf16[162,128]{1,0:T(8,128)(2,1)S(1)}, bf16[162,128]{1,0:T(8,128)(2,1)S(1)}, u32[]{:S(2)}, u32[]{:S(2)}) collective-permute-start(bf16[162,128]{1,0:T(8,128)(2,1)S(1)} %bitcast.50), channel_id=1, source_target_pairs={{0,256},{16,272},{32,288},{48,304},{64,320},{80,336},{96,352},{112... | collective-permute-start | bytes 124424 | tf_op jit(solution)/shard_map/ppermute | solution.py:274
  26.2 0.0 copy-start.4
  26.2 0.0 copy-start.5
  26.3 0.6 copy-done.4
  26.9 0.0 copy-done.5
  26.9 0.7 fusion.7
  30.3 0.0 collective-permute-done
  30.3 0.0 all-to-all-done
  30.3 0.7 broadcast_select_fusion.1
  31.0 0.0 copy-start
  31.0 10.4 %all-to-all-start.1 = ((bf16[4,162,128]{2,1,0:T(8,128)(2,1)}), bf16[4,162,128]{2,1,0:T(8,128)(2,1)S(1)}, u32[]{:S(2)}, u32[]{:S(2)}) async-start(bf16[4,162,128]{2,1,0:T(8,128)(2,1)} %broadcast_select_fusion.1), calls=%async_computation.1 | async-start | bytes 344064 | tf_op jit(solution)/shard_map/all_to_all | solution.py:293
  41.4 0.0 copy-done
  41.4 0.0 copy-start.1
  41.4 1.4 %collective-permute-start.3 = (bf16[4,64,256]{2,1,0:T(8,128)(2,1)S(1)}, bf16[4,64,256]{2,1,0:T(8,128)(2,1)S(1)}, u32[]{:S(2)}, u32[]{:S(2)}) collective-permute-start(bf16[4,64,256]{2,1,0:T(8,128)(2,1)S(1)} %bitcast.40), channel_id=1, source_target_pairs={{1,0},{2,1},{3,2},{4,3},{5,4},{6,5},{7,6},{8,7},{9,8},{10,9},{11,1... | collective-permute-start | bytes 393224 | tf_op jit(solution)/shard_map/ppermute | solution.py:308
  42.9 3.0 %collective-permute-start.2 = (bf16[4,64,256]{2,1,0:T(8,128)(2,1)S(1)}, bf16[4,64,256]{2,1,0:T(8,128)(2,1)S(1)}, u32[]{:S(2)}, u32[]{:S(2)}) collective-permute-start(bf16[4,64,256]{2,1,0:T(8,128)(2,1)S(1)} %bitcast.41), channel_id=1, source_target_pairs={{0,1},{1,2},{2,3},{3,4},{4,5},{5,6},{6,7},{7,8},{8,9},{9,10},{10,1... | collective-permute-start | bytes 393224 | tf_op jit(solution)/shard_map/ppermute | solution.py:308
  45.9 1.3 collective-permute-start.4
  47.2 5.1 %collective-permute-start.1 = (bf16[1,64,256]{2,1,0:T(8,128)(2,1)S(1)}, bf16[1,64,256]{2,1,0:T(8,128)(2,1)S(1)}, u32[]{:S(2)}, u32[]{:S(2)}) collective-permute-start(bf16[1,64,256]{2,1,0:T(8,128)(2,1)S(1)} %get-tuple-element.46), channel_id=1, source_target_pairs={{0,2},{1,3},{2,4},{3,5},{4,6},{5,7},{6,8},{7,9},{8,10},{9,11},{10,... | collective-permute-start | bytes 98312 | tf_op jit(solution)/shard_map/ppermute | solution.py:308
  52.4 0.0 copy-done.1
  52.4 0.1 copy.15
  52.6 0.0 copy-start.6
  52.6 0.0 collective-permute-done.4.far_high
  52.6 1.3 %collective-permute-done.1.far_low = bf16[1,64,256]{2,1,0:T(8,128)(2,1)S(1)} collective-permute-done((bf16[1,64,256]{2,1,0:T(8,128)(2,1)S(1)}, bf16[1,64,256]{2,1,0:T(8,128)(2,1)S(1)}, u32[]{:S(2)}, u32[]{:S(2)}) %collective-permute-start.1) | collective-permute-done | bytes 32800 | tf_op jit(solution)/shard_map/ppermute | solution.py:308
  54.0 0.0 collective-permute-done.3.high
  54.0 0.0 collective-permute-done.2.low
  54.0 3.7 %all-to-all-done.1 = bf16[4,162,128]{2,1,0:T(8,128)(2,1)S(1)} async-done(((bf16[4,162,128]{2,1,0:T(8,128)(2,1)}), bf16[4,162,128]{2,1,0:T(8,128)(2,1)S(1)}, u32[]{:S(2)}, u32[]{:S(2)}) %all-to-all-start.1) | async-done | bytes 165920 | tf_op jit(solution)/shard_map/all_to_all | solution.py:293
  57.7 0.0 copy-done.6
  57.7 0.1 broadcast_in_dim.79.score_ref
  57.8 2.4 %collective-permute-start.5 = (bf16[2,162,128]{2,1,0:T(8,128)(2,1)S(1)}, bf16[2,162,128]{2,1,0:T(8,128)(2,1)S(1)}, u32[]{:S(2)}, u32[]{:S(2)}) collective-permute-start(bf16[2,162,128]{2,1,0:T(8,128)(2,1)S(1)} %constant_dynamic-slice_fusion), channel_id=1, source_target_pairs={{0,4},{1,5},{2,6},{3,7},{4,0},{5,1},{6,2},{7,3},{8,12},{9,13},{10,... | collective-permute-start | bytes 248840 | tf_op jit(solution)/shard_map/ppermute | solution.py:274
  60.3 4.8 %collective-permute-done.5 = bf16[2,162,128]{2,1,0:T(8,128)(2,1)S(1)} collective-permute-done((bf16[2,162,128]{2,1,0:T(8,128)(2,1)S(1)}, bf16[2,162,128]{2,1,0:T(8,128)(2,1)S(1)}, u32[]{:S(2)}, u32[]{:S(2)}) %collective-permute-start.5) | collective-permute-done | bytes 82976 | tf_op jit(solution)/shard_map/ppermute | solution.py:274
  65.1 4.0 %collective-permute-start.6 = (bf16[4,162,128]{2,1,0:T(8,128)(2,1)S(1)}, bf16[4,162,128]{2,1,0:T(8,128)(2,1)S(1)}, u32[]{:S(2)}, u32[]{:S(2)}) collective-permute-start(bf16[4,162,128]{2,1,0:T(8,128)(2,1)S(1)} %pad_maximum_fusion.1), channel_id=1, source_target_pairs={{0,2},{1,3},{2,0},{3,1},{4,6},{5,7},{6,4},{7,5},{8,10},{9,11},{10,... | collective-permute-start | bytes 497672 | tf_op jit(solution)/shard_map/ppermute | solution.py:274
  69.1 3.4 %collective-permute-done.6 = bf16[4,162,128]{2,1,0:T(8,128)(2,1)S(1)} collective-permute-done((bf16[4,162,128]{2,1,0:T(8,128)(2,1)S(1)}, bf16[4,162,128]{2,1,0:T(8,128)(2,1)S(1)}, u32[]{:S(2)}, u32[]{:S(2)}) %collective-permute-start.6) | collective-permute-done | bytes 165920 | tf_op jit(solution)/shard_map/ppermute | solution.py:274
  72.5 1.9 %collective-permute-start.7 = (bf16[8,162,128]{2,1,0:T(8,128)(2,1)S(1)}, bf16[8,162,128]{2,1,0:T(8,128)(2,1)S(1)}, u32[]{:S(2)}, u32[]{:S(2)}) collective-permute-start(bf16[8,162,128]{2,1,0:T(8,128)(2,1)S(1)} %pad_maximum_fusion.held_ref), channel_id=1, source_target_pairs={{0,1},{1,0},{2,3},{3,2},{4,5},{5,4},{6,7},{7,6},{8,9},{9,8},{10,11... | collective-permute-start | bytes 995336 | tf_op jit(solution)/shard_map/ppermute | solution.py:274
  74.4 0.1 fusion.4
  74.5 1.0 broadcast_select_fusion
  75.5 7.2 %all-to-all-start.2 = ((bf16[16,162,128]{2,1,0:T(8,128)(2,1)}), bf16[16,162,128]{2,1,0:T(8,128)(2,1)S(1)}, u32[]{:S(2)}, u32[]{:S(2)}) async-start(bf16[16,162,128]{2,1,0:T(8,128)(2,1)} %broadcast_select_fusion), calls=%async_computation.2 | async-start | bytes 1376256 | tf_op jit(solution)/shard_map/all_to_all | solution.py:279
  82.7 0.1 copy.16.critic_ref
  82.9 0.0 collective-permute-done.7.got_ref
  82.9 7.1 %local_step.1 = (bf16[4,64,256]{2,1,0:T(8,128)(2,1)}, f32[8,162,128]{2,1,0:T(8,128)S(1)}, bf16[8,162,128]{2,1,0:T(8,128)(2,1)S(1)}) custom-call(s32[1]{0:T(128)} %bitcast.slab_ref, bf16[1,64,256]{2,1,0:T(8,128)(2,1)S(1)} %collective-permute-done.1.far_low, bf16[4,64,256]{2,1,0:T(8,128)(2,1)S(1)} %collective-permute-done.2.low, ...), custom_call_target="tpu_custom_call" | custom-call | flops 6000000000 | bytes 4000000 | tf_op jit(solution)/shard_map/local_step/pallas_call | solution.py:239
  90.0 5.5 %all-to-all-done.2 = bf16[16,162,128]{2,1,0:T(8,128)(2,1)S(1)} async-done(((bf16[16,162,128]{2,1,0:T(8,128)(2,1)}), bf16[16,162,128]{2,1,0:T(8,128)(2,1)S(1)}, u32[]{:S(2)}, u32[]{:S(2)}) %all-to-all-start.2) | async-done | bytes 663584 | tf_op jit(solution)/shard_map/all_to_all | solution.py:279
  95.5 1.9 %collective-permute-start.8 = (bf16[8,162,128]{2,1,0:T(8,128)(2,1)S(1)}, bf16[8,162,128]{2,1,0:T(8,128)(2,1)S(1)}, u32[]{:S(2)}, u32[]{:S(2)}) collective-permute-start(bf16[8,162,128]{2,1,0:T(8,128)(2,1)S(1)} %get-tuple-element.40), channel_id=1, source_target_pairs={{0,1},{1,0},{2,3},{3,2},{4,5},{5,4},{6,7},{7,6},{8,9},{9,8},{10,11... | collective-permute-start | bytes 995336 | tf_op jit(solution)/shard_map/ppermute | solution.py:274
  97.4 1.6 %collective-permute-done.8 = bf16[8,162,128]{2,1,0:T(8,128)(2,1)S(1)} collective-permute-done((bf16[8,162,128]{2,1,0:T(8,128)(2,1)S(1)}, bf16[8,162,128]{2,1,0:T(8,128)(2,1)S(1)}, u32[]{:S(2)}, u32[]{:S(2)}) %collective-permute-start.8) | collective-permute-done | bytes 331808 | tf_op jit(solution)/shard_map/ppermute | solution.py:274
  99.0 0.8 add_convert_fusion
  99.8 7.9 %all-to-all-start.3 = ((bf16[8,162,128]{2,1,0:T(8,128)(2,1)}), bf16[8,162,128]{2,1,0:T(8,128)(2,1)S(1)}, u32[]{:S(2)}, u32[]{:S(2)}) async-start(bf16[8,162,128]{2,1,0:T(8,128)(2,1)} %add_convert_fusion), calls=%async_computation.3 | async-start | bytes 688128 | tf_op jit(solution)/shard_map/all_to_all | solution.py:299
  109.8 0.0 copy-start.2
  109.8 19.3 %all-to-all-done.3 = bf16[8,162,128]{2,1,0:T(8,128)(2,1)S(1)} async-done(((bf16[8,162,128]{2,1,0:T(8,128)(2,1)}), bf16[8,162,128]{2,1,0:T(8,128)(2,1)S(1)}, u32[]{:S(2)}, u32[]{:S(2)}) %all-to-all-start.3) | async-done | bytes 331808 | tf_op jit(solution)/shard_map/all_to_all | solution.py:299
  129.1 0.0 copy-done.2
  129.1 1.0 fusion
  (11 shorter events, 0.2 us)
Async XLA Ops:
  2.7 9.3 %copy-start.3 = (f32[1,20736]{1,0:T(1,128)S(1)}, f32[1,20736]{1,0:T(1,128)}, u32[]{:S(2)}) copy-start(f32[1,20736]{1,0:T(1,128)} %param.9) | copy-start | bytes 248836
  2.7 27.6 %all-to-all-start = ((bf16[16,162,128]{2,1,0:T(8,128)(2,1)}), bf16[16,162,128]{2,1,0:T(8,128)(2,1)S(1)}, u32[]{:S(2)}, u32[]{:S(2)}) async-start(bf16[16,162,128]{2,1,0:T(8,128)(2,1)} %broadcast_in_dim.73), calls=%async_computation | async-start | bytes 1376256 | tf_op jit(solution)/shard_map/all_to_all | solution.py:279
  12.2 18.0 %collective-permute-start = (bf16[162,128]{1,0:T(8,128)(2,1)S(1)}, bf16[162,128]{1,0:T(8,128)(2,1)S(1)}, u32[]{:S(2)}, u32[]{:S(2)}) collective-permute-start(bf16[162,128]{1,0:T(8,128)(2,1)S(1)} %bitcast.50), channel_id=1, source_target_pairs={{0,256},{16,272},{32,288},{48,304},{64,320},{80,336},{96,352},{112... | collective-permute-start | bytes 124424 | tf_op jit(solution)/shard_map/ppermute | solution.py:274
  26.2 0.7 copy-start.4
  26.2 0.7 copy-start.5
  31.0 10.4 %copy-start = (bf16[1,4,64,256]{3,2,1,0:T(8,128)(2,1)S(1)}, bf16[1,4,64,256]{3,2,1,0:T(8,128)(2,1)}, u32[]{:S(2)}) copy-start(bf16[1,4,64,256]{3,2,1,0:T(8,128)(2,1)} %param.7) | copy-start | bytes 393220
  31.0 26.7 %all-to-all-start.1 = ((bf16[4,162,128]{2,1,0:T(8,128)(2,1)}), bf16[4,162,128]{2,1,0:T(8,128)(2,1)S(1)}, u32[]{:S(2)}, u32[]{:S(2)}) async-start(bf16[4,162,128]{2,1,0:T(8,128)(2,1)} %broadcast_select_fusion.1), calls=%async_computation.1 | async-start | bytes 344064 | tf_op jit(solution)/shard_map/all_to_all | solution.py:293
  41.4 11.0 %copy-start.1 = (bf16[1,8,128,64]{2,3,1,0:T(8,128)(2,1)S(1)}, bf16[1,8,128,64]{2,3,1,0:T(8,128)(2,1)}, u32[]{:S(2)}) copy-start(bf16[1,8,128,64]{2,3,1,0:T(8,128)(2,1)} %param.10) | copy-start | bytes 393220
  41.4 12.5 %collective-permute-start.3 = (bf16[4,64,256]{2,1,0:T(8,128)(2,1)S(1)}, bf16[4,64,256]{2,1,0:T(8,128)(2,1)S(1)}, u32[]{:S(2)}, u32[]{:S(2)}) collective-permute-start(bf16[4,64,256]{2,1,0:T(8,128)(2,1)S(1)} %bitcast.40), channel_id=1, source_target_pairs={{1,0},{2,1},{3,2},{4,3},{5,4},{6,5},{7,6},{8,7},{9,8},{10,9},{11,1... | collective-permute-start | bytes 393224 | tf_op jit(solution)/shard_map/ppermute | solution.py:308
  42.9 11.1 %collective-permute-start.2 = (bf16[4,64,256]{2,1,0:T(8,128)(2,1)S(1)}, bf16[4,64,256]{2,1,0:T(8,128)(2,1)S(1)}, u32[]{:S(2)}, u32[]{:S(2)}) collective-permute-start(bf16[4,64,256]{2,1,0:T(8,128)(2,1)S(1)} %bitcast.41), channel_id=1, source_target_pairs={{0,1},{1,2},{2,3},{3,4},{4,5},{5,6},{6,7},{7,8},{8,9},{9,10},{10,1... | collective-permute-start | bytes 393224 | tf_op jit(solution)/shard_map/ppermute | solution.py:308
  45.9 6.7 %collective-permute-start.4 = (bf16[1,64,256]{2,1,0:T(8,128)(2,1)S(1)}, bf16[1,64,256]{2,1,0:T(8,128)(2,1)S(1)}, u32[]{:S(2)}, u32[]{:S(2)}) collective-permute-start(bf16[1,64,256]{2,1,0:T(8,128)(2,1)S(1)} %get-tuple-element.45), channel_id=1, source_target_pairs={{2,0},{3,1},{4,2},{5,3},{6,4},{7,5},{8,6},{9,7},{10,8},{11,9},{12,... | collective-permute-start | bytes 98312 | tf_op jit(solution)/shard_map/ppermute | solution.py:308
  47.2 6.7 %collective-permute-start.1 = (bf16[1,64,256]{2,1,0:T(8,128)(2,1)S(1)}, bf16[1,64,256]{2,1,0:T(8,128)(2,1)S(1)}, u32[]{:S(2)}, u32[]{:S(2)}) collective-permute-start(bf16[1,64,256]{2,1,0:T(8,128)(2,1)S(1)} %get-tuple-element.46), channel_id=1, source_target_pairs={{0,2},{1,3},{2,4},{3,5},{4,6},{5,7},{6,8},{7,9},{8,10},{9,11},{10,... | collective-permute-start | bytes 98312 | tf_op jit(solution)/shard_map/ppermute | solution.py:308
  52.6 5.1 %copy-start.6 = (f32[1,128]{1,0:T(1,128)S(1)}, f32[1,128]{1,0:T(1,128)}, u32[]{:S(2)}) copy-start(f32[1,128]{1,0:T(1,128)} %param.11) | copy-start | bytes 1540
  57.8 7.3 %collective-permute-start.5 = (bf16[2,162,128]{2,1,0:T(8,128)(2,1)S(1)}, bf16[2,162,128]{2,1,0:T(8,128)(2,1)S(1)}, u32[]{:S(2)}, u32[]{:S(2)}) collective-permute-start(bf16[2,162,128]{2,1,0:T(8,128)(2,1)S(1)} %constant_dynamic-slice_fusion), channel_id=1, source_target_pairs={{0,4},{1,5},{2,6},{3,7},{4,0},{5,1},{6,2},{7,3},{8,12},{9,13},{10,... | collective-permute-start | bytes 248840 | tf_op jit(solution)/shard_map/ppermute | solution.py:274
  65.1 7.3 %collective-permute-start.6 = (bf16[4,162,128]{2,1,0:T(8,128)(2,1)S(1)}, bf16[4,162,128]{2,1,0:T(8,128)(2,1)S(1)}, u32[]{:S(2)}, u32[]{:S(2)}) collective-permute-start(bf16[4,162,128]{2,1,0:T(8,128)(2,1)S(1)} %pad_maximum_fusion.1), channel_id=1, source_target_pairs={{0,2},{1,3},{2,0},{3,1},{4,6},{5,7},{6,4},{7,5},{8,10},{9,11},{10,... | collective-permute-start | bytes 497672 | tf_op jit(solution)/shard_map/ppermute | solution.py:274
  72.5 10.4 %collective-permute-start.7 = (bf16[8,162,128]{2,1,0:T(8,128)(2,1)S(1)}, bf16[8,162,128]{2,1,0:T(8,128)(2,1)S(1)}, u32[]{:S(2)}, u32[]{:S(2)}) collective-permute-start(bf16[8,162,128]{2,1,0:T(8,128)(2,1)S(1)} %pad_maximum_fusion.held_ref), channel_id=1, source_target_pairs={{0,1},{1,0},{2,3},{3,2},{4,5},{5,4},{6,7},{7,6},{8,9},{9,8},{10,11... | collective-permute-start | bytes 995336 | tf_op jit(solution)/shard_map/ppermute | solution.py:274
  75.5 20.0 %all-to-all-start.2 = ((bf16[16,162,128]{2,1,0:T(8,128)(2,1)}), bf16[16,162,128]{2,1,0:T(8,128)(2,1)S(1)}, u32[]{:S(2)}, u32[]{:S(2)}) async-start(bf16[16,162,128]{2,1,0:T(8,128)(2,1)} %broadcast_select_fusion), calls=%async_computation.2 | async-start | bytes 1376256 | tf_op jit(solution)/shard_map/all_to_all | solution.py:279
  95.5 3.5 %collective-permute-start.8 = (bf16[8,162,128]{2,1,0:T(8,128)(2,1)S(1)}, bf16[8,162,128]{2,1,0:T(8,128)(2,1)S(1)}, u32[]{:S(2)}, u32[]{:S(2)}) collective-permute-start(bf16[8,162,128]{2,1,0:T(8,128)(2,1)S(1)} %get-tuple-element.40), channel_id=1, source_target_pairs={{0,1},{1,0},{2,3},{3,2},{4,5},{5,4},{6,7},{7,6},{8,9},{9,8},{10,11... | collective-permute-start | bytes 995336 | tf_op jit(solution)/shard_map/ppermute | solution.py:274
  99.8 29.2 %all-to-all-start.3 = ((bf16[8,162,128]{2,1,0:T(8,128)(2,1)}), bf16[8,162,128]{2,1,0:T(8,128)(2,1)S(1)}, u32[]{:S(2)}, u32[]{:S(2)}) async-start(bf16[8,162,128]{2,1,0:T(8,128)(2,1)} %add_convert_fusion), calls=%async_computation.3 | async-start | bytes 688128 | tf_op jit(solution)/shard_map/all_to_all | solution.py:299
  109.8 19.3 %copy-start.2 = (f32[1,20736]{1,0:T(1,128)S(1)}, f32[1,20736]{1,0:T(1,128)}, u32[]{:S(2)}) copy-start(f32[1,20736]{1,0:T(1,128)} %param.8) | copy-start | bytes 248836

commit v4 on v3

--- a/solution.py
+++ b/solution.py
@@ -6,6 +6,7 @@
 from jax.experimental import pallas as pl
 from jax.experimental.pallas import tpu as pltpu
 from jax.sharding import PartitionSpec as P
+
 
 CH = 64
 ROW = 128
@@ -315,25 +316,15 @@
     return forward, backward
 
 
-def on_device(noise, gen_weight, gen_momentum, disc_weight, score_weight, pairing, flags):
+def one_step(noise, gen_weight, gen_momentum, disc_weight, score_weight, pairing, flags):
     together = lax.optimization_barrier
     rank = lax.axis_index("trainer")
     slab = lax.axis_index("depth").astype(jnp.int32)
     half = rank // 16
     own_weight = gen_weight.reshape(ROWS, ROW)
     own_moment = gen_momentum.reshape(ROWS, ROW)
-    sent_moment = own_moment.astype(jnp.bfloat16)
-    heard = plane_exchange(
-        jnp.broadcast_to(own_weight.astype(jnp.bfloat16)[None], (16, ROWS, ROW))
-    )
-    across = move(sent_moment, "trainer", lambda i: i ^ 16)
-    latent, heard, across = together((noise[0], heard, across))
-    source = source_of(rank, pairing, flags)
-    other_source = source_of(rank ^ 16, pairing, flags)
-    for_own = lax.dynamic_index_in_dim(heard, source % 16, 0)
-    for_other = lax.dynamic_index_in_dim(heard, other_source % 16, 0)
-    to_own = (jnp.arange(4) // 2 == half)[:, None, None]
-    got = far_exchange(jnp.where(to_own, for_own, for_other))
+    latent = noise[0]
+    heard = plane_exchange(jnp.broadcast_to(own_weight.astype(jnp.bfloat16)[None], (16, ROWS, ROW)))
     pieces = (
         shifted(latent[PLANES - 1 :], 2),
         shifted(latent, 1),
@@ -341,17 +332,24 @@
         shifted(latent, -1),
         shifted(latent[:1], -2),
     )
+    source = source_of(rank, pairing, flags)
+    other_source = source_of(rank ^ 16, pairing, flags)
+    to_own = jnp.arange(4) // 2 == half
+    heard, pieces, source, other_source, to_own = together(
+        (heard, pieces, source, other_source, to_own)
+    )
+    for_own = lax.dynamic_index_in_dim(heard, source % 16, 0)
+    for_other = lax.dynamic_index_in_dim(heard, other_source % 16, 0)
+    got = far_exchange(jnp.where(to_own[:, None, None], for_own, for_other))
     critic, critic_back = critic_forms(disc_weight[0])
     score = jnp.broadcast_to(score_weight[0][:, None], (ROW, ROW))
-    got, pieces, critic, critic_back, score, across = together(
-        (got, pieces, critic, critic_back, score, across)
+    moment_slots = jnp.broadcast_to(own_moment.astype(jnp.bfloat16)[None], (16, ROWS, ROW))
+    got, critic, critic_back, score, moment_slots = together(
+        (got, critic, critic_back, score, moment_slots)
     )
     held = lax.dynamic_slice_in_dim(got, 2 * (source // 16), 2, 0)
     other_weight = lax.dynamic_index_in_dim(held, slab // 8, 0, keepdims=False)
-    wanted = lax.dynamic_slice_in_dim(pairing, half * 16, 16) // 16 == half
-    heard_moment = plane_exchange(
-        jnp.where(wanted[:, None, None], sent_moment[None], across[None])
-    )
+    heard_moment = plane_exchange(moment_slots)
     for mask in (4, 2):
         held = jnp.concatenate([held, move(held, "depth", lambda i: i ^ mask)])
     near = move(held, "depth", lambda i: i ^ 1)
@@ -360,7 +358,10 @@
     )
     keep, send, heard_moment = together((keep, send, heard_moment))
     grad_share = sum_depth(keep, send)
-    other_moment = lax.dynamic_index_in_dim(heard_moment, pairing[rank] % 16, 0, keepdims=False)
+    moment_own = lax.dynamic_index_in_dim(heard_moment, source % 16, 0, keepdims=False)
+    moment_other = lax.dynamic_index_in_dim(heard_moment, other_source % 16, 0, keepdims=False)
+    moment_far = move(moment_other, "trainer", lambda i: i ^ 16)
+    other_moment = jnp.where(source // 16 == half, moment_own, moment_far)
     keeper = flags[rank] == 1
     chosen_weight = jnp.where(keeper, own_weight, other_weight.astype(jnp.float32))
     chosen_momentum = jnp.where(keeper, own_moment, other_moment.astype(jnp.float32))
@@ -384,7 +385,7 @@
         P(),
     )
     return jax.shard_map(
-        on_device,
+        one_step,
         mesh=mesh,
         in_specs=placed,
         out_specs=(P("trainer", "depth", None, None), P("trainer", "depth"), P("trainer", "depth")),

time: 131 us -> 133 us (1.015)
  the two profiles are of different devices: /device:TPU:8 before, /device:TPU:65 now
where the time goes in v4:
time: 133 us; the launch traced here: 132 us
  starting transfers between devices  67.2 us (51%)
  waiting for transfers between devices  45.7 us (34%)
  Pallas kernels  7.1 us (5%)
  local copies, waits for them, and re-layouts  5.72 us (4%)
  between operations  3.5 us (3%)
  other arithmetic  3.04 us (2%)
    ppermute x5, starting transfers between devices, move(): return lax.ppermute(value, axis, [(i, target_of(i)) for i in range(count)])  23.9 us
    ppermute x5, waiting for transfers between devices, move(): return lax.ppermute(value, axis, [(i, target_of(i)) for i in range(count)])  17 us
    all_to_all x1, waiting for transfers between devices, far_exchange(): lax.all_to_all(slots, ('trainer', 'depth'), 0, 0, axis_index_groups=groups)  14.9 us
    all_to_all x2, starting transfers between devices, plane_exchange(): return lax.all_to_all(slots, 'trainer', 0, 0, axis_index_groups=groups)  14 us
    ppermute x4, starting transfers between devices, shifted(): return lax.ppermute(value, 'depth', links)  13 us
    all_to_all x1, starting transfers between devices, far_exchange(): lax.all_to_all(slots, ('trainer', 'depth'), 0, 0, axis_index_groups=groups)  11.5 us
    all_to_all x1, waiting for transfers between devices, sum_depth(): lax.all_to_all(mine.astype(jnp.bfloat16), 'depth', 0, 0, axis_index_group...  9.17 us
    pallas_call x1, Pallas kernels, local_step(): pl.pallas_call(local_kernel, out_shape=(jax.ShapeDtypeStruct((PLANES, CH,...  7.1 us
  transfers between devices with their start and end apart: 13, of which 7 were waited for; matrix products, arithmetic and copies ran while one was open for 1% of the time, Pallas kernels for 5%

profile of v4, /device:TPU:65, one launch (start us, length us, event | category | flops | bytes accessed | tf_op | source)
XLA Modules:
  0.0 132.2 jit_solution(5456604187201401165)
XLA Ops:
  0.6 1.1 reduce
  1.7 1.0 broadcast_in_dim.51
  2.7 0.0 copy-start
  2.7 6.9 %all-to-all-start = ((bf16[16,162,128]{2,1,0:T(8,128)(2,1)}), bf16[16,162,128]{2,1,0:T(8,128)(2,1)S(1)}, u32[]{:S(2)}, u32[]{:S(2)}) async-start(bf16[16,162,128]{2,1,0:T(8,128)(2,1)} %broadcast_in_dim.51), calls=%async_computation | async-start | bytes 1376256 | tf_op jit(solution)/shard_map/all_to_all | solution.py:280
  9.6 0.0 copy-done
  9.6 2.9 %collective-permute-start.2 = (bf16[4,64,256]{2,1,0:T(8,128)(2,1)S(1)}, bf16[4,64,256]{2,1,0:T(8,128)(2,1)S(1)}, u32[]{:S(2)}, u32[]{:S(2)}) collective-permute-start(bf16[4,64,256]{2,1,0:T(8,128)(2,1)S(1)} %bitcast.64), channel_id=1, source_target_pairs={{1,0},{2,1},{3,2},{4,3},{5,4},{6,5},{7,6},{8,7},{9,8},{10,9},{11,1... | collective-permute-start | bytes 393224 | tf_op jit(solution)/shard_map/ppermute | solution.py:309
  12.5 3.4 %collective-permute-start.1 = (bf16[4,64,256]{2,1,0:T(8,128)(2,1)S(1)}, bf16[4,64,256]{2,1,0:T(8,128)(2,1)S(1)}, u32[]{:S(2)}, u32[]{:S(2)}) collective-permute-start(bf16[4,64,256]{2,1,0:T(8,128)(2,1)S(1)} %bitcast.65), channel_id=1, source_target_pairs={{0,1},{1,2},{2,3},{3,4},{4,5},{5,6},{6,7},{7,8},{8,9},{9,10},{10,1... | collective-permute-start | bytes 393224 | tf_op jit(solution)/shard_map/ppermute | solution.py:309
  15.9 1.9 %collective-permute-start.3 = (bf16[1,64,256]{2,1,0:T(8,128)(2,1)S(1)}, bf16[1,64,256]{2,1,0:T(8,128)(2,1)S(1)}, u32[]{:S(2)}, u32[]{:S(2)}) collective-permute-start(bf16[1,64,256]{2,1,0:T(8,128)(2,1)S(1)} %get-tuple-element.47), channel_id=1, source_target_pairs={{2,0},{3,1},{4,2},{5,3},{6,4},{7,5},{8,6},{9,7},{10,8},{11,9},{12,... | collective-permute-start | bytes 98312 | tf_op jit(solution)/shard_map/ppermute | solution.py:309
  17.9 4.8 %collective-permute-start = (bf16[1,64,256]{2,1,0:T(8,128)(2,1)S(1)}, bf16[1,64,256]{2,1,0:T(8,128)(2,1)S(1)}, u32[]{:S(2)}, u32[]{:S(2)}) collective-permute-start(bf16[1,64,256]{2,1,0:T(8,128)(2,1)S(1)} %get-tuple-element.48), channel_id=1, source_target_pairs={{0,2},{1,3},{2,4},{3,5},{4,6},{5,7},{6,8},{7,9},{8,10},{9,11},{10,... | collective-permute-start | bytes 98312 | tf_op jit(solution)/shard_map/ppermute | solution.py:309
  22.7 0.0 copy-start.3
  22.7 0.0 copy-start.4
  22.7 0.6 copy-done.3
  23.3 0.0 copy-done.4
  23.3 0.6 fusion.6
  26.5 0.0 collective-permute-done.3.far_high
  26.5 0.0 collective-permute-done.far_low
  26.5 0.0 collective-permute-done.2.high
  26.5 0.0 collective-permute-done.1.low
  26.5 0.0 all-to-all-done
  26.6 0.8 broadcast_select_fusion
  27.3 0.0 copy-start.2
  27.3 11.5 %all-to-all-start.1 = ((bf16[4,162,128]{2,1,0:T(8,128)(2,1)}), bf16[4,162,128]{2,1,0:T(8,128)(2,1)S(1)}, u32[]{:S(2)}, u32[]{:S(2)}) async-start(bf16[4,162,128]{2,1,0:T(8,128)(2,1)} %broadcast_select_fusion), calls=%async_computation.1 | async-start | bytes 344064 | tf_op jit(solution)/shard_map/all_to_all | solution.py:294
  38.8 0.0 copy-done.2
  38.8 0.0 copy-start.1
  38.8 0.2 reduce.1
  39.0 0.7 copy-done.1
  39.7 0.1 copy.15
  40.0 0.0 copy-start.5
  40.0 14.9 %all-to-all-done.1 = bf16[4,162,128]{2,1,0:T(8,128)(2,1)S(1)} async-done(((bf16[4,162,128]{2,1,0:T(8,128)(2,1)}), bf16[4,162,128]{2,1,0:T(8,128)(2,1)S(1)}, u32[]{:S(2)}, u32[]{:S(2)}) %all-to-all-start.1) | async-done | bytes 165920 | tf_op jit(solution)/shard_map/all_to_all | solution.py:294
  54.9 0.0 copy-done.5
  54.9 0.1 broadcast_in_dim.58.score_ref
  55.0 1.0 broadcast_in_dim.59
  55.9 1.9 %collective-permute-start.4 = (bf16[2,162,128]{2,1,0:T(8,128)(2,1)S(1)}, bf16[2,162,128]{2,1,0:T(8,128)(2,1)S(1)}, u32[]{:S(2)}, u32[]{:S(2)}) collective-permute-start(bf16[2,162,128]{2,1,0:T(8,128)(2,1)S(1)} %constant_dynamic-slice_fusion), channel_id=1, source_target_pairs={{0,4},{1,5},{2,6},{3,7},{4,0},{5,1},{6,2},{7,3},{8,12},{9,13},{10,... | collective-permute-start | bytes 248840 | tf_op jit(solution)/shard_map/ppermute | solution.py:275
  57.9 4.3 %collective-permute-done.4 = bf16[2,162,128]{2,1,0:T(8,128)(2,1)S(1)} collective-permute-done((bf16[2,162,128]{2,1,0:T(8,128)(2,1)S(1)}, bf16[2,162,128]{2,1,0:T(8,128)(2,1)S(1)}, u32[]{:S(2)}, u32[]{:S(2)}) %collective-permute-start.4) | collective-permute-done | bytes 82976 | tf_op jit(solution)/shard_map/ppermute | solution.py:275
  62.2 5.5 %collective-permute-start.5 = (bf16[4,162,128]{2,1,0:T(8,128)(2,1)S(1)}, bf16[4,162,128]{2,1,0:T(8,128)(2,1)S(1)}, u32[]{:S(2)}, u32[]{:S(2)}) collective-permute-start(bf16[4,162,128]{2,1,0:T(8,128)(2,1)S(1)} %pad_maximum_fusion.1), channel_id=1, source_target_pairs={{0,2},{1,3},{2,0},{3,1},{4,6},{5,7},{6,4},{7,5},{8,10},{9,11},{10,... | collective-permute-start | bytes 497672 | tf_op jit(solution)/shard_map/ppermute | solution.py:275
  67.7 4.4 %collective-permute-done.5 = bf16[4,162,128]{2,1,0:T(8,128)(2,1)S(1)} collective-permute-done((bf16[4,162,128]{2,1,0:T(8,128)(2,1)S(1)}, bf16[4,162,128]{2,1,0:T(8,128)(2,1)S(1)}, u32[]{:S(2)}, u32[]{:S(2)}) %collective-permute-start.5) | collective-permute-done | bytes 165920 | tf_op jit(solution)/shard_map/ppermute | solution.py:275
  72.1 2.8 %collective-permute-start.6 = (bf16[8,162,128]{2,1,0:T(8,128)(2,1)S(1)}, bf16[8,162,128]{2,1,0:T(8,128)(2,1)S(1)}, u32[]{:S(2)}, u32[]{:S(2)}) collective-permute-start(bf16[8,162,128]{2,1,0:T(8,128)(2,1)S(1)} %pad_maximum_fusion.held_ref), channel_id=1, source_target_pairs={{0,1},{1,0},{2,3},{3,2},{4,5},{5,4},{6,7},{7,6},{8,9},{9,8},{10,11... | collective-permute-start | bytes 995336 | tf_op jit(solution)/shard_map/ppermute | solution.py:275
  75.0 7.1 %all-to-all-start.2 = ((bf16[16,162,128]{2,1,0:T(8,128)(2,1)}), bf16[16,162,128]{2,1,0:T(8,128)(2,1)S(1)}, u32[]{:S(2)}, u32[]{:S(2)}) async-start(bf16[16,162,128]{2,1,0:T(8,128)(2,1)} %broadcast_in_dim.59), calls=%async_computation.2 | async-start | bytes 1376256 | tf_op jit(solution)/shard_map/all_to_all | solution.py:280
  82.1 0.1 copy.16.critic_ref
  82.2 0.0 collective-permute-done.6.got_ref
  82.2 7.1 %local_step.1 = (bf16[4,64,256]{2,1,0:T(8,128)(2,1)}, f32[8,162,128]{2,1,0:T(8,128)S(1)}, bf16[8,162,128]{2,1,0:T(8,128)(2,1)S(1)}) custom-call(s32[1]{0:T(128)} %bitcast.slab_ref, bf16[1,64,256]{2,1,0:T(8,128)(2,1)S(1)} %collective-permute-done.far_low, bf16[4,64,256]{2,1,0:T(8,128)(2,1)S(1)} %collective-permute-done.1.low, ...), custom_call_target="tpu_custom_call" | custom-call | flops 6000000000 | bytes 4000000 | tf_op jit(solution)/shard_map/local_step/pallas_call | solution.py:240
  89.3 4.6 %all-to-all-done.2 = bf16[16,162,128]{2,1,0:T(8,128)(2,1)S(1)} async-done(((bf16[16,162,128]{2,1,0:T(8,128)(2,1)}), bf16[16,162,128]{2,1,0:T(8,128)(2,1)S(1)}, u32[]{:S(2)}, u32[]{:S(2)}) %all-to-all-start.2) | async-done | bytes 663584 | tf_op jit(solution)/shard_map/all_to_all | solution.py:280
  93.9 4.5 %collective-permute-start.8 = (bf16[8,162,128]{2,1,0:T(8,128)(2,1)S(1)}, bf16[8,162,128]{2,1,0:T(8,128)(2,1)S(1)}, u32[]{:S(2)}, u32[]{:S(2)}) collective-permute-start(bf16[8,162,128]{2,1,0:T(8,128)(2,1)S(1)} %get-tuple-element.42), channel_id=1, source_target_pairs={{0,1},{1,0},{2,3},{3,2},{4,5},{5,4},{6,7},{7,6},{8,9},{9,8},{10,11... | collective-permute-start | bytes 995336 | tf_op jit(solution)/shard_map/ppermute | solution.py:275
  98.4 1.3 collective-permute-done.8
  99.6 0.8 add_convert_fusion
  100.5 4.8 %all-to-all-start.3 = ((bf16[8,162,128]{2,1,0:T(8,128)(2,1)}), bf16[8,162,128]{2,1,0:T(8,128)(2,1)S(1)}, u32[]{:S(2)}, u32[]{:S(2)}) async-start(bf16[8,162,128]{2,1,0:T(8,128)(2,1)} %add_convert_fusion), calls=%async_computation.3 | async-start | bytes 688128 | tf_op jit(solution)/shard_map/all_to_all | solution.py:300
  105.3 9.2 %collective-permute-start.7 = (bf16[162,128]{1,0:T(8,128)(2,1)S(1)}, bf16[162,128]{1,0:T(8,128)(2,1)S(1)}, u32[]{:S(2)}, u32[]{:S(2)}) collective-permute-start(bf16[162,128]{1,0:T(8,128)(2,1)S(1)} %dynamic-slice_bitcast_fusion), channel_id=1, source_target_pairs={{0,256},{16,272},{32,288},{48,304},{64,320},{80,336},{96,352},{112... | collective-permute-start | bytes 124424 | tf_op jit(solution)/shard_map/ppermute | solution.py:275
  114.5 9.2 %all-to-all-done.3 = bf16[8,162,128]{2,1,0:T(8,128)(2,1)S(1)} async-done(((bf16[8,162,128]{2,1,0:T(8,128)(2,1)}), bf16[8,162,128]{2,1,0:T(8,128)(2,1)S(1)}, u32[]{:S(2)}, u32[]{:S(2)}) %all-to-all-start.3) | async-done | bytes 331808 | tf_op jit(solution)/shard_map/all_to_all | solution.py:300
  123.7 7.0 %collective-permute-done.7 = bf16[162,128]{1,0:T(8,128)(2,1)S(1)} collective-permute-done((bf16[162,128]{1,0:T(8,128)(2,1)S(1)}, bf16[162,128]{1,0:T(8,128)(2,1)S(1)}, u32[]{:S(2)}, u32[]{:S(2)}) %collective-permute-start.7) | collective-permute-done | bytes 41504 | tf_op jit(solution)/shard_map/ppermute | solution.py:275
  130.7 0.7 copy.25
  131.5 0.7 copy.24
  (13 shorter events, 0.2 us)
Async XLA Ops:
  2.7 6.9 %copy-start = (bf16[1,4,64,256]{3,2,1,0:T(8,128)(2,1)S(1)}, bf16[1,4,64,256]{3,2,1,0:T(8,128)(2,1)}, u32[]{:S(2)}) copy-start(bf16[1,4,64,256]{3,2,1,0:T(8,128)(2,1)} %param.7) | copy-start | bytes 393220
  2.7 23.8 %all-to-all-start = ((bf16[16,162,128]{2,1,0:T(8,128)(2,1)}), bf16[16,162,128]{2,1,0:T(8,128)(2,1)S(1)}, u32[]{:S(2)}, u32[]{:S(2)}) async-start(bf16[16,162,128]{2,1,0:T(8,128)(2,1)} %broadcast_in_dim.51), calls=%async_computation | async-start | bytes 1376256 | tf_op jit(solution)/shard_map/all_to_all | solution.py:280
  9.6 16.9 %collective-permute-start.2 = (bf16[4,64,256]{2,1,0:T(8,128)(2,1)S(1)}, bf16[4,64,256]{2,1,0:T(8,128)(2,1)S(1)}, u32[]{:S(2)}, u32[]{:S(2)}) collective-permute-start(bf16[4,64,256]{2,1,0:T(8,128)(2,1)S(1)} %bitcast.64), channel_id=1, source_target_pairs={{1,0},{2,1},{3,2},{4,3},{5,4},{6,5},{7,6},{8,7},{9,8},{10,9},{11,1... | collective-permute-start | bytes 393224 | tf_op jit(solution)/shard_map/ppermute | solution.py:309
  12.5 14.0 %collective-permute-start.1 = (bf16[4,64,256]{2,1,0:T(8,128)(2,1)S(1)}, bf16[4,64,256]{2,1,0:T(8,128)(2,1)S(1)}, u32[]{:S(2)}, u32[]{:S(2)}) collective-permute-start(bf16[4,64,256]{2,1,0:T(8,128)(2,1)S(1)} %bitcast.65), channel_id=1, source_target_pairs={{0,1},{1,2},{2,3},{3,4},{4,5},{5,6},{6,7},{7,8},{8,9},{9,10},{10,1... | collective-permute-start | bytes 393224 | tf_op jit(solution)/shard_map/ppermute | solution.py:309
  15.9 10.5 %collective-permute-start.3 = (bf16[1,64,256]{2,1,0:T(8,128)(2,1)S(1)}, bf16[1,64,256]{2,1,0:T(8,128)(2,1)S(1)}, u32[]{:S(2)}, u32[]{:S(2)}) collective-permute-start(bf16[1,64,256]{2,1,0:T(8,128)(2,1)S(1)} %get-tuple-element.47), channel_id=1, source_target_pairs={{2,0},{3,1},{4,2},{5,3},{6,4},{7,5},{8,6},{9,7},{10,8},{11,9},{12,... | collective-permute-start | bytes 98312 | tf_op jit(solution)/shard_map/ppermute | solution.py:309
  17.9 8.6 %collective-permute-start = (bf16[1,64,256]{2,1,0:T(8,128)(2,1)S(1)}, bf16[1,64,256]{2,1,0:T(8,128)(2,1)S(1)}, u32[]{:S(2)}, u32[]{:S(2)}) collective-permute-start(bf16[1,64,256]{2,1,0:T(8,128)(2,1)S(1)} %get-tuple-element.48), channel_id=1, source_target_pairs={{0,2},{1,3},{2,4},{3,5},{4,6},{5,7},{6,8},{7,9},{8,10},{9,11},{10,... | collective-permute-start | bytes 98312 | tf_op jit(solution)/shard_map/ppermute | solution.py:309
  22.7 0.7 copy-start.3
  22.7 0.7 copy-start.4
  27.3 11.5 %copy-start.2 = (f32[1,20736]{1,0:T(1,128)S(1)}, f32[1,20736]{1,0:T(1,128)}, u32[]{:S(2)}) copy-start(f32[1,20736]{1,0:T(1,128)} %param.9) | copy-start | bytes 248836
  27.3 27.6 %all-to-all-start.1 = ((bf16[4,162,128]{2,1,0:T(8,128)(2,1)}), bf16[4,162,128]{2,1,0:T(8,128)(2,1)S(1)}, u32[]{:S(2)}, u32[]{:S(2)}) async-start(bf16[4,162,128]{2,1,0:T(8,128)(2,1)} %broadcast_select_fusion), calls=%async_computation.1 | async-start | bytes 344064 | tf_op jit(solution)/shard_map/all_to_all | solution.py:294
  38.8 0.9 copy-start.1
  40.0 14.9 %copy-start.5 = (f32[1,128]{1,0:T(1,128)S(1)}, f32[1,128]{1,0:T(1,128)}, u32[]{:S(2)}) copy-start(f32[1,128]{1,0:T(1,128)} %param.11) | copy-start | bytes 1540
  55.9 6.2 %collective-permute-start.4 = (bf16[2,162,128]{2,1,0:T(8,128)(2,1)S(1)}, bf16[2,162,128]{2,1,0:T(8,128)(2,1)S(1)}, u32[]{:S(2)}, u32[]{:S(2)}) collective-permute-start(bf16[2,162,128]{2,1,0:T(8,128)(2,1)S(1)} %constant_dynamic-slice_fusion), channel_id=1, source_target_pairs={{0,4},{1,5},{2,6},{3,7},{4,0},{5,1},{6,2},{7,3},{8,12},{9,13},{10,... | collective-permute-start | bytes 248840 | tf_op jit(solution)/shard_map/ppermute | solution.py:275
  62.2 9.9 %collective-permute-start.5 = (bf16[4,162,128]{2,1,0:T(8,128)(2,1)S(1)}, bf16[4,162,128]{2,1,0:T(8,128)(2,1)S(1)}, u32[]{:S(2)}, u32[]{:S(2)}) collective-permute-start(bf16[4,162,128]{2,1,0:T(8,128)(2,1)S(1)} %pad_maximum_fusion.1), channel_id=1, source_target_pairs={{0,2},{1,3},{2,0},{3,1},{4,6},{5,7},{6,4},{7,5},{8,10},{9,11},{10,... | collective-permute-start | bytes 497672 | tf_op jit(solution)/shard_map/ppermute | solution.py:275
  72.1 10.1 %collective-permute-start.6 = (bf16[8,162,128]{2,1,0:T(8,128)(2,1)S(1)}, bf16[8,162,128]{2,1,0:T(8,128)(2,1)S(1)}, u32[]{:S(2)}, u32[]{:S(2)}) collective-permute-start(bf16[8,162,128]{2,1,0:T(8,128)(2,1)S(1)} %pad_maximum_fusion.held_ref), channel_id=1, source_target_pairs={{0,1},{1,0},{2,3},{3,2},{4,5},{5,4},{6,7},{7,6},{8,9},{9,8},{10,11... | collective-permute-start | bytes 995336 | tf_op jit(solution)/shard_map/ppermute | solution.py:275
  75.0 19.0 %all-to-all-start.2 = ((bf16[16,162,128]{2,1,0:T(8,128)(2,1)}), bf16[16,162,128]{2,1,0:T(8,128)(2,1)S(1)}, u32[]{:S(2)}, u32[]{:S(2)}) async-start(bf16[16,162,128]{2,1,0:T(8,128)(2,1)} %broadcast_in_dim.59), calls=%async_computation.2 | async-start | bytes 1376256 | tf_op jit(solution)/shard_map/all_to_all | solution.py:280
  93.9 5.7 %collective-permute-start.8 = (bf16[8,162,128]{2,1,0:T(8,128)(2,1)S(1)}, bf16[8,162,128]{2,1,0:T(8,128)(2,1)S(1)}, u32[]{:S(2)}, u32[]{:S(2)}) collective-permute-start(bf16[8,162,128]{2,1,0:T(8,128)(2,1)S(1)} %get-tuple-element.42), channel_id=1, source_target_pairs={{0,1},{1,0},{2,3},{3,2},{4,5},{5,4},{6,7},{7,6},{8,9},{9,8},{10,11... | collective-permute-start | bytes 995336 | tf_op jit(solution)/shard_map/ppermute | solution.py:275
  100.5 23.2 %all-to-all-start.3 = ((bf16[8,162,128]{2,1,0:T(8,128)(2,1)}), bf16[8,162,128]{2,1,0:T(8,128)(2,1)S(1)}, u32[]{:S(2)}, u32[]{:S(2)}) async-start(bf16[8,162,128]{2,1,0:T(8,128)(2,1)} %add_convert_fusion), calls=%async_computation.3 | async-start | bytes 688128 | tf_op jit(solution)/shard_map/all_to_all | solution.py:300
  105.3 25.4 %collective-permute-start.7 = (bf16[162,128]{1,0:T(8,128)(2,1)S(1)}, bf16[162,128]{1,0:T(8,128)(2,1)S(1)}, u32[]{:S(2)}, u32[]{:S(2)}) collective-permute-start(bf16[162,128]{1,0:T(8,128)(2,1)S(1)} %dynamic-slice_bitcast_fusion), channel_id=1, source_target_pairs={{0,256},{16,272},{32,288},{48,304},{64,320},{80,336},{96,352},{112... | collective-permute-start | bytes 124424 | tf_op jit(solution)/shard_map/ppermute | solution.py:275

commit v5 on v4

--- a/solution.py
+++ b/solution.py
@@ -323,45 +323,47 @@
     half = rank // 16
     own_weight = gen_weight.reshape(ROWS, ROW)
     own_moment = gen_momentum.reshape(ROWS, ROW)
-    latent = noise[0]
+    sent_moment = own_moment.astype(jnp.bfloat16)
     heard = plane_exchange(jnp.broadcast_to(own_weight.astype(jnp.bfloat16)[None], (16, ROWS, ROW)))
-    pieces = (
-        shifted(latent[PLANES - 1 :], 2),
-        shifted(latent, 1),
-        latent,
-        shifted(latent, -1),
-        shifted(latent[:1], -2),
-    )
+    across = move(sent_moment, "trainer", lambda i: i ^ 16)
     source = source_of(rank, pairing, flags)
     other_source = source_of(rank ^ 16, pairing, flags)
     to_own = jnp.arange(4) // 2 == half
-    heard, pieces, source, other_source, to_own = together(
-        (heard, pieces, source, other_source, to_own)
+    wanted = lax.dynamic_slice_in_dim(pairing, half * 16, 16) // 16 == half
+    latent, heard, across, source, other_source, to_own, wanted = together(
+        (noise[0], heard, across, source, other_source, to_own, wanted)
     )
     for_own = lax.dynamic_index_in_dim(heard, source % 16, 0)
     for_other = lax.dynamic_index_in_dim(heard, other_source % 16, 0)
     got = far_exchange(jnp.where(to_own[:, None, None], for_own, for_other))
+    low, high = shifted(latent, 1), shifted(latent, -1)
     critic, critic_back = critic_forms(disc_weight[0])
     score = jnp.broadcast_to(score_weight[0][:, None], (ROW, ROW))
-    moment_slots = jnp.broadcast_to(own_moment.astype(jnp.bfloat16)[None], (16, ROWS, ROW))
-    got, critic, critic_back, score, moment_slots = together(
-        (got, critic, critic_back, score, moment_slots)
+    moment_slots = jnp.where(wanted[:, None, None], sent_moment[None], across[None])
+    got, low, high, critic, critic_back, score, moment_slots, latent = together(
+        (got, low, high, critic, critic_back, score, moment_slots, latent)
     )
     held = lax.dynamic_slice_in_dim(got, 2 * (source // 16), 2, 0)
     other_weight = lax.dynamic_index_in_dim(held, slab // 8, 0, keepdims=False)
     heard_moment = plane_exchange(moment_slots)
-    for mask in (4, 2):
-        held = jnp.concatenate([held, move(held, "depth", lambda i: i ^ mask)])
+    held = jnp.concatenate([held, move(held, "depth", lambda i: i ^ 4)])
+    held = jnp.concatenate([held, move(held, "depth", lambda i: i ^ 2)])
+    far_low = shifted(latent[PLANES - 1 :], 2)
+    far_high = shifted(latent[:1], -2)
+    held, far_low, far_high = together((held, far_low, far_high))
     near = move(held, "depth", lambda i: i ^ 1)
     generated, keep, send = local_step(
-        slab.reshape(1), pieces, held, near, critic, critic_back, score
+        slab.reshape(1),
+        (far_low, low, latent, high, far_high),
+        held,
+        near,
+        critic,
+        critic_back,
+        score,
     )
     keep, send, heard_moment = together((keep, send, heard_moment))
     grad_share = sum_depth(keep, send)
-    moment_own = lax.dynamic_index_in_dim(heard_moment, source % 16, 0, keepdims=False)
-    moment_other = lax.dynamic_index_in_dim(heard_moment, other_source % 16, 0, keepdims=False)
-    moment_far = move(moment_other, "trainer", lambda i: i ^ 16)
-    other_moment = jnp.where(source // 16 == half, moment_own, moment_far)
+    other_moment = lax.dynamic_index_in_dim(heard_moment, pairing[rank] % 16, 0, keepdims=False)
     keeper = flags[rank] == 1
     chosen_weight = jnp.where(keeper, own_weight, other_weight.astype(jnp.float32))
     chosen_momentum = jnp.where(keeper, own_moment, other_moment.astype(jnp.float32))

time: 133 us -> 132 us (level)
  the two profiles are of different devices: /device:TPU:65 before, /device:TPU:8 now
where the time goes in v5:
time: 132 us; the launch traced here: 131 us
  starting transfers between devices  66 us (50%)
  waiting for transfers between devices  42.9 us (32%)
  Pallas kernels  7.1 us (5%)
  between operations  5.58 us (4%)
  other arithmetic  5.12 us (4%)
  local copies, waits for them, and re-layouts  4.19 us (3%)
    ppermute x5, starting transfers between devices, move(): return lax.ppermute(value, axis, [(i, target_of(i)) for i in range(count)])  24.7 us
    all_to_all x1, waiting for transfers between devices, sum_depth(): lax.all_to_all(mine.astype(jnp.bfloat16), 'depth', 0, 0, axis_index_group...  19.3 us
    all_to_all x2, starting transfers between devices, plane_exchange(): return lax.all_to_all(slots, 'trainer', 0, 0, axis_index_groups=groups)  16.6 us
    ppermute x4, starting transfers between devices, shifted(): return lax.ppermute(value, 'depth', links)  10.2 us
    all_to_all x1, waiting for transfers between devices, far_exchange(): lax.all_to_all(slots, ('trainer', 'depth'), 0, 0, axis_index_groups=groups)  9.98 us
    all_to_all x1, starting transfers between devices, far_exchange(): lax.all_to_all(slots, ('trainer', 'depth'), 0, 0, axis_index_groups=groups)  9.68 us
    pallas_call x1, Pallas kernels, local_step(): pl.pallas_call(local_kernel, out_shape=(jax.ShapeDtypeStruct((PLANES, CH,...  7.1 us
    ppermute x5, waiting for transfers between devices, move(): return lax.ppermute(value, axis, [(i, target_of(i)) for i in range(count)])  6.65 us
  transfers between devices with their start and end apart: 13, of which 6 were waited for; matrix products, arithmetic and copies ran while one was open for 2% of the time, Pallas kernels for 5%

profile of v5, /device:TPU:8, one launch (start us, length us, event | category | flops | bytes accessed | tf_op | source)
XLA Modules:
  0.0 130.9 jit_solution(10179463077185129672)
XLA Ops:
  0.6 1.1 convert_reduce_fusion.2
  1.7 1.0 broadcast_in_dim.72
  2.7 0.0 copy-start.3
  2.7 9.3 %all-to-all-start = ((bf16[16,162,128]{2,1,0:T(8,128)(2,1)}), bf16[16,162,128]{2,1,0:T(8,128)(2,1)S(1)}, u32[]{:S(2)}, u32[]{:S(2)}) async-start(bf16[16,162,128]{2,1,0:T(8,128)(2,1)} %broadcast_in_dim.72), calls=%async_computation | async-start | bytes 1376256 | tf_op jit(solution)/shard_map/all_to_all | solution.py:280
  12.0 0.0 copy-done.3
  12.0 0.2 convert_reduce_fusion.1
  12.2 13.9 %collective-permute-start = (bf16[162,128]{1,0:T(8,128)(2,1)S(1)}, bf16[162,128]{1,0:T(8,128)(2,1)S(1)}, u32[]{:S(2)}, u32[]{:S(2)}) collective-permute-start(bf16[162,128]{1,0:T(8,128)(2,1)S(1)} %bitcast.50), channel_id=1, source_target_pairs={{0,256},{16,272},{32,288},{48,304},{64,320},{80,336},{96,352},{112... | collective-permute-start | bytes 124424 | tf_op jit(solution)/shard_map/ppermute | solution.py:275
  26.2 0.0 copy-start.4
  26.2 0.6 copy-done.4
  26.9 0.1 fusion.4
  27.0 0.0 copy-start.5
  27.0 0.7 copy-done.5
  27.6 0.7 fusion.7
  30.9 0.0 collective-permute-done
  30.9 0.0 all-to-all-done
  31.0 0.8 broadcast_select_fusion.1
  31.8 0.0 copy-start.1
  31.8 9.7 %all-to-all-start.1 = ((bf16[4,162,128]{2,1,0:T(8,128)(2,1)}), bf16[4,162,128]{2,1,0:T(8,128)(2,1)S(1)}, u32[]{:S(2)}, u32[]{:S(2)}) async-start(bf16[4,162,128]{2,1,0:T(8,128)(2,1)} %broadcast_select_fusion.1), calls=%async_computation.1 | async-start | bytes 344064 | tf_op jit(solution)/shard_map/all_to_all | solution.py:294
  41.4 0.0 copy-done.1
  41.5 0.1 copy.15
  41.6 0.0 copy-start
  41.7 0.9 copy-done
  42.5 1.3 collective-permute-start.2
  43.8 3.0 %collective-permute-start.1 = (bf16[4,64,256]{2,1,0:T(8,128)(2,1)S(1)}, bf16[4,64,256]{2,1,0:T(8,128)(2,1)S(1)}, u32[]{:S(2)}, u32[]{:S(2)}) collective-permute-start(bf16[4,64,256]{2,1,0:T(8,128)(2,1)S(1)} %bitcast.41), channel_id=1, source_target_pairs={{0,1},{1,2},{2,3},{3,4},{4,5},{5,6},{6,7},{7,8},{8,9},{9,10},{10,1... | collective-permute-start | bytes 393224 | tf_op jit(solution)/shard_map/ppermute | solution.py:309
  46.9 1.0 broadcast_select_fusion
  47.9 0.0 copy-start.6
  47.9 0.0 collective-permute-done.2.high
  47.9 0.0 collective-permute-done.1.low
  47.9 10.0 %all-to-all-done.1 = bf16[4,162,128]{2,1,0:T(8,128)(2,1)S(1)} async-done(((bf16[4,162,128]{2,1,0:T(8,128)(2,1)}), bf16[4,162,128]{2,1,0:T(8,128)(2,1)S(1)}, u32[]{:S(2)}, u32[]{:S(2)}) %all-to-all-start.1) | async-done | bytes 165920 | tf_op jit(solution)/shard_map/all_to_all | solution.py:294
  57.9 0.0 copy-done.6
  57.9 0.1 broadcast_in_dim.79.score_ref
  57.9 2.3 %collective-permute-start.3 = (bf16[2,162,128]{2,1,0:T(8,128)(2,1)S(1)}, bf16[2,162,128]{2,1,0:T(8,128)(2,1)S(1)}, u32[]{:S(2)}, u32[]{:S(2)}) collective-permute-start(bf16[2,162,128]{2,1,0:T(8,128)(2,1)S(1)} %constant_dynamic-slice_fusion), channel_id=1, source_target_pairs={{0,4},{1,5},{2,6},{3,7},{4,0},{5,1},{6,2},{7,3},{8,12},{9,13},{10,... | collective-permute-start | bytes 248840 | tf_op jit(solution)/shard_map/ppermute | solution.py:275
  60.3 5.0 %collective-permute-done.3 = bf16[2,162,128]{2,1,0:T(8,128)(2,1)S(1)} collective-permute-done((bf16[2,162,128]{2,1,0:T(8,128)(2,1)S(1)}, bf16[2,162,128]{2,1,0:T(8,128)(2,1)S(1)}, u32[]{:S(2)}, u32[]{:S(2)}) %collective-permute-start.3) | collective-permute-done | bytes 82976 | tf_op jit(solution)/shard_map/ppermute | solution.py:275
  65.3 4.7 %collective-permute-start.4 = (bf16[4,162,128]{2,1,0:T(8,128)(2,1)S(1)}, bf16[4,162,128]{2,1,0:T(8,128)(2,1)S(1)}, u32[]{:S(2)}, u32[]{:S(2)}) collective-permute-start(bf16[4,162,128]{2,1,0:T(8,128)(2,1)S(1)} %pad_maximum_fusion.1), channel_id=1, source_target_pairs={{0,2},{1,3},{2,0},{3,1},{4,6},{5,7},{6,4},{7,5},{8,10},{9,11},{10,... | collective-permute-start | bytes 497672 | tf_op jit(solution)/shard_map/ppermute | solution.py:275
  70.0 1.3 collective-permute-start.6
  71.3 4.5 %collective-permute-start.5 = (bf16[1,64,256]{2,1,0:T(8,128)(2,1)S(1)}, bf16[1,64,256]{2,1,0:T(8,128)(2,1)S(1)}, u32[]{:S(2)}, u32[]{:S(2)}) collective-permute-start(bf16[1,64,256]{2,1,0:T(8,128)(2,1)S(1)} %get-tuple-element.56), channel_id=1, source_target_pairs={{0,2},{1,3},{2,4},{3,5},{4,6},{5,7},{6,8},{7,9},{8,10},{9,11},{10,... | collective-permute-start | bytes 98312 | tf_op jit(solution)/shard_map/ppermute | solution.py:309
  75.8 0.0 collective-permute-done.4
  75.9 0.0 collective-permute-done.6.far_high
  75.9 1.5 %collective-permute-done.5.far_low = bf16[1,64,256]{2,1,0:T(8,128)(2,1)S(1)} collective-permute-done((bf16[1,64,256]{2,1,0:T(8,128)(2,1)S(1)}, bf16[1,64,256]{2,1,0:T(8,128)(2,1)S(1)}, u32[]{:S(2)}, u32[]{:S(2)}) %collective-permute-start.5) | collective-permute-done | bytes 32800 | tf_op jit(solution)/shard_map/ppermute | solution.py:309
  77.4 1.9 %collective-permute-start.7 = (bf16[8,162,128]{2,1,0:T(8,128)(2,1)S(1)}, bf16[8,162,128]{2,1,0:T(8,128)(2,1)S(1)}, u32[]{:S(2)}, u32[]{:S(2)}) collective-permute-start(bf16[8,162,128]{2,1,0:T(8,128)(2,1)S(1)} %pad_maximum_fusion.held_ref), channel_id=1, source_target_pairs={{0,1},{1,0},{2,3},{3,2},{4,5},{5,4},{6,7},{7,6},{8,9},{9,8},{10,11... | collective-permute-start | bytes 995336 | tf_op jit(solution)/shard_map/ppermute | solution.py:275
  79.3 7.2 %all-to-all-start.2 = ((bf16[16,162,128]{2,1,0:T(8,128)(2,1)}), bf16[16,162,128]{2,1,0:T(8,128)(2,1)S(1)}, u32[]{:S(2)}, u32[]{:S(2)}) async-start(bf16[16,162,128]{2,1,0:T(8,128)(2,1)} %broadcast_select_fusion), calls=%async_computation.2 | async-start | bytes 1376256 | tf_op jit(solution)/shard_map/all_to_all | solution.py:280
  86.6 0.1 copy.16.critic_ref
  86.7 0.0 collective-permute-done.7.got_ref
  86.7 7.1 %local_step.1 = (bf16[4,64,256]{2,1,0:T(8,128)(2,1)}, f32[8,162,128]{2,1,0:T(8,128)S(1)}, bf16[8,162,128]{2,1,0:T(8,128)(2,1)S(1)}) custom-call(s32[1]{0:T(128)} %bitcast.slab_ref, bf16[1,64,256]{2,1,0:T(8,128)(2,1)S(1)} %collective-permute-done.5.far_low, bf16[4,64,256]{2,1,0:T(8,128)(2,1)S(1)} %collective-permute-done.1.low, ...), custom_call_target="tpu_custom_call" | custom-call | flops 6000000000 | bytes 4000000 | tf_op jit(solution)/shard_map/local_step/pallas_call | solution.py:240
  93.8 5.5 %all-to-all-done.2 = bf16[16,162,128]{2,1,0:T(8,128)(2,1)S(1)} async-done(((bf16[16,162,128]{2,1,0:T(8,128)(2,1)}), bf16[16,162,128]{2,1,0:T(8,128)(2,1)S(1)}, u32[]{:S(2)}, u32[]{:S(2)}) %all-to-all-start.2) | async-done | bytes 663584 | tf_op jit(solution)/shard_map/all_to_all | solution.py:280
  99.3 1.9 %collective-permute-start.8 = (bf16[8,162,128]{2,1,0:T(8,128)(2,1)S(1)}, bf16[8,162,128]{2,1,0:T(8,128)(2,1)S(1)}, u32[]{:S(2)}, u32[]{:S(2)}) collective-permute-start(bf16[8,162,128]{2,1,0:T(8,128)(2,1)S(1)} %get-tuple-element.50), channel_id=1, source_target_pairs={{0,1},{1,0},{2,3},{3,2},{4,5},{5,4},{6,7},{7,6},{8,9},{9,8},{10,11... | collective-permute-start | bytes 995336 | tf_op jit(solution)/shard_map/ppermute | solution.py:275
  101.2 1.6 %collective-permute-done.8 = bf16[8,162,128]{2,1,0:T(8,128)(2,1)S(1)} collective-permute-done((bf16[8,162,128]{2,1,0:T(8,128)(2,1)S(1)}, bf16[8,162,128]{2,1,0:T(8,128)(2,1)S(1)}, u32[]{:S(2)}, u32[]{:S(2)}) %collective-permute-start.8) | collective-permute-done | bytes 331808 | tf_op jit(solution)/shard_map/ppermute | solution.py:275
  102.9 0.8 add_convert_fusion
  103.7 4.9 %all-to-all-start.3 = ((bf16[8,162,128]{2,1,0:T(8,128)(2,1)}), bf16[8,162,128]{2,1,0:T(8,128)(2,1)S(1)}, u32[]{:S(2)}, u32[]{:S(2)}) async-start(bf16[8,162,128]{2,1,0:T(8,128)(2,1)} %add_convert_fusion), calls=%async_computation.3 | async-start | bytes 688128 | tf_op jit(solution)/shard_map/all_to_all | solution.py:300
  110.6 0.0 copy-start.2
  110.6 19.3 %all-to-all-done.3 = bf16[8,162,128]{2,1,0:T(8,128)(2,1)S(1)} async-done(((bf16[8,162,128]{2,1,0:T(8,128)(2,1)}), bf16[8,162,128]{2,1,0:T(8,128)(2,1)S(1)}, u32[]{:S(2)}, u32[]{:S(2)}) %all-to-all-start.3) | async-done | bytes 331808 | tf_op jit(solution)/shard_map/all_to_all | solution.py:300
  129.9 0.0 copy-done.2
  129.9 1.0 fusion
  (11 shorter events, 0.2 us)
Async XLA Ops:
  2.7 9.3 %copy-start.3 = (f32[1,20736]{1,0:T(1,128)S(1)}, f32[1,20736]{1,0:T(1,128)}, u32[]{:S(2)}) copy-start(f32[1,20736]{1,0:T(1,128)} %param.9) | copy-start | bytes 248836
  2.7 28.2 %all-to-all-start = ((bf16[16,162,128]{2,1,0:T(8,128)(2,1)}), bf16[16,162,128]{2,1,0:T(8,128)(2,1)S(1)}, u32[]{:S(2)}, u32[]{:S(2)}) async-start(bf16[16,162,128]{2,1,0:T(8,128)(2,1)} %broadcast_in_dim.72), calls=%async_computation | async-start | bytes 1376256 | tf_op jit(solution)/shard_map/all_to_all | solution.py:280
  12.2 18.7 %collective-permute-start = (bf16[162,128]{1,0:T(8,128)(2,1)S(1)}, bf16[162,128]{1,0:T(8,128)(2,1)S(1)}, u32[]{:S(2)}, u32[]{:S(2)}) collective-permute-start(bf16[162,128]{1,0:T(8,128)(2,1)S(1)} %bitcast.50), channel_id=1, source_target_pairs={{0,256},{16,272},{32,288},{48,304},{64,320},{80,336},{96,352},{112... | collective-permute-start | bytes 124424 | tf_op jit(solution)/shard_map/ppermute | solution.py:275
  26.2 0.7 copy-start.4
  27.0 0.7 copy-start.5
  31.8 9.7 %copy-start.1 = (bf16[1,8,128,64]{2,3,1,0:T(8,128)(2,1)S(1)}, bf16[1,8,128,64]{2,3,1,0:T(8,128)(2,1)}, u32[]{:S(2)}) copy-start(bf16[1,8,128,64]{2,3,1,0:T(8,128)(2,1)} %param.10) | copy-start | bytes 393220
  31.8 26.1 %all-to-all-start.1 = ((bf16[4,162,128]{2,1,0:T(8,128)(2,1)}), bf16[4,162,128]{2,1,0:T(8,128)(2,1)S(1)}, u32[]{:S(2)}, u32[]{:S(2)}) async-start(bf16[4,162,128]{2,1,0:T(8,128)(2,1)} %broadcast_select_fusion.1), calls=%async_computation.1 | async-start | bytes 344064 | tf_op jit(solution)/shard_map/all_to_all | solution.py:294
  41.6 0.9 copy-start
  42.5 5.3 %collective-permute-start.2 = (bf16[4,64,256]{2,1,0:T(8,128)(2,1)S(1)}, bf16[4,64,256]{2,1,0:T(8,128)(2,1)S(1)}, u32[]{:S(2)}, u32[]{:S(2)}) collective-permute-start(bf16[4,64,256]{2,1,0:T(8,128)(2,1)S(1)} %bitcast.40), channel_id=1, source_target_pairs={{1,0},{2,1},{3,2},{4,3},{5,4},{6,5},{7,6},{8,7},{9,8},{10,9},{11,1... | collective-permute-start | bytes 393224 | tf_op jit(solution)/shard_map/ppermute | solution.py:309
  43.8 4.1 %collective-permute-start.1 = (bf16[4,64,256]{2,1,0:T(8,128)(2,1)S(1)}, bf16[4,64,256]{2,1,0:T(8,128)(2,1)S(1)}, u32[]{:S(2)}, u32[]{:S(2)}) collective-permute-start(bf16[4,64,256]{2,1,0:T(8,128)(2,1)S(1)} %bitcast.41), channel_id=1, source_target_pairs={{0,1},{1,2},{2,3},{3,4},{4,5},{5,6},{6,7},{7,8},{8,9},{9,10},{10,1... | collective-permute-start | bytes 393224 | tf_op jit(solution)/shard_map/ppermute | solution.py:309
  47.9 10.0 %copy-start.6 = (f32[1,128]{1,0:T(1,128)S(1)}, f32[1,128]{1,0:T(1,128)}, u32[]{:S(2)}) copy-start(f32[1,128]{1,0:T(1,128)} %param.11) | copy-start | bytes 1540
  57.9 7.3 %collective-permute-start.3 = (bf16[2,162,128]{2,1,0:T(8,128)(2,1)S(1)}, bf16[2,162,128]{2,1,0:T(8,128)(2,1)S(1)}, u32[]{:S(2)}, u32[]{:S(2)}) collective-permute-start(bf16[2,162,128]{2,1,0:T(8,128)(2,1)S(1)} %constant_dynamic-slice_fusion), channel_id=1, source_target_pairs={{0,4},{1,5},{2,6},{3,7},{4,0},{5,1},{6,2},{7,3},{8,12},{9,13},{10,... | collective-permute-start | bytes 248840 | tf_op jit(solution)/shard_map/ppermute | solution.py:275
  65.3 10.5 %collective-permute-start.4 = (bf16[4,162,128]{2,1,0:T(8,128)(2,1)S(1)}, bf16[4,162,128]{2,1,0:T(8,128)(2,1)S(1)}, u32[]{:S(2)}, u32[]{:S(2)}) collective-permute-start(bf16[4,162,128]{2,1,0:T(8,128)(2,1)S(1)} %pad_maximum_fusion.1), channel_id=1, source_target_pairs={{0,2},{1,3},{2,0},{3,1},{4,6},{5,7},{6,4},{7,5},{8,10},{9,11},{10,... | collective-permute-start | bytes 497672 | tf_op jit(solution)/shard_map/ppermute | solution.py:275
  70.0 5.9 %collective-permute-start.6 = (bf16[1,64,256]{2,1,0:T(8,128)(2,1)S(1)}, bf16[1,64,256]{2,1,0:T(8,128)(2,1)S(1)}, u32[]{:S(2)}, u32[]{:S(2)}) collective-permute-start(bf16[1,64,256]{2,1,0:T(8,128)(2,1)S(1)} %get-tuple-element.55), channel_id=1, source_target_pairs={{2,0},{3,1},{4,2},{5,3},{6,4},{7,5},{8,6},{9,7},{10,8},{11,9},{12,... | collective-permute-start | bytes 98312 | tf_op jit(solution)/shard_map/ppermute | solution.py:309
  71.3 6.1 %collective-permute-start.5 = (bf16[1,64,256]{2,1,0:T(8,128)(2,1)S(1)}, bf16[1,64,256]{2,1,0:T(8,128)(2,1)S(1)}, u32[]{:S(2)}, u32[]{:S(2)}) collective-permute-start(bf16[1,64,256]{2,1,0:T(8,128)(2,1)S(1)} %get-tuple-element.56), channel_id=1, source_target_pairs={{0,2},{1,3},{2,4},{3,5},{4,6},{5,7},{6,8},{7,9},{8,10},{9,11},{10,... | collective-permute-start | bytes 98312 | tf_op jit(solution)/shard_map/ppermute | solution.py:309
  77.4 9.3 %collective-permute-start.7 = (bf16[8,162,128]{2,1,0:T(8,128)(2,1)S(1)}, bf16[8,162,128]{2,1,0:T(8,128)(2,1)S(1)}, u32[]{:S(2)}, u32[]{:S(2)}) collective-permute-start(bf16[8,162,128]{2,1,0:T(8,128)(2,1)S(1)} %pad_maximum_fusion.held_ref), channel_id=1, source_target_pairs={{0,1},{1,0},{2,3},{3,2},{4,5},{5,4},{6,7},{7,6},{8,9},{9,8},{10,11... | collective-permute-start | bytes 995336 | tf_op jit(solution)/shard_map/ppermute | solution.py:275
  79.3 20.0 %all-to-all-start.2 = ((bf16[16,162,128]{2,1,0:T(8,128)(2,1)}), bf16[16,162,128]{2,1,0:T(8,128)(2,1)S(1)}, u32[]{:S(2)}, u32[]{:S(2)}) async-start(bf16[16,162,128]{2,1,0:T(8,128)(2,1)} %broadcast_select_fusion), calls=%async_computation.2 | async-start | bytes 1376256 | tf_op jit(solution)/shard_map/all_to_all | solution.py:280
  99.3 3.5 %collective-permute-start.8 = (bf16[8,162,128]{2,1,0:T(8,128)(2,1)S(1)}, bf16[8,162,128]{2,1,0:T(8,128)(2,1)S(1)}, u32[]{:S(2)}, u32[]{:S(2)}) collective-permute-start(bf16[8,162,128]{2,1,0:T(8,128)(2,1)S(1)} %get-tuple-element.50), channel_id=1, source_target_pairs={{0,1},{1,0},{2,3},{3,2},{4,5},{5,4},{6,7},{7,6},{8,9},{9,8},{10,11... | collective-permute-start | bytes 995336 | tf_op jit(solution)/shard_map/ppermute | solution.py:275
  103.7 26.2 %all-to-all-start.3 = ((bf16[8,162,128]{2,1,0:T(8,128)(2,1)}), bf16[8,162,128]{2,1,0:T(8,128)(2,1)S(1)}, u32[]{:S(2)}, u32[]{:S(2)}) async-start(bf16[8,162,128]{2,1,0:T(8,128)(2,1)} %add_convert_fusion), calls=%async_computation.3 | async-start | bytes 688128 | tf_op jit(solution)/shard_map/all_to_all | solution.py:300
  110.6 19.3 %copy-start.2 = (f32[1,20736]{1,0:T(1,128)S(1)}, f32[1,20736]{1,0:T(1,128)}, u32[]{:S(2)}) copy-start(f32[1,20736]{1,0:T(1,128)} %param.8) | copy-start | bytes 248836

commit v6 on v4

--- a/solution.py
+++ b/solution.py
@@ -11,6 +11,7 @@
 CH = 64
 ROW = 128
 ROWS = 162
+SECOND = 168
 SLABS = 16
 PLANES = 4
 DEPTH = 64
@@ -280,8 +281,101 @@
     return lax.all_to_all(slots, "trainer", 0, 0, axis_index_groups=groups)
 
 
-def source_of(trainer, pairing, flags):
-    return jnp.where(flags[trainer] == 1, trainer, pairing[trainer])
+def pack_kernel(weight_ref, moment_ref, out_ref, rows):
+    rows[...] = jnp.zeros(rows.shape, jnp.float32)
+    for index, source in enumerate((weight_ref, moment_ref)):
+        for r in range(ROWS):
+            spot = index * SECOND + r
+            rows[spot : spot + 1, :] = source[:, r * ROW : (r + 1) * ROW]
+    packed = rows[...].astype(jnp.bfloat16)
+    for slot in range(16):
+        out_ref[slot] = packed
+
+
+def pack_slots(weight, moment):
+    vmem = pl.BlockSpec(memory_space=pltpu.VMEM)
+    return pl.pallas_call(
+        pack_kernel,
+        out_shape=(
+            jax.ShapeDtypeStruct((16, 2 * SECOND, ROW), jnp.bfloat16),
+            jax.ShapeDtypeStruct((2 * SECOND, ROW), jnp.float32),
+        ),
+        in_specs=[vmem, vmem],
+        out_specs=(vmem, vmem),
+        cost_estimate=pl.CostEstimate(flops=100_000, bytes_accessed=1_500_000, transcendentals=0),
+        name="pack_slots",
+    )(weight, moment)
+
+
+def update_kernel(info, rows, held, moment_own, across, heard, weight_ref, moment_ref, fresh):
+    grad = heard[0].astype(jnp.float32)
+    for member in range(1, heard.shape[0]):
+        grad = grad + heard[member].astype(jnp.float32)
+    keeper = info[2] == 1
+    far = lax.axis_index("depth") >> 3
+    other_weight = held[far].astype(jnp.float32)
+    other_moment = jnp.where(
+        info[1] == 1, moment_own[...].astype(jnp.float32), across[...].astype(jnp.float32)
+    )
+    weight = jnp.where(keeper, rows[0:ROWS, :], other_weight)
+    moment = jnp.where(keeper, rows[SECOND : SECOND + ROWS, :], other_moment)
+    moment = momentum_decay * moment + grad
+    fresh[0] = weight - step_length * moment
+    fresh[1] = moment
+    for index, target in enumerate((weight_ref, moment_ref)):
+        for r in range(ROWS):
+            target[:, r * ROW : (r + 1) * ROW] = fresh[index, r : r + 1, :]
+
+
+def update(info, rows, held, moment_own, across, heard):
+    vmem = pl.BlockSpec(memory_space=pltpu.VMEM)
+    flat = jax.ShapeDtypeStruct((1, ROWS * ROW), jnp.float32)
+    return pl.pallas_call(
+        update_kernel,
+        out_shape=(flat, flat),
+        in_specs=[pl.BlockSpec(memory_space=pltpu.SMEM)] + [vmem] * 5,
+        out_specs=(vmem, vmem),
+        scratch_shapes=[pltpu.VMEM((2, ROWS, ROW), jnp.float32)],
+        cost_estimate=pl.CostEstimate(flops=500_000, bytes_accessed=1_000_000, transcendentals=0),
+        name="update",
+    )(info, rows, held, moment_own, across, heard)
+
+
+def pick_kernel(pairing, flags, heard, slots, moment_own, moment_other, info):
+    rank = lax.axis_index("trainer")
+    half = rank >> 4
+    across = rank ^ 16
+    source = jnp.where(flags[rank] == 1, rank, pairing[rank])
+    other = jnp.where(flags[across] == 1, across, pairing[across])
+    for_own = heard[source & 15, 0:ROWS, :]
+    for_other = heard[other & 15, 0:ROWS, :]
+    for member in range(4):
+        slots[member] = jnp.where(half == member // 2, for_own, for_other)
+    moment_own[...] = heard[source & 15, SECOND : SECOND + ROWS, :]
+    moment_other[...] = heard[other & 15, SECOND : SECOND + ROWS, :]
+    info[0] = 2 * (source >> 4)
+    info[1] = jnp.where((source >> 4) == half, 1, 0)
+    info[2] = flags[rank]
+    info[3] = half
+
+
+def pick_slots(pairing, flags, heard):
+    vmem = pl.BlockSpec(memory_space=pltpu.VMEM)
+    smem = pl.BlockSpec(memory_space=pltpu.SMEM)
+    share = jax.ShapeDtypeStruct((ROWS, ROW), jnp.bfloat16)
+    return pl.pallas_call(
+        pick_kernel,
+        out_shape=(
+            jax.ShapeDtypeStruct((4, ROWS, ROW), jnp.bfloat16),
+            share,
+            share,
+            jax.ShapeDtypeStruct((4,), jnp.int32),
+        ),
+        in_specs=[smem, smem, vmem],
+        out_specs=(vmem, vmem, vmem, smem),
+        cost_estimate=pl.CostEstimate(flops=100_000, bytes_accessed=1_500_000, transcendentals=0),
+        name="pick_slots",
+    )(pairing, flags, heard)
 
 
 def far_exchange(slots):
@@ -294,13 +388,12 @@
     return lax.all_to_all(slots, ("trainer", "depth"), 0, 0, axis_index_groups=groups)
 
 
-def sum_depth(keep, send):
+def exchange_depth(keep, send):
     groups = [list(range(core, 16, 2)) for core in range(2)]
     mine = keep + move(send, "depth", lambda i: i ^ 1).astype(jnp.float32)
-    heard = lax.all_to_all(
+    return lax.all_to_all(
         mine.astype(jnp.bfloat16), "depth", 0, 0, axis_index_groups=groups
     )
-    return jnp.sum(heard.astype(jnp.float32), axis=0)
 
 
 def shifted(value, by):
@@ -318,13 +411,10 @@
 
 def one_step(noise, gen_weight, gen_momentum, disc_weight, score_weight, pairing, flags):
     together = lax.optimization_barrier
-    rank = lax.axis_index("trainer")
     slab = lax.axis_index("depth").astype(jnp.int32)
-    half = rank // 16
-    own_weight = gen_weight.reshape(ROWS, ROW)
-    own_moment = gen_momentum.reshape(ROWS, ROW)
     latent = noise[0]
-    heard = plane_exchange(jnp.broadcast_to(own_weight.astype(jnp.bfloat16)[None], (16, ROWS, ROW)))
+    packed, rows = pack_slots(gen_weight, gen_momentum)
+    heard = plane_exchange(packed)
     pieces = (
         shifted(latent[PLANES - 1 :], 2),
         shifted(latent, 1),
@@ -332,46 +422,28 @@
         shifted(latent, -1),
         shifted(latent[:1], -2),
     )
-    source = source_of(rank, pairing, flags)
-    other_source = source_of(rank ^ 16, pairing, flags)
-    to_own = jnp.arange(4) // 2 == half
-    heard, pieces, source, other_source, to_own = together(
-        (heard, pieces, source, other_source, to_own)
-    )
-    for_own = lax.dynamic_index_in_dim(heard, source % 16, 0)
-    for_other = lax.dynamic_index_in_dim(heard, other_source % 16, 0)
-    got = far_exchange(jnp.where(to_own[:, None, None], for_own, for_other))
     critic, critic_back = critic_forms(disc_weight[0])
     score = jnp.broadcast_to(score_weight[0][:, None], (ROW, ROW))
-    moment_slots = jnp.broadcast_to(own_moment.astype(jnp.bfloat16)[None], (16, ROWS, ROW))
-    got, critic, critic_back, score, moment_slots = together(
-        (got, critic, critic_back, score, moment_slots)
-    )
-    held = lax.dynamic_slice_in_dim(got, 2 * (source // 16), 2, 0)
-    other_weight = lax.dynamic_index_in_dim(held, slab // 8, 0, keepdims=False)
-    heard_moment = plane_exchange(moment_slots)
-    for mask in (4, 2):
-        held = jnp.concatenate([held, move(held, "depth", lambda i: i ^ mask)])
+    heard, pieces, critic, critic_back, score = together(
+        (heard, pieces, critic, critic_back, score)
+    )
+    slots, moment_own, moment_other, info = pick_slots(pairing, flags, heard)
+    got = far_exchange(slots)
+    got, moment_other = together((got, moment_other))
+    held = lax.dynamic_slice_in_dim(got, info[0], 2, 0)
+    both = held
+    across = move(moment_other, "trainer", lambda i: i ^ 16)
+    held = jnp.concatenate([held, move(held, "depth", lambda i: i ^ 4)])
+    held = jnp.concatenate([held, move(held, "depth", lambda i: i ^ 2)])
     near = move(held, "depth", lambda i: i ^ 1)
     generated, keep, send = local_step(
         slab.reshape(1), pieces, held, near, critic, critic_back, score
     )
-    keep, send, heard_moment = together((keep, send, heard_moment))
-    grad_share = sum_depth(keep, send)
-    moment_own = lax.dynamic_index_in_dim(heard_moment, source % 16, 0, keepdims=False)
-    moment_other = lax.dynamic_index_in_dim(heard_moment, other_source % 16, 0, keepdims=False)
-    moment_far = move(moment_other, "trainer", lambda i: i ^ 16)
-    other_moment = jnp.where(source // 16 == half, moment_own, moment_far)
-    keeper = flags[rank] == 1
-    chosen_weight = jnp.where(keeper, own_weight, other_weight.astype(jnp.float32))
-    chosen_momentum = jnp.where(keeper, own_moment, other_moment.astype(jnp.float32))
-    new_momentum = momentum_decay * chosen_momentum + grad_share
-    new_weight = chosen_weight - step_length * new_momentum
-    return (
-        generated[None],
-        new_weight.reshape(gen_weight.shape),
-        new_momentum.reshape(gen_weight.shape),
-    )
+    keep, send, across = together((keep, send, across))
+    new_weight, new_momentum = update(
+        info, rows, both, moment_own, across, exchange_depth(keep, send)
+    )
+    return generated[None], new_weight, new_momentum
 
 
 def solution(mesh):

time: 133 us -> 130 us (0.977)
  the two profiles are of different devices: /device:TPU:65 before, /device:TPU:8 now
where the time goes in v6:
time: 130 us; the launch traced here: 129 us
  starting transfers between devices  49.4 us (38%)
  waiting for transfers between devices  37.3 us (29%)
  blocking collectives  24.9 us (19%)
  Pallas kernels  13.4 us (10%)
  between operations  2.5 us (2%)
  local copies, waits for them, and re-layouts  1.41 us (1%)
    all_to_all x1, blocking collectives, exchange_depth(): lax.all_to_all(mine.astype(jnp.bfloat16), 'depth', 0, 0, axis_index_group...  24.9 us
    all_to_all x1, starting transfers between devices, far_exchange(): lax.all_to_all(slots, ('trainer', 'depth'), 0, 0, axis_index_groups=groups)  15.8 us
    ppermute x5, waiting for transfers between devices, move(): return lax.ppermute(value, axis, [(i, target_of(i)) for i in range(count)])  15.8 us
    ppermute x5, starting transfers between devices, move(): return lax.ppermute(value, axis, [(i, target_of(i)) for i in range(count)])  15.4 us
    all_to_all x1, waiting for transfers between devices, far_exchange(): lax.all_to_all(slots, ('trainer', 'depth'), 0, 0, axis_index_groups=groups)  13.1 us
    all_to_all x1, starting transfers between devices, plane_exchange(): return lax.all_to_all(slots, 'trainer', 0, 0, axis_index_groups=groups)  9.43 us
    ppermute x4, starting transfers between devices, shifted(): return lax.ppermute(value, 'depth', links)  8.78 us
    pallas_call x1, Pallas kernels, local_step(): pl.pallas_call(local_kernel, out_shape=(jax.ShapeDtypeStruct((PLANES, CH,...  7.11 us
  transfers between devices with their start and end apart: 11, of which 8 were waited for; matrix products, arithmetic and copies ran while one was open for 0% of the time, Pallas kernels for 6%

profile of v6, /device:TPU:8, one launch (start us, length us, event | category | flops | bytes accessed | tf_op | source)
XLA Modules:
  0.0 129.0 jit_solution(16729227485533996890)
XLA Ops:
  0.6 2.1 %pack_slots.1 = (bf16[16,336,128]{2,1,0:T(8,128)(2,1)}, f32[336,128]{1,0:T(8,128)}) custom-call(f32[1,20736]{1,0:T(1,128)} %weight_ref.1, f32[1,20736]{1,0:T(1,128)} %moment_ref.1), custom_call_target="tpu_custom_call" | custom-call | flops 100000 | bytes 1500000 | tf_op jit(solution)/shard_map/pack_slots/pallas_call | solution.py:297
  2.8 0.0 copy-start
  2.8 0.0 copy-start.3
  2.8 0.0 copy-start.5
  2.8 9.4 %all-to-all-start = ((bf16[16,336,128]{2,1,0:T(8,128)(2,1)}), bf16[16,336,128]{2,1,0:T(8,128)(2,1)S(1)}, u32[]{:S(2)}, u32[]{:S(2)}) async-start(bf16[16,336,128]{2,1,0:T(8,128)(2,1)} %get-tuple-element.28), calls=%async_computation | async-start | bytes 2752512 | tf_op jit(solution)/shard_map/all_to_all | solution.py:281
  12.2 0.0 copy-done
  12.2 1.3 %collective-permute-start.1 = (bf16[4,64,256]{2,1,0:T(8,128)(2,1)S(1)}, bf16[4,64,256]{2,1,0:T(8,128)(2,1)S(1)}, u32[]{:S(2)}, u32[]{:S(2)}) collective-permute-start(bf16[4,64,256]{2,1,0:T(8,128)(2,1)S(1)} %bitcast.22), channel_id=1, source_target_pairs={{0,1},{1,2},{2,3},{3,4},{4,5},{5,6},{6,7},{7,8},{8,9},{9,10},{10,1... | collective-permute-start | bytes 393224 | tf_op jit(solution)/shard_map/ppermute | solution.py:402
  13.5 1.3 %collective-permute-start.2 = (bf16[4,64,256]{2,1,0:T(8,128)(2,1)S(1)}, bf16[4,64,256]{2,1,0:T(8,128)(2,1)S(1)}, u32[]{:S(2)}, u32[]{:S(2)}) collective-permute-start(bf16[4,64,256]{2,1,0:T(8,128)(2,1)S(1)} %bitcast.23), channel_id=1, source_target_pairs={{1,0},{2,1},{3,2},{4,3},{5,4},{6,5},{7,6},{8,7},{9,8},{10,9},{11,1... | collective-permute-start | bytes 393224 | tf_op jit(solution)/shard_map/ppermute | solution.py:402
  14.8 4.9 %collective-permute-start = (bf16[1,64,256]{2,1,0:T(8,128)(2,1)S(1)}, bf16[1,64,256]{2,1,0:T(8,128)(2,1)S(1)}, u32[]{:S(2)}, u32[]{:S(2)}) collective-permute-start(bf16[1,64,256]{2,1,0:T(8,128)(2,1)S(1)} %get-tuple-element.54), channel_id=1, source_target_pairs={{0,2},{1,3},{2,4},{3,5},{4,6},{5,7},{6,8},{7,9},{8,10},{9,11},{10,... | collective-permute-start | bytes 98312 | tf_op jit(solution)/shard_map/ppermute | solution.py:402
  19.7 1.3 %collective-permute-start.3 = (bf16[1,64,256]{2,1,0:T(8,128)(2,1)S(1)}, bf16[1,64,256]{2,1,0:T(8,128)(2,1)S(1)}, u32[]{:S(2)}, u32[]{:S(2)}) collective-permute-start(bf16[1,64,256]{2,1,0:T(8,128)(2,1)S(1)} %get-tuple-element.53), channel_id=1, source_target_pairs={{2,0},{3,1},{4,2},{5,3},{6,4},{7,5},{8,6},{9,7},{10,8},{11,9},{12,... | collective-permute-start | bytes 98312 | tf_op jit(solution)/shard_map/ppermute | solution.py:402
  21.0 0.0 copy-done.3
  21.1 0.1 copy.15
  21.2 0.1 collective-permute-done.far_low
  21.3 4.2 %collective-permute-done.3.far_high = bf16[1,64,256]{2,1,0:T(8,128)(2,1)S(1)} collective-permute-done((bf16[1,64,256]{2,1,0:T(8,128)(2,1)S(1)}, bf16[1,64,256]{2,1,0:T(8,128)(2,1)S(1)}, u32[]{:S(2)}, u32[]{:S(2)}) %collective-permute-start.3) | collective-permute-done | bytes 32800 | tf_op jit(solution)/shard_map/ppermute | solution.py:402
  25.6 0.0 collective-permute-done.1.low
  25.6 0.0 collective-permute-done.2.high
  25.6 4.2 %all-to-all-done.heard = bf16[16,336,128]{2,1,0:T(8,128)(2,1)S(1)} async-done(((bf16[16,336,128]{2,1,0:T(8,128)(2,1)}), bf16[16,336,128]{2,1,0:T(8,128)(2,1)S(1)}, u32[]{:S(2)}, u32[]{:S(2)}) %all-to-all-start) | async-done | bytes 1376288 | tf_op jit(solution)/shard_map/all_to_all | solution.py:281
  29.7 0.0 copy-start.1
  29.7 0.0 copy-done.5
  29.8 0.1 broadcast_in_dim.11.score_ref
  29.8 1.0 copy-done.1
  30.8 2.1 %pick_slots.1 = (bf16[4,162,128]{2,1,0:T(8,128)(2,1)}, bf16[162,128]{1,0:T(8,128)(2,1)}, bf16[162,128]{1,0:T(8,128)(2,1)}, s32[4]{0:T(128)}) custom-call(s32[32]{0:T(128)} %pairing.1, s32[32]{0:T(128)} %flags.1, bf16[16,336,128]{2,1,0:T(8,128)(2,1)} %copy-done.1), custom_call_target="tpu_custom_call" | custom-call | flops 100000 | bytes 1500000 | tf_op jit(solution)/shard_map/pick_slots/pallas_call | solution.py:366
  32.9 0.0 copy-start.6
  33.0 15.8 %all-to-all-start.1 = ((bf16[4,162,128]{2,1,0:T(8,128)(2,1)}), bf16[4,162,128]{2,1,0:T(8,128)(2,1)S(1)}, u32[]{:S(2)}, u32[]{:S(2)}) async-start(bf16[4,162,128]{2,1,0:T(8,128)(2,1)} %get-tuple-element.35), calls=%async_computation.1 | async-start | bytes 344064 | tf_op jit(solution)/shard_map/all_to_all | solution.py:388
  50.5 13.1 %all-to-all-done.1 = bf16[4,162,128]{2,1,0:T(8,128)(2,1)S(1)} async-done(((bf16[4,162,128]{2,1,0:T(8,128)(2,1)}), bf16[4,162,128]{2,1,0:T(8,128)(2,1)S(1)}, u32[]{:S(2)}, u32[]{:S(2)}) %all-to-all-start.1) | async-done | bytes 165920 | tf_op jit(solution)/shard_map/all_to_all | solution.py:388
  63.5 0.0 copy-start.2
  63.6 4.6 %collective-permute-start.4 = (bf16[2,162,128]{2,1,0:T(8,128)(2,1)S(1)}, bf16[2,162,128]{2,1,0:T(8,128)(2,1)S(1)}, u32[]{:S(2)}, u32[]{:S(2)}) collective-permute-start(bf16[2,162,128]{2,1,0:T(8,128)(2,1)S(1)} %constant_dynamic-slice_fusion.held), channel_id=1, source_target_pairs={{0,4},{1,5},{2,6},{3,7},{4,0},{5,1},{6,2},{7,3},{8,12},{9,13},{10,... | collective-permute-start | bytes 248840 | tf_op jit(solution)/shard_map/ppermute | solution.py:276
  68.1 2.9 %collective-permute-done.4 = bf16[2,162,128]{2,1,0:T(8,128)(2,1)S(1)} collective-permute-done((bf16[2,162,128]{2,1,0:T(8,128)(2,1)S(1)}, bf16[2,162,128]{2,1,0:T(8,128)(2,1)S(1)}, u32[]{:S(2)}, u32[]{:S(2)}) %collective-permute-start.4) | collective-permute-done | bytes 82976 | tf_op jit(solution)/shard_map/ppermute | solution.py:276
  71.1 4.6 %collective-permute-start.5 = (bf16[4,162,128]{2,1,0:T(8,128)(2,1)S(1)}, bf16[4,162,128]{2,1,0:T(8,128)(2,1)S(1)}, u32[]{:S(2)}, u32[]{:S(2)}) collective-permute-start(bf16[4,162,128]{2,1,0:T(8,128)(2,1)S(1)} %pad_maximum_fusion.1), channel_id=1, source_target_pairs={{0,2},{1,3},{2,0},{3,1},{4,6},{5,7},{6,4},{7,5},{8,10},{9,11},{10,... | collective-permute-start | bytes 497672 | tf_op jit(solution)/shard_map/ppermute | solution.py:276
  75.7 3.4 %collective-permute-done.5 = bf16[4,162,128]{2,1,0:T(8,128)(2,1)S(1)} collective-permute-done((bf16[4,162,128]{2,1,0:T(8,128)(2,1)S(1)}, bf16[4,162,128]{2,1,0:T(8,128)(2,1)S(1)}, u32[]{:S(2)}, u32[]{:S(2)}) %collective-permute-start.5) | collective-permute-done | bytes 165920 | tf_op jit(solution)/shard_map/ppermute | solution.py:276
  79.1 1.9 %collective-permute-start.6 = (bf16[8,162,128]{2,1,0:T(8,128)(2,1)S(1)}, bf16[8,162,128]{2,1,0:T(8,128)(2,1)S(1)}, u32[]{:S(2)}, u32[]{:S(2)}) collective-permute-start(bf16[8,162,128]{2,1,0:T(8,128)(2,1)S(1)} %pad_maximum_fusion.held_ref), channel_id=1, source_target_pairs={{0,1},{1,0},{2,3},{3,2},{4,5},{5,4},{6,7},{7,6},{8,9},{9,8},{10,11... | collective-permute-start | bytes 995336 | tf_op jit(solution)/shard_map/ppermute | solution.py:276
  81.0 0.1 copy.16.critic_ref
  81.1 0.0 copy-done.6
  81.2 2.4 %collective-permute-start.7 = (bf16[162,128]{1,0:T(8,128)(2,1)S(1)}, bf16[162,128]{1,0:T(8,128)(2,1)S(1)}, u32[]{:S(2)}, u32[]{:S(2)}) collective-permute-start(bf16[162,128]{1,0:T(8,128)(2,1)S(1)} %copy-done.6), channel_id=1, source_target_pairs={{0,256},{16,272},{32,288},{48,304},{64,320},{80,336},{96,352},{112... | collective-permute-start | bytes 124424 | tf_op jit(solution)/shard_map/ppermute | solution.py:276
  83.5 0.0 collective-permute-done.6.got_ref
  83.5 7.1 %local_step.1 = (bf16[4,64,256]{2,1,0:T(8,128)(2,1)}, f32[8,162,128]{2,1,0:T(8,128)S(1)}, bf16[8,162,128]{2,1,0:T(8,128)(2,1)S(1)}) custom-call(s32[1]{0:T(128)} %bitcast.slab_ref, bf16[1,64,256]{2,1,0:T(8,128)(2,1)S(1)} %collective-permute-done.far_low, bf16[4,64,256]{2,1,0:T(8,128)(2,1)S(1)} %collective-permute-done.1.low, ...), custom_call_target="tpu_custom_call" | custom-call | flops 6000000000 | bytes 4000000 | tf_op jit(solution)/shard_map/local_step/pallas_call | solution.py:241
  90.7 0.0 copy-done.2
  90.7 7.9 %collective-permute-done.7.across = bf16[162,128]{1,0:T(8,128)(2,1)S(1)} collective-permute-done((bf16[162,128]{1,0:T(8,128)(2,1)S(1)}, bf16[162,128]{1,0:T(8,128)(2,1)S(1)}, u32[]{:S(2)}, u32[]{:S(2)}) %collective-permute-start.7) | collective-permute-done | bytes 41504 | tf_op jit(solution)/shard_map/ppermute | solution.py:276
  98.5 0.0 copy-start.4
  98.5 1.9 %collective-permute-start.8 = (bf16[8,162,128]{2,1,0:T(8,128)(2,1)S(1)}, bf16[8,162,128]{2,1,0:T(8,128)(2,1)S(1)}, u32[]{:S(2)}, u32[]{:S(2)}) collective-permute-start(bf16[8,162,128]{2,1,0:T(8,128)(2,1)S(1)} %get-tuple-element.50), channel_id=1, source_target_pairs={{0,1},{1,0},{2,3},{3,2},{4,5},{5,4},{6,7},{7,6},{8,9},{9,8},{10,11... | collective-permute-start | bytes 995336 | tf_op jit(solution)/shard_map/ppermute | solution.py:276
  100.5 1.6 %collective-permute-done.8 = bf16[8,162,128]{2,1,0:T(8,128)(2,1)S(1)} collective-permute-done((bf16[8,162,128]{2,1,0:T(8,128)(2,1)S(1)}, bf16[8,162,128]{2,1,0:T(8,128)(2,1)S(1)}, u32[]{:S(2)}, u32[]{:S(2)}) %collective-permute-start.8) | collective-permute-done | bytes 331808 | tf_op jit(solution)/shard_map/ppermute | solution.py:276
  102.1 0.1 add_convert_fusion
  102.2 24.9 %all_to_all.15.heard = bf16[8,162,128]{2,1,0:T(8,128)(2,1)} all-to-all(bf16[8,162,128]{2,1,0:T(8,128)(2,1)S(1)} %add_convert_fusion), channel_id=1, replica_groups={{0,2,4,6,8,10,12,14},{1,3,5,7,9,11,13,15},{16,18,20,22,24,26,28,30},{17..., dimensions={0} | all-to-all | bytes 663552 | tf_op jit(solution)/shard_map/all_to_all | solution.py:394
  127.0 0.0 copy-done.4
  127.0 2.0 %update.1 = (f32[1,20736]{1,0:T(1,128)}, f32[1,20736]{1,0:T(1,128)}) custom-call(s32[4]{0:T(128)} %get-tuple-element.38.info, f32[336,128]{1,0:T(8,128)} %get-tuple-element.43.rows, bf16[2,162,128]{2,1,0:T(8,128)(2,1)} %copy-done.2, bf16[162,128]{1,0:T(8,128)(2,1)} %get-tuple-element.44.moment_own, bf16[162,128]{1,0:T(8,128)(2,1)} %copy-done.4, ...), custom_call_target="tpu_custom_call" | custom-call | flops 500000 | bytes 1000000 | tf_op jit(solution)/shard_map/update/pallas_call | solution.py:333
  (6 shorter events, 0.1 us)
Async XLA Ops:
  2.8 9.4 %copy-start = (bf16[1,4,64,256]{3,2,1,0:T(8,128)(2,1)S(1)}, bf16[1,4,64,256]{3,2,1,0:T(8,128)(2,1)}, u32[]{:S(2)}) copy-start(bf16[1,4,64,256]{3,2,1,0:T(8,128)(2,1)} %param.7) | copy-start | bytes 393220
  2.8 18.3 %copy-start.3 = (bf16[1,8,128,64]{2,3,1,0:T(8,128)(2,1)S(1)}, bf16[1,8,128,64]{2,3,1,0:T(8,128)(2,1)}, u32[]{:S(2)}) copy-start(bf16[1,8,128,64]{2,3,1,0:T(8,128)(2,1)} %param.10) | copy-start | bytes 393220
  2.8 27.0 %copy-start.5 = (f32[1,128]{1,0:T(1,128)S(1)}, f32[1,128]{1,0:T(1,128)}, u32[]{:S(2)}) copy-start(f32[1,128]{1,0:T(1,128)} %param.11) | copy-start | bytes 1540
  2.8 27.0 %all-to-all-start = ((bf16[16,336,128]{2,1,0:T(8,128)(2,1)}), bf16[16,336,128]{2,1,0:T(8,128)(2,1)S(1)}, u32[]{:S(2)}, u32[]{:S(2)}) async-start(bf16[16,336,128]{2,1,0:T(8,128)(2,1)} %get-tuple-element.28), calls=%async_computation | async-start | bytes 2752512 | tf_op jit(solution)/shard_map/all_to_all | solution.py:281
  12.2 13.3 %collective-permute-start.1 = (bf16[4,64,256]{2,1,0:T(8,128)(2,1)S(1)}, bf16[4,64,256]{2,1,0:T(8,128)(2,1)S(1)}, u32[]{:S(2)}, u32[]{:S(2)}) collective-permute-start(bf16[4,64,256]{2,1,0:T(8,128)(2,1)S(1)} %bitcast.22), channel_id=1, source_target_pairs={{0,1},{1,2},{2,3},{3,4},{4,5},{5,6},{6,7},{7,8},{8,9},{9,10},{10,1... | collective-permute-start | bytes 393224 | tf_op jit(solution)/shard_map/ppermute | solution.py:402
  13.5 12.0 %collective-permute-start.2 = (bf16[4,64,256]{2,1,0:T(8,128)(2,1)S(1)}, bf16[4,64,256]{2,1,0:T(8,128)(2,1)S(1)}, u32[]{:S(2)}, u32[]{:S(2)}) collective-permute-start(bf16[4,64,256]{2,1,0:T(8,128)(2,1)S(1)} %bitcast.23), channel_id=1, source_target_pairs={{1,0},{2,1},{3,2},{4,3},{5,4},{6,5},{7,6},{8,7},{9,8},{10,9},{11,1... | collective-permute-start | bytes 393224 | tf_op jit(solution)/shard_map/ppermute | solution.py:402
  14.8 6.5 %collective-permute-start = (bf16[1,64,256]{2,1,0:T(8,128)(2,1)S(1)}, bf16[1,64,256]{2,1,0:T(8,128)(2,1)S(1)}, u32[]{:S(2)}, u32[]{:S(2)}) collective-permute-start(bf16[1,64,256]{2,1,0:T(8,128)(2,1)S(1)} %get-tuple-element.54), channel_id=1, source_target_pairs={{0,2},{1,3},{2,4},{3,5},{4,6},{5,7},{6,8},{7,9},{8,10},{9,11},{10,... | collective-permute-start | bytes 98312 | tf_op jit(solution)/shard_map/ppermute | solution.py:402
  19.7 5.8 %collective-permute-start.3 = (bf16[1,64,256]{2,1,0:T(8,128)(2,1)S(1)}, bf16[1,64,256]{2,1,0:T(8,128)(2,1)S(1)}, u32[]{:S(2)}, u32[]{:S(2)}) collective-permute-start(bf16[1,64,256]{2,1,0:T(8,128)(2,1)S(1)} %get-tuple-element.53), channel_id=1, source_target_pairs={{2,0},{3,1},{4,2},{5,3},{6,4},{7,5},{8,6},{9,7},{10,8},{11,9},{12,... | collective-permute-start | bytes 98312 | tf_op jit(solution)/shard_map/ppermute | solution.py:402
  29.7 1.1 copy-start.1
  32.9 48.2 %copy-start.6 = (bf16[162,128]{1,0:T(8,128)(2,1)S(1)}, bf16[162,128]{1,0:T(8,128)(2,1)}, u32[]{:S(2)}) copy-start(bf16[162,128]{1,0:T(8,128)(2,1)} %get-tuple-element.47) | copy-start | bytes 124420
  33.0 30.6 %all-to-all-start.1 = ((bf16[4,162,128]{2,1,0:T(8,128)(2,1)}), bf16[4,162,128]{2,1,0:T(8,128)(2,1)S(1)}, u32[]{:S(2)}, u32[]{:S(2)}) async-start(bf16[4,162,128]{2,1,0:T(8,128)(2,1)} %get-tuple-element.35), calls=%async_computation.1 | async-start | bytes 344064 | tf_op jit(solution)/shard_map/all_to_all | solution.py:388
  63.5 27.1 %copy-start.2 = (bf16[2,162,128]{2,1,0:T(8,128)(2,1)}, bf16[2,162,128]{2,1,0:T(8,128)(2,1)S(1)}, u32[]{:S(2)}) copy-start(bf16[2,162,128]{2,1,0:T(8,128)(2,1)S(1)} %constant_dynamic-slice_fusion.held) | copy-start | bytes 248836
  63.6 7.5 %collective-permute-start.4 = (bf16[2,162,128]{2,1,0:T(8,128)(2,1)S(1)}, bf16[2,162,128]{2,1,0:T(8,128)(2,1)S(1)}, u32[]{:S(2)}, u32[]{:S(2)}) collective-permute-start(bf16[2,162,128]{2,1,0:T(8,128)(2,1)S(1)} %constant_dynamic-slice_fusion.held), channel_id=1, source_target_pairs={{0,4},{1,5},{2,6},{3,7},{4,0},{5,1},{6,2},{7,3},{8,12},{9,13},{10,... | collective-permute-start | bytes 248840 | tf_op jit(solution)/shard_map/ppermute | solution.py:276
  71.1 8.0 %collective-permute-start.5 = (bf16[4,162,128]{2,1,0:T(8,128)(2,1)S(1)}, bf16[4,162,128]{2,1,0:T(8,128)(2,1)S(1)}, u32[]{:S(2)}, u32[]{:S(2)}) collective-permute-start(bf16[4,162,128]{2,1,0:T(8,128)(2,1)S(1)} %pad_maximum_fusion.1), channel_id=1, source_target_pairs={{0,2},{1,3},{2,0},{3,1},{4,6},{5,7},{6,4},{7,5},{8,10},{9,11},{10,... | collective-permute-start | bytes 497672 | tf_op jit(solution)/shard_map/ppermute | solution.py:276
  79.1 4.4 %collective-permute-start.6 = (bf16[8,162,128]{2,1,0:T(8,128)(2,1)S(1)}, bf16[8,162,128]{2,1,0:T(8,128)(2,1)S(1)}, u32[]{:S(2)}, u32[]{:S(2)}) collective-permute-start(bf16[8,162,128]{2,1,0:T(8,128)(2,1)S(1)} %pad_maximum_fusion.held_ref), channel_id=1, source_target_pairs={{0,1},{1,0},{2,3},{3,2},{4,5},{5,4},{6,7},{7,6},{8,9},{9,8},{10,11... | collective-permute-start | bytes 995336 | tf_op jit(solution)/shard_map/ppermute | solution.py:276
  81.2 17.4 %collective-permute-start.7 = (bf16[162,128]{1,0:T(8,128)(2,1)S(1)}, bf16[162,128]{1,0:T(8,128)(2,1)S(1)}, u32[]{:S(2)}, u32[]{:S(2)}) collective-permute-start(bf16[162,128]{1,0:T(8,128)(2,1)S(1)} %copy-done.6), channel_id=1, source_target_pairs={{0,256},{16,272},{32,288},{48,304},{64,320},{80,336},{96,352},{112... | collective-permute-start | bytes 124424 | tf_op jit(solution)/shard_map/ppermute | solution.py:276
  98.5 28.5 %copy-start.4 = (bf16[162,128]{1,0:T(8,128)(2,1)}, bf16[162,128]{1,0:T(8,128)(2,1)S(1)}, u32[]{:S(2)}) copy-start(bf16[162,128]{1,0:T(8,128)(2,1)S(1)} %collective-permute-done.7.across) | copy-start | bytes 124420
  98.5 3.5 %collective-permute-start.8 = (bf16[8,162,128]{2,1,0:T(8,128)(2,1)S(1)}, bf16[8,162,128]{2,1,0:T(8,128)(2,1)S(1)}, u32[]{:S(2)}, u32[]{:S(2)}) collective-permute-start(bf16[8,162,128]{2,1,0:T(8,128)(2,1)S(1)} %get-tuple-element.50), channel_id=1, source_target_pairs={{0,1},{1,0},{2,3},{3,2},{4,5},{5,4},{6,7},{7,6},{8,9},{9,8},{10,11... | collective-permute-start | bytes 995336 | tf_op jit(solution)/shard_map/ppermute | solution.py:276

commit v7 on v6

--- a/solution.py
+++ b/solution.py
@@ -263,7 +263,7 @@
             pltpu.VMEM((2 * K_ROWS, ROW), f32),
             pltpu.VMEM((FLAT_ROWS, ROW), f32),
         ],
-        compiler_params=pltpu.CompilerParams(vmem_limit_bytes=48 << 20),
+        compiler_params=pltpu.CompilerParams(vmem_limit_bytes=24 << 20),
         cost_estimate=pl.CostEstimate(
             flops=6_000_000_000, bytes_accessed=4_000_000, transcendentals=1_000_000
         ),
@@ -303,6 +303,7 @@
         in_specs=[vmem, vmem],
         out_specs=(vmem, vmem),
         cost_estimate=pl.CostEstimate(flops=100_000, bytes_accessed=1_500_000, transcendentals=0),
+        compiler_params=pltpu.CompilerParams(vmem_limit_bytes=8 << 20),
         name="pack_slots",
     )(weight, moment)
 
@@ -337,26 +338,33 @@
         out_specs=(vmem, vmem),
         scratch_shapes=[pltpu.VMEM((2, ROWS, ROW), jnp.float32)],
         cost_estimate=pl.CostEstimate(flops=500_000, bytes_accessed=1_000_000, transcendentals=0),
+        compiler_params=pltpu.CompilerParams(vmem_limit_bytes=8 << 20),
         name="update",
     )(info, rows, held, moment_own, across, heard)
 
 
-def pick_kernel(pairing, flags, heard, slots, moment_own, moment_other, info):
+def pick_kernel(
+    pairing, flags, heard, slots, moment_own, moment_other, info, for_own, for_other, sems
+):
     rank = lax.axis_index("trainer")
     half = rank >> 4
     across = rank ^ 16
     source = jnp.where(flags[rank] == 1, rank, pairing[rank])
     other = jnp.where(flags[across] == 1, across, pairing[across])
-    for_own = heard[source & 15, 0:ROWS, :]
-    for_other = heard[other & 15, 0:ROWS, :]
-    for member in range(4):
-        slots[member] = jnp.where(half == member // 2, for_own, for_other)
-    moment_own[...] = heard[source & 15, SECOND : SECOND + ROWS, :]
-    moment_other[...] = heard[other & 15, SECOND : SECOND + ROWS, :]
+    first = pltpu.make_async_copy(heard.at[source & 15], for_own, sems.at[0])
+    second = pltpu.make_async_copy(heard.at[other & 15], for_other, sems.at[1])
+    first.start()
+    second.start()
     info[0] = 2 * (source >> 4)
     info[1] = jnp.where((source >> 4) == half, 1, 0)
     info[2] = flags[rank]
     info[3] = half
+    first.wait()
+    second.wait()
+    for member in range(4):
+        slots[member] = jnp.where(half == member // 2, for_own[0:ROWS, :], for_other[0:ROWS, :])
+    moment_own[...] = for_own[SECOND : SECOND + ROWS, :]
+    moment_other[...] = for_other[SECOND : SECOND + ROWS, :]
 
 
 def pick_slots(pairing, flags, heard):
@@ -371,9 +379,15 @@
             share,
             jax.ShapeDtypeStruct((4,), jnp.int32),
         ),
-        in_specs=[smem, smem, vmem],
+        in_specs=[smem, smem, pl.BlockSpec(memory_space=pl.ANY)],
         out_specs=(vmem, vmem, vmem, smem),
-        cost_estimate=pl.CostEstimate(flops=100_000, bytes_accessed=1_500_000, transcendentals=0),
+        scratch_shapes=[
+            pltpu.VMEM((2 * SECOND, ROW), jnp.bfloat16),
+            pltpu.VMEM((2 * SECOND, ROW), jnp.bfloat16),
+            pltpu.SemaphoreType.DMA((2,)),
+        ],
+        cost_estimate=pl.CostEstimate(flops=100_000, bytes_accessed=400_000, transcendentals=0),
+        compiler_params=pltpu.CompilerParams(vmem_limit_bytes=8 << 20),
         name="pick_slots",
     )(pairing, flags, heard)
 
@@ -429,10 +443,9 @@
     )
     slots, moment_own, moment_other, info = pick_slots(pairing, flags, heard)
     got = far_exchange(slots)
-    got, moment_other = together((got, moment_other))
+    across = move(moment_other, "trainer", lambda i: i ^ 16)
     held = lax.dynamic_slice_in_dim(got, info[0], 2, 0)
     both = held
-    across = move(moment_other, "trainer", lambda i: i ^ 16)
     held = jnp.concatenate([held, move(held, "depth", lambda i: i ^ 4)])
     held = jnp.concatenate([held, move(held, "depth", lambda i: i ^ 2)])
     near = move(held, "depth", lambda i: i ^ 1)

time: 130 us -> 128 us (0.985)
  Pallas kernels: 13.4 us -> 11.2 us
  waiting for transfers between devices: 37.3 us -> 38.9 us
  between operations: 2.5 us -> 0.94 us
    all_to_all x1, waiting for transfers between devices: 13.1 us -> 14.6 us  [far_exchange(): lax.all_to_all(slots, ('trainer', 'depth'), 0, 0, axis_index_groups=groups)]
where the time goes in v7:
time: 128 us
  starting transfers between devices  49.4 us (39%)
  waiting for transfers between devices  38.9 us (30%)
  blocking collectives  24.8 us (19%)
  Pallas kernels  11.2 us (9%)
  local copies, waits for them, and re-layouts  2.16 us (2%)
    all_to_all x1, blocking collectives, exchange_depth(): lax.all_to_all(mine.astype(jnp.bfloat16), 'depth', 0, 0, axis_index_group...  24.8 us
    all_to_all x1, starting transfers between devices, far_exchange(): lax.all_to_all(slots, ('trainer', 'depth'), 0, 0, axis_index_groups=groups)  15.8 us
    ppermute x5, waiting for transfers between devices, move(): return lax.ppermute(value, axis, [(i, target_of(i)) for i in range(count)])  15.8 us
    ppermute x5, starting transfers between devices, move(): return lax.ppermute(value, axis, [(i, target_of(i)) for i in range(count)])  15.4 us
    all_to_all x1, waiting for transfers between devices, far_exchange(): lax.all_to_all(slots, ('trainer', 'depth'), 0, 0, axis_index_groups=groups)  14.6 us
    all_to_all x1, starting transfers between devices, plane_exchange(): return lax.all_to_all(slots, 'trainer', 0, 0, axis_index_groups=groups)  9.43 us
    ppermute x4, starting transfers between devices, shifted(): return lax.ppermute(value, 'depth', links)  8.78 us
    pallas_call x1, Pallas kernels, local_step(): pl.pallas_call(local_kernel, out_shape=(jax.ShapeDtypeStruct((PLANES, CH,...  7.12 us
  transfers between devices with their start and end apart: 11, of which 8 were waited for; matrix products, arithmetic and copies ran while one was open for 0% of the time, Pallas kernels for 6%

profile of v7, /device:TPU:8, one launch (start us, length us, event | category | flops | bytes accessed | tf_op | source)
XLA Modules:
  0.0 127.6 jit_solution(15053981183893091201)
XLA Ops:
  0.6 0.0 copy-start
  0.6 0.9 copy-done
  1.5 0.0 copy-start.1
  1.5 0.9 copy-done.1
  2.4 1.2 pack_slots.1
  3.6 0.0 copy-start.2
  3.6 0.0 copy-start.5
  3.6 0.0 copy-start.6
  3.6 0.0 copy-start.3
  3.6 0.0 copy-start.4
  3.6 9.4 %all-to-all-start = ((bf16[16,336,128]{2,1,0:T(8,128)(2,1)}), bf16[16,336,128]{2,1,0:T(8,128)(2,1)S(1)}, u32[]{:S(2)}, u32[]{:S(2)}) async-start(bf16[16,336,128]{2,1,0:T(8,128)(2,1)} %get-tuple-element.26), calls=%async_computation | async-start | bytes 2752512 | tf_op jit(solution)/shard_map/all_to_all | solution.py:281
  13.1 0.0 copy-done.2
  13.1 1.3 %collective-permute-start.1 = (bf16[4,64,256]{2,1,0:T(8,128)(2,1)S(1)}, bf16[4,64,256]{2,1,0:T(8,128)(2,1)S(1)}, u32[]{:S(2)}, u32[]{:S(2)}) collective-permute-start(bf16[4,64,256]{2,1,0:T(8,128)(2,1)S(1)} %bitcast.22), channel_id=1, source_target_pairs={{0,1},{1,2},{2,3},{3,4},{4,5},{5,6},{6,7},{7,8},{8,9},{9,10},{10,1... | collective-permute-start | bytes 393224 | tf_op jit(solution)/shard_map/ppermute | solution.py:416
  14.4 1.3 %collective-permute-start.2 = (bf16[4,64,256]{2,1,0:T(8,128)(2,1)S(1)}, bf16[4,64,256]{2,1,0:T(8,128)(2,1)S(1)}, u32[]{:S(2)}, u32[]{:S(2)}) collective-permute-start(bf16[4,64,256]{2,1,0:T(8,128)(2,1)S(1)} %bitcast.23), channel_id=1, source_target_pairs={{1,0},{2,1},{3,2},{4,3},{5,4},{6,5},{7,6},{8,7},{9,8},{10,9},{11,1... | collective-permute-start | bytes 393224 | tf_op jit(solution)/shard_map/ppermute | solution.py:416
  15.7 4.9 %collective-permute-start = (bf16[1,64,256]{2,1,0:T(8,128)(2,1)S(1)}, bf16[1,64,256]{2,1,0:T(8,128)(2,1)S(1)}, u32[]{:S(2)}, u32[]{:S(2)}) collective-permute-start(bf16[1,64,256]{2,1,0:T(8,128)(2,1)S(1)} %get-tuple-element.50), channel_id=1, source_target_pairs={{0,2},{1,3},{2,4},{3,5},{4,6},{5,7},{6,8},{7,9},{8,10},{9,11},{10,... | collective-permute-start | bytes 98312 | tf_op jit(solution)/shard_map/ppermute | solution.py:416
  20.6 1.3 %collective-permute-start.3 = (bf16[1,64,256]{2,1,0:T(8,128)(2,1)S(1)}, bf16[1,64,256]{2,1,0:T(8,128)(2,1)S(1)}, u32[]{:S(2)}, u32[]{:S(2)}) collective-permute-start(bf16[1,64,256]{2,1,0:T(8,128)(2,1)S(1)} %get-tuple-element.49), channel_id=1, source_target_pairs={{2,0},{3,1},{4,2},{5,3},{6,4},{7,5},{8,6},{9,7},{10,8},{11,9},{12,... | collective-permute-start | bytes 98312 | tf_op jit(solution)/shard_map/ppermute | solution.py:416
  21.9 0.0 copy-done.5
  21.9 0.1 copy.15
  22.1 0.1 collective-permute-done.far_low
  22.2 4.2 %collective-permute-done.3.far_high = bf16[1,64,256]{2,1,0:T(8,128)(2,1)S(1)} collective-permute-done((bf16[1,64,256]{2,1,0:T(8,128)(2,1)S(1)}, bf16[1,64,256]{2,1,0:T(8,128)(2,1)S(1)}, u32[]{:S(2)}, u32[]{:S(2)}) %collective-permute-start.3) | collective-permute-done | bytes 32800 | tf_op jit(solution)/shard_map/ppermute | solution.py:416
  26.4 0.0 collective-permute-done.1.low
  26.4 0.0 collective-permute-done.2.high
  26.4 4.2 %all-to-all-done.heard = bf16[16,336,128]{2,1,0:T(8,128)(2,1)S(1)} async-done(((bf16[16,336,128]{2,1,0:T(8,128)(2,1)}), bf16[16,336,128]{2,1,0:T(8,128)(2,1)S(1)}, u32[]{:S(2)}, u32[]{:S(2)}) %all-to-all-start) | async-done | bytes 1376288 | tf_op jit(solution)/shard_map/all_to_all | solution.py:281
  30.6 0.0 copy-done.6
  30.6 0.1 broadcast_in_dim.11.score_ref
  30.7 0.0 copy-done.3
  30.7 0.0 copy-done.4
  30.7 1.5 %pick_slots.1 = (bf16[4,162,128]{2,1,0:T(8,128)(2,1)}, bf16[162,128]{1,0:T(8,128)(2,1)S(1)}, bf16[162,128]{1,0:T(8,128)(2,1)S(1)}, s32[4]{0:T(128)S(1)}) custom-call(s32[32]{0:T(128)S(1)} %copy-done.3, s32[32]{0:T(128)S(1)} %copy-done.4, bf16[16,336,128]{2,1,0:T(8,128)(2,1)S(1)} %all-to-all-done.heard), custom_call_target="tpu_custom_call" | custom-call | flops 100000 | bytes 400000 | tf_op jit(solution)/shard_map/pick_slots/pallas_call | solution.py:374
  32.2 15.8 %all-to-all-start.1 = ((bf16[4,162,128]{2,1,0:T(8,128)(2,1)}), bf16[4,162,128]{2,1,0:T(8,128)(2,1)S(1)}, u32[]{:S(2)}, u32[]{:S(2)}) async-start(bf16[4,162,128]{2,1,0:T(8,128)(2,1)} %get-tuple-element.33), calls=%async_computation.1 | async-start | bytes 344064 | tf_op jit(solution)/shard_map/all_to_all | solution.py:402
  48.2 14.6 %all-to-all-done.1 = bf16[4,162,128]{2,1,0:T(8,128)(2,1)S(1)} async-done(((bf16[4,162,128]{2,1,0:T(8,128)(2,1)}), bf16[4,162,128]{2,1,0:T(8,128)(2,1)S(1)}, u32[]{:S(2)}, u32[]{:S(2)}) %all-to-all-start.1) | async-done | bytes 165920 | tf_op jit(solution)/shard_map/all_to_all | solution.py:402
  62.8 4.6 %collective-permute-start.4 = (bf16[2,162,128]{2,1,0:T(8,128)(2,1)S(1)}, bf16[2,162,128]{2,1,0:T(8,128)(2,1)S(1)}, u32[]{:S(2)}, u32[]{:S(2)}) collective-permute-start(bf16[2,162,128]{2,1,0:T(8,128)(2,1)S(1)} %constant_dynamic-slice_fusion.held), channel_id=1, source_target_pairs={{0,4},{1,5},{2,6},{3,7},{4,0},{5,1},{6,2},{7,3},{8,12},{9,13},{10,... | collective-permute-start | bytes 248840 | tf_op jit(solution)/shard_map/ppermute | solution.py:276
  67.4 2.9 %collective-permute-done.4 = bf16[2,162,128]{2,1,0:T(8,128)(2,1)S(1)} collective-permute-done((bf16[2,162,128]{2,1,0:T(8,128)(2,1)S(1)}, bf16[2,162,128]{2,1,0:T(8,128)(2,1)S(1)}, u32[]{:S(2)}, u32[]{:S(2)}) %collective-permute-start.4) | collective-permute-done | bytes 82976 | tf_op jit(solution)/shard_map/ppermute | solution.py:276
  70.3 4.6 %collective-permute-start.5 = (bf16[4,162,128]{2,1,0:T(8,128)(2,1)S(1)}, bf16[4,162,128]{2,1,0:T(8,128)(2,1)S(1)}, u32[]{:S(2)}, u32[]{:S(2)}) collective-permute-start(bf16[4,162,128]{2,1,0:T(8,128)(2,1)S(1)} %pad_maximum_fusion.1), channel_id=1, source_target_pairs={{0,2},{1,3},{2,0},{3,1},{4,6},{5,7},{6,4},{7,5},{8,10},{9,11},{10,... | collective-permute-start | bytes 497672 | tf_op jit(solution)/shard_map/ppermute | solution.py:276
  74.9 3.4 %collective-permute-done.5 = bf16[4,162,128]{2,1,0:T(8,128)(2,1)S(1)} collective-permute-done((bf16[4,162,128]{2,1,0:T(8,128)(2,1)S(1)}, bf16[4,162,128]{2,1,0:T(8,128)(2,1)S(1)}, u32[]{:S(2)}, u32[]{:S(2)}) %collective-permute-start.5) | collective-permute-done | bytes 165920 | tf_op jit(solution)/shard_map/ppermute | solution.py:276
  78.4 1.9 %collective-permute-start.6 = (bf16[8,162,128]{2,1,0:T(8,128)(2,1)S(1)}, bf16[8,162,128]{2,1,0:T(8,128)(2,1)S(1)}, u32[]{:S(2)}, u32[]{:S(2)}) collective-permute-start(bf16[8,162,128]{2,1,0:T(8,128)(2,1)S(1)} %pad_maximum_fusion.held_ref), channel_id=1, source_target_pairs={{0,1},{1,0},{2,3},{3,2},{4,5},{5,4},{6,7},{7,6},{8,9},{9,8},{10,11... | collective-permute-start | bytes 995336 | tf_op jit(solution)/shard_map/ppermute | solution.py:276
  80.3 0.1 copy.16.critic_ref
  80.4 2.4 %collective-permute-start.7 = (bf16[162,128]{1,0:T(8,128)(2,1)S(1)}, bf16[162,128]{1,0:T(8,128)(2,1)S(1)}, u32[]{:S(2)}, u32[]{:S(2)}) collective-permute-start(bf16[162,128]{1,0:T(8,128)(2,1)S(1)} %get-tuple-element.43), channel_id=1, source_target_pairs={{0,256},{16,272},{32,288},{48,304},{64,320},{80,336},{96,352},{112... | collective-permute-start | bytes 124424 | tf_op jit(solution)/shard_map/ppermute | solution.py:276
  82.8 0.0 collective-permute-done.6.got_ref
  82.8 7.1 %local_step.1 = (bf16[4,64,256]{2,1,0:T(8,128)(2,1)}, f32[8,162,128]{2,1,0:T(8,128)S(1)}, bf16[8,162,128]{2,1,0:T(8,128)(2,1)S(1)}) custom-call(s32[1]{0:T(128)} %bitcast.slab_ref, bf16[1,64,256]{2,1,0:T(8,128)(2,1)S(1)} %collective-permute-done.far_low, bf16[4,64,256]{2,1,0:T(8,128)(2,1)S(1)} %collective-permute-done.1.low, ...), custom_call_target="tpu_custom_call" | custom-call | flops 6000000000 | bytes 4000000 | tf_op jit(solution)/shard_map/local_step/pallas_call | solution.py:241
  89.9 7.9 %collective-permute-done.7.across = bf16[162,128]{1,0:T(8,128)(2,1)S(1)} collective-permute-done((bf16[162,128]{1,0:T(8,128)(2,1)S(1)}, bf16[162,128]{1,0:T(8,128)(2,1)S(1)}, u32[]{:S(2)}, u32[]{:S(2)}) %collective-permute-start.7) | collective-permute-done | bytes 41504 | tf_op jit(solution)/shard_map/ppermute | solution.py:276
  97.8 1.9 %collective-permute-start.8 = (bf16[8,162,128]{2,1,0:T(8,128)(2,1)S(1)}, bf16[8,162,128]{2,1,0:T(8,128)(2,1)S(1)}, u32[]{:S(2)}, u32[]{:S(2)}) collective-permute-start(bf16[8,162,128]{2,1,0:T(8,128)(2,1)S(1)} %get-tuple-element.46), channel_id=1, source_target_pairs={{0,1},{1,0},{2,3},{3,2},{4,5},{5,4},{6,7},{7,6},{8,9},{9,8},{10,11... | collective-permute-start | bytes 995336 | tf_op jit(solution)/shard_map/ppermute | solution.py:276
  99.7 1.6 %collective-permute-done.8 = bf16[8,162,128]{2,1,0:T(8,128)(2,1)S(1)} collective-permute-done((bf16[8,162,128]{2,1,0:T(8,128)(2,1)S(1)}, bf16[8,162,128]{2,1,0:T(8,128)(2,1)S(1)}, u32[]{:S(2)}, u32[]{:S(2)}) %collective-permute-start.8) | collective-permute-done | bytes 331808 | tf_op jit(solution)/shard_map/ppermute | solution.py:276
  101.3 0.1 add_convert_fusion
  101.4 24.8 %all_to_all.15.heard = bf16[8,162,128]{2,1,0:T(8,128)(2,1)S(1)} all-to-all(bf16[8,162,128]{2,1,0:T(8,128)(2,1)S(1)} %add_convert_fusion), channel_id=1, replica_groups={{0,2,4,6,8,10,12,14},{1,3,5,7,9,11,13,15},{16,18,20,22,24,26,28,30},{17..., dimensions={0} | all-to-all | bytes 663552 | tf_op jit(solution)/shard_map/all_to_all | solution.py:408
  126.2 1.4 %update.1 = (f32[1,20736]{1,0:T(1,128)}, f32[1,20736]{1,0:T(1,128)}) custom-call(s32[4]{0:T(128)S(1)} %get-tuple-element.34.info, f32[336,128]{1,0:T(8,128)S(1)} %get-tuple-element.39.rows, bf16[2,162,128]{2,1,0:T(8,128)(2,1)S(1)} %constant_dynamic-slice_fusion.held, bf16[162,128]{1,0:T(8,128)(2,1)S(1)} %get-tuple-element.40.moment_own, ...), custom_call_target="tpu_custom_call" | custom-call | flops 500000 | bytes 1000000 | tf_op jit(solution)/shard_map/update/pallas_call | solution.py:334
  (6 shorter events, 0.1 us)
Async XLA Ops:
  0.6 0.9 copy-start
  1.5 0.9 copy-start.1
  3.6 9.5 %copy-start.2 = (bf16[1,4,64,256]{3,2,1,0:T(8,128)(2,1)S(1)}, bf16[1,4,64,256]{3,2,1,0:T(8,128)(2,1)}, u32[]{:S(2)}) copy-start(bf16[1,4,64,256]{3,2,1,0:T(8,128)(2,1)} %param.7) | copy-start | bytes 393220
  3.6 18.3 %copy-start.5 = (bf16[1,8,128,64]{2,3,1,0:T(8,128)(2,1)S(1)}, bf16[1,8,128,64]{2,3,1,0:T(8,128)(2,1)}, u32[]{:S(2)}) copy-start(bf16[1,8,128,64]{2,3,1,0:T(8,128)(2,1)} %param.10) | copy-start | bytes 393220
  3.6 27.0 %copy-start.6 = (f32[1,128]{1,0:T(1,128)S(1)}, f32[1,128]{1,0:T(1,128)}, u32[]{:S(2)}) copy-start(f32[1,128]{1,0:T(1,128)} %param.11) | copy-start | bytes 1540
  3.6 27.1 %copy-start.3 = (s32[32]{0:T(128)S(1)}, s32[32]{0:T(128)}, u32[]{:S(2)}) copy-start(s32[32]{0:T(128)} %pairing.1) | copy-start | bytes 388
  3.6 27.1 %copy-start.4 = (s32[32]{0:T(128)S(1)}, s32[32]{0:T(128)}, u32[]{:S(2)}) copy-start(s32[32]{0:T(128)} %flags.1) | copy-start | bytes 388
  3.6 27.0 %all-to-all-start = ((bf16[16,336,128]{2,1,0:T(8,128)(2,1)}), bf16[16,336,128]{2,1,0:T(8,128)(2,1)S(1)}, u32[]{:S(2)}, u32[]{:S(2)}) async-start(bf16[16,336,128]{2,1,0:T(8,128)(2,1)} %get-tuple-element.26), calls=%async_computation | async-start | bytes 2752512 | tf_op jit(solution)/shard_map/all_to_all | solution.py:281
  13.1 13.3 %collective-permute-start.1 = (bf16[4,64,256]{2,1,0:T(8,128)(2,1)S(1)}, bf16[4,64,256]{2,1,0:T(8,128)(2,1)S(1)}, u32[]{:S(2)}, u32[]{:S(2)}) collective-permute-start(bf16[4,64,256]{2,1,0:T(8,128)(2,1)S(1)} %bitcast.22), channel_id=1, source_target_pairs={{0,1},{1,2},{2,3},{3,4},{4,5},{5,6},{6,7},{7,8},{8,9},{9,10},{10,1... | collective-permute-start | bytes 393224 | tf_op jit(solution)/shard_map/ppermute | solution.py:416
  14.4 12.0 %collective-permute-start.2 = (bf16[4,64,256]{2,1,0:T(8,128)(2,1)S(1)}, bf16[4,64,256]{2,1,0:T(8,128)(2,1)S(1)}, u32[]{:S(2)}, u32[]{:S(2)}) collective-permute-start(bf16[4,64,256]{2,1,0:T(8,128)(2,1)S(1)} %bitcast.23), channel_id=1, source_target_pairs={{1,0},{2,1},{3,2},{4,3},{5,4},{6,5},{7,6},{8,7},{9,8},{10,9},{11,1... | collective-permute-start | bytes 393224 | tf_op jit(solution)/shard_map/ppermute | solution.py:416
  15.7 6.5 %collective-permute-start = (bf16[1,64,256]{2,1,0:T(8,128)(2,1)S(1)}, bf16[1,64,256]{2,1,0:T(8,128)(2,1)S(1)}, u32[]{:S(2)}, u32[]{:S(2)}) collective-permute-start(bf16[1,64,256]{2,1,0:T(8,128)(2,1)S(1)} %get-tuple-element.50), channel_id=1, source_target_pairs={{0,2},{1,3},{2,4},{3,5},{4,6},{5,7},{6,8},{7,9},{8,10},{9,11},{10,... | collective-permute-start | bytes 98312 | tf_op jit(solution)/shard_map/ppermute | solution.py:416
  20.6 5.8 %collective-permute-start.3 = (bf16[1,64,256]{2,1,0:T(8,128)(2,1)S(1)}, bf16[1,64,256]{2,1,0:T(8,128)(2,1)S(1)}, u32[]{:S(2)}, u32[]{:S(2)}) collective-permute-start(bf16[1,64,256]{2,1,0:T(8,128)(2,1)S(1)} %get-tuple-element.49), channel_id=1, source_target_pairs={{2,0},{3,1},{4,2},{5,3},{6,4},{7,5},{8,6},{9,7},{10,8},{11,9},{12,... | collective-permute-start | bytes 98312 | tf_op jit(solution)/shard_map/ppermute | solution.py:416
  32.2 30.6 %all-to-all-start.1 = ((bf16[4,162,128]{2,1,0:T(8,128)(2,1)}), bf16[4,162,128]{2,1,0:T(8,128)(2,1)S(1)}, u32[]{:S(2)}, u32[]{:S(2)}) async-start(bf16[4,162,128]{2,1,0:T(8,128)(2,1)} %get-tuple-element.33), calls=%async_computation.1 | async-start | bytes 344064 | tf_op jit(solution)/shard_map/all_to_all | solution.py:402
  62.8 7.5 %collective-permute-start.4 = (bf16[2,162,128]{2,1,0:T(8,128)(2,1)S(1)}, bf16[2,162,128]{2,1,0:T(8,128)(2,1)S(1)}, u32[]{:S(2)}, u32[]{:S(2)}) collective-permute-start(bf16[2,162,128]{2,1,0:T(8,128)(2,1)S(1)} %constant_dynamic-slice_fusion.held), channel_id=1, source_target_pairs={{0,4},{1,5},{2,6},{3,7},{4,0},{5,1},{6,2},{7,3},{8,12},{9,13},{10,... | collective-permute-start | bytes 248840 | tf_op jit(solution)/shard_map/ppermute | solution.py:276
  70.3 8.0 %collective-permute-start.5 = (bf16[4,162,128]{2,1,0:T(8,128)(2,1)S(1)}, bf16[4,162,128]{2,1,0:T(8,128)(2,1)S(1)}, u32[]{:S(2)}, u32[]{:S(2)}) collective-permute-start(bf16[4,162,128]{2,1,0:T(8,128)(2,1)S(1)} %pad_maximum_fusion.1), channel_id=1, source_target_pairs={{0,2},{1,3},{2,0},{3,1},{4,6},{5,7},{6,4},{7,5},{8,10},{9,11},{10,... | collective-permute-start | bytes 497672 | tf_op jit(solution)/shard_map/ppermute | solution.py:276
  78.4 4.4 %collective-permute-start.6 = (bf16[8,162,128]{2,1,0:T(8,128)(2,1)S(1)}, bf16[8,162,128]{2,1,0:T(8,128)(2,1)S(1)}, u32[]{:S(2)}, u32[]{:S(2)}) collective-permute-start(bf16[8,162,128]{2,1,0:T(8,128)(2,1)S(1)} %pad_maximum_fusion.held_ref), channel_id=1, source_target_pairs={{0,1},{1,0},{2,3},{3,2},{4,5},{5,4},{6,7},{7,6},{8,9},{9,8},{10,11... | collective-permute-start | bytes 995336 | tf_op jit(solution)/shard_map/ppermute | solution.py:276
  80.4 17.4 %collective-permute-start.7 = (bf16[162,128]{1,0:T(8,128)(2,1)S(1)}, bf16[162,128]{1,0:T(8,128)(2,1)S(1)}, u32[]{:S(2)}, u32[]{:S(2)}) collective-permute-start(bf16[162,128]{1,0:T(8,128)(2,1)S(1)} %get-tuple-element.43), channel_id=1, source_target_pairs={{0,256},{16,272},{32,288},{48,304},{64,320},{80,336},{96,352},{112... | collective-permute-start | bytes 124424 | tf_op jit(solution)/shard_map/ppermute | solution.py:276
  97.8 3.5 %collective-permute-start.8 = (bf16[8,162,128]{2,1,0:T(8,128)(2,1)S(1)}, bf16[8,162,128]{2,1,0:T(8,128)(2,1)S(1)}, u32[]{:S(2)}, u32[]{:S(2)}) collective-permute-start(bf16[8,162,128]{2,1,0:T(8,128)(2,1)S(1)} %get-tuple-element.46), channel_id=1, source_target_pairs={{0,1},{1,0},{2,3},{3,2},{4,5},{5,4},{6,7},{7,6},{8,9},{9,8},{10,11... | collective-permute-start | bytes 995336 | tf_op jit(solution)/shard_map/ppermute | solution.py:276

commit v8 on v7

--- a/solution.py
+++ b/solution.py
@@ -11,7 +11,6 @@
 CH = 64
 ROW = 128
 ROWS = 162
-SECOND = 168
 SLABS = 16
 PLANES = 4
 DEPTH = 64
@@ -281,15 +280,14 @@
     return lax.all_to_all(slots, "trainer", 0, 0, axis_index_groups=groups)
 
 
-def pack_kernel(weight_ref, moment_ref, out_ref, rows):
-    rows[...] = jnp.zeros(rows.shape, jnp.float32)
+def pack_kernel(weight_ref, moment_ref, out_ref, own_ref, rows_ref):
     for index, source in enumerate((weight_ref, moment_ref)):
         for r in range(ROWS):
-            spot = index * SECOND + r
-            rows[spot : spot + 1, :] = source[:, r * ROW : (r + 1) * ROW]
-    packed = rows[...].astype(jnp.bfloat16)
+            rows_ref[index, r : r + 1, :] = source[:, r * ROW : (r + 1) * ROW]
+    packed = rows_ref[0].astype(jnp.bfloat16)
     for slot in range(16):
         out_ref[slot] = packed
+    own_ref[...] = rows_ref[1].astype(jnp.bfloat16)
 
 
 def pack_slots(weight, moment):
@@ -297,55 +295,18 @@
     return pl.pallas_call(
         pack_kernel,
         out_shape=(
-            jax.ShapeDtypeStruct((16, 2 * SECOND, ROW), jnp.bfloat16),
-            jax.ShapeDtypeStruct((2 * SECOND, ROW), jnp.float32),
+            jax.ShapeDtypeStruct((16, ROWS, ROW), jnp.bfloat16),
+            jax.ShapeDtypeStruct((ROWS, ROW), jnp.bfloat16),
+            jax.ShapeDtypeStruct((2, ROWS, ROW), jnp.float32),
         ),
         in_specs=[vmem, vmem],
-        out_specs=(vmem, vmem),
-        cost_estimate=pl.CostEstimate(flops=100_000, bytes_accessed=1_500_000, transcendentals=0),
-        compiler_params=pltpu.CompilerParams(vmem_limit_bytes=8 << 20),
+        out_specs=(vmem, vmem, vmem),
+        cost_estimate=pl.CostEstimate(flops=100_000, bytes_accessed=1_000_000, transcendentals=0),
         name="pack_slots",
     )(weight, moment)
 
 
-def update_kernel(info, rows, held, moment_own, across, heard, weight_ref, moment_ref, fresh):
-    grad = heard[0].astype(jnp.float32)
-    for member in range(1, heard.shape[0]):
-        grad = grad + heard[member].astype(jnp.float32)
-    keeper = info[2] == 1
-    far = lax.axis_index("depth") >> 3
-    other_weight = held[far].astype(jnp.float32)
-    other_moment = jnp.where(
-        info[1] == 1, moment_own[...].astype(jnp.float32), across[...].astype(jnp.float32)
-    )
-    weight = jnp.where(keeper, rows[0:ROWS, :], other_weight)
-    moment = jnp.where(keeper, rows[SECOND : SECOND + ROWS, :], other_moment)
-    moment = momentum_decay * moment + grad
-    fresh[0] = weight - step_length * moment
-    fresh[1] = moment
-    for index, target in enumerate((weight_ref, moment_ref)):
-        for r in range(ROWS):
-            target[:, r * ROW : (r + 1) * ROW] = fresh[index, r : r + 1, :]
-
-
-def update(info, rows, held, moment_own, across, heard):
-    vmem = pl.BlockSpec(memory_space=pltpu.VMEM)
-    flat = jax.ShapeDtypeStruct((1, ROWS * ROW), jnp.float32)
-    return pl.pallas_call(
-        update_kernel,
-        out_shape=(flat, flat),
-        in_specs=[pl.BlockSpec(memory_space=pltpu.SMEM)] + [vmem] * 5,
-        out_specs=(vmem, vmem),
-        scratch_shapes=[pltpu.VMEM((2, ROWS, ROW), jnp.float32)],
-        cost_estimate=pl.CostEstimate(flops=500_000, bytes_accessed=1_000_000, transcendentals=0),
-        compiler_params=pltpu.CompilerParams(vmem_limit_bytes=8 << 20),
-        name="update",
-    )(info, rows, held, moment_own, across, heard)
-
-
-def pick_kernel(
-    pairing, flags, heard, slots, moment_own, moment_other, info, for_own, for_other, sems
-):
+def pick_kernel(pairing, flags, heard, slots, info, for_own, for_other, sems):
     rank = lax.axis_index("trainer")
     half = rank >> 4
     across = rank ^ 16
@@ -356,40 +317,99 @@
     first.start()
     second.start()
     info[0] = 2 * (source >> 4)
-    info[1] = jnp.where((source >> 4) == half, 1, 0)
+    info[1] = pairing[rank] & 15
     info[2] = flags[rank]
     info[3] = half
     first.wait()
     second.wait()
     for member in range(4):
-        slots[member] = jnp.where(half == member // 2, for_own[0:ROWS, :], for_other[0:ROWS, :])
-    moment_own[...] = for_own[SECOND : SECOND + ROWS, :]
-    moment_other[...] = for_other[SECOND : SECOND + ROWS, :]
+        slots[member] = jnp.where(half == member // 2, for_own[...], for_other[...])
 
 
 def pick_slots(pairing, flags, heard):
     vmem = pl.BlockSpec(memory_space=pltpu.VMEM)
     smem = pl.BlockSpec(memory_space=pltpu.SMEM)
-    share = jax.ShapeDtypeStruct((ROWS, ROW), jnp.bfloat16)
     return pl.pallas_call(
         pick_kernel,
         out_shape=(
             jax.ShapeDtypeStruct((4, ROWS, ROW), jnp.bfloat16),
-            share,
-            share,
             jax.ShapeDtypeStruct((4,), jnp.int32),
         ),
         in_specs=[smem, smem, pl.BlockSpec(memory_space=pl.ANY)],
-        out_specs=(vmem, vmem, vmem, smem),
+        out_specs=(vmem, smem),
         scratch_shapes=[
-            pltpu.VMEM((2 * SECOND, ROW), jnp.bfloat16),
-            pltpu.VMEM((2 * SECOND, ROW), jnp.bfloat16),
+            pltpu.VMEM((ROWS, ROW), jnp.bfloat16),
+            pltpu.VMEM((ROWS, ROW), jnp.bfloat16),
             pltpu.SemaphoreType.DMA((2,)),
         ],
-        cost_estimate=pl.CostEstimate(flops=100_000, bytes_accessed=400_000, transcendentals=0),
+        cost_estimate=pl.CostEstimate(flops=100_000, bytes_accessed=300_000, transcendentals=0),
         compiler_params=pltpu.CompilerParams(vmem_limit_bytes=8 << 20),
         name="pick_slots",
     )(pairing, flags, heard)
+
+
+def moment_kernel(pairing, own, across, out_ref):
+    half = lax.axis_index("trainer") >> 4
+    for slot in range(16):
+        here = (pairing[half * 16 + slot] >> 4) == half
+        out_ref[slot] = jnp.where(here, own[...], across[...])
+
+
+def moment_slots(pairing, own, across):
+    vmem = pl.BlockSpec(memory_space=pltpu.VMEM)
+    return pl.pallas_call(
+        moment_kernel,
+        out_shape=jax.ShapeDtypeStruct((16, ROWS, ROW), jnp.bfloat16),
+        in_specs=[pl.BlockSpec(memory_space=pltpu.SMEM), vmem, vmem],
+        out_specs=vmem,
+        cost_estimate=pl.CostEstimate(flops=100_000, bytes_accessed=800_000, transcendentals=0),
+        compiler_params=pltpu.CompilerParams(vmem_limit_bytes=8 << 20),
+        name="moment_slots",
+    )(pairing, own, across)
+
+
+def update_kernel(info, rows, held, moments, heard, weight_ref, moment_ref, other, fresh, sem):
+    fetch = pltpu.make_async_copy(moments.at[info[1]], other, sem)
+    fetch.start()
+    grad = heard[0].astype(jnp.float32)
+    for member in range(1, heard.shape[0]):
+        grad = grad + heard[member].astype(jnp.float32)
+    keeper = info[2] == 1
+    far = lax.axis_index("depth") >> 3
+    weight = jnp.where(keeper, rows[0], held[far].astype(jnp.float32))
+    fetch.wait()
+    moment = jnp.where(keeper, rows[1], other[...].astype(jnp.float32))
+    moment = momentum_decay * moment + grad
+    fresh[0] = weight - step_length * moment
+    fresh[1] = moment
+    for index, target in enumerate((weight_ref, moment_ref)):
+        for r in range(ROWS):
+            target[:, r * ROW : (r + 1) * ROW] = fresh[index, r : r + 1, :]
+
+
+def update(info, rows, held, moments, heard):
+    vmem = pl.BlockSpec(memory_space=pltpu.VMEM)
+    flat = jax.ShapeDtypeStruct((1, ROWS * ROW), jnp.float32)
+    return pl.pallas_call(
+        update_kernel,
+        out_shape=(flat, flat),
+        in_specs=[
+            pl.BlockSpec(memory_space=pltpu.SMEM),
+            vmem,
+            vmem,
+            pl.BlockSpec(memory_space=pl.ANY),
+            vmem,
+        ],
+        out_specs=(vmem, vmem),
+        scratch_shapes=[
+            pltpu.VMEM((ROWS, ROW), jnp.bfloat16),
+            pltpu.VMEM((2, ROWS, ROW), jnp.float32),
+            pltpu.SemaphoreType.DMA,
+        ],
+        cost_estimate=pl.CostEstimate(flops=500_000, bytes_accessed=1_000_000, transcendentals=0),
+        compiler_params=pltpu.CompilerParams(vmem_limit_bytes=8 << 20),
+        name="update",
+    )(info, rows, held, moments, heard)
 
 
 def far_exchange(slots):
@@ -427,35 +447,34 @@
     together = lax.optimization_barrier
     slab = lax.axis_index("depth").astype(jnp.int32)
     latent = noise[0]
-    packed, rows = pack_slots(gen_weight, gen_momentum)
+    packed, own_moment, rows = pack_slots(gen_weight, gen_momentum)
     heard = plane_exchange(packed)
-    pieces = (
-        shifted(latent[PLANES - 1 :], 2),
-        shifted(latent, 1),
-        latent,
-        shifted(latent, -1),
-        shifted(latent[:1], -2),
-    )
+    low, high = shifted(latent, 1), shifted(latent, -1)
     critic, critic_back = critic_forms(disc_weight[0])
     score = jnp.broadcast_to(score_weight[0][:, None], (ROW, ROW))
-    heard, pieces, critic, critic_back, score = together(
-        (heard, pieces, critic, critic_back, score)
-    )
-    slots, moment_own, moment_other, info = pick_slots(pairing, flags, heard)
+    heard, low, high, critic, critic_back, score = together(
+        (heard, low, high, critic, critic_back, score)
+    )
+    slots, info = pick_slots(pairing, flags, heard)
     got = far_exchange(slots)
-    across = move(moment_other, "trainer", lambda i: i ^ 16)
+    across = move(own_moment, "trainer", lambda i: i ^ 16)
     held = lax.dynamic_slice_in_dim(got, info[0], 2, 0)
     both = held
     held = jnp.concatenate([held, move(held, "depth", lambda i: i ^ 4)])
+    far_low = shifted(latent[PLANES - 1 :], 2)
+    far_high = shifted(latent[:1], -2)
+    moments = moment_slots(pairing, own_moment, across)
+    held, far_low, far_high, moments = together((held, far_low, far_high, moments))
     held = jnp.concatenate([held, move(held, "depth", lambda i: i ^ 2)])
+    moments = plane_exchange(moments)
     near = move(held, "depth", lambda i: i ^ 1)
+    pieces = (far_low, low, latent, high, far_high)
     generated, keep, send = local_step(
         slab.reshape(1), pieces, held, near, critic, critic_back, score
     )
-    keep, send, across = together((keep, send, across))
-    new_weight, new_momentum = update(
-        info, rows, both, moment_own, across, exchange_depth(keep, send)
-    )
+    keep, send, moments = together((keep, send, moments))
+    sums = exchange_depth(keep, send)
+    new_weight, new_momentum = update(info, rows, both, moments, sums)
     return generated[None], new_weight, new_momentum
 
 

time: 128 us -> 131 us (1.023)
  the two profiles are of different devices: /device:TPU:8 before, /device:TPU:1 now
where the time goes in v8:
time: 131 us; the launch traced here: 130 us
  starting transfers between devices  76.1 us (58%)
  blocking collectives  25.8 us (20%)
  Pallas kernels  13.3 us (10%)
  waiting for transfers between devices  13 us (10%)
    ppermute x5, starting transfers between devices, move(): return lax.ppermute(value, axis, [(i, target_of(i)) for i in range(count)])  34.9 us
    all_to_all x1, blocking collectives, exchange_depth(): lax.all_to_all(mine.astype(jnp.bfloat16), 'depth', 0, 0, axis_index_group...  25.8 us
    all_to_all x1, starting transfers between devices, far_exchange(): lax.all_to_all(slots, ('trainer', 'depth'), 0, 0, axis_index_groups=groups)  16.1 us
    all_to_all x2, starting transfers between devices, plane_exchange(): return lax.all_to_all(slots, 'trainer', 0, 0, axis_index_groups=groups)  13.1 us
    ppermute x4, starting transfers between devices, shifted(): return lax.ppermute(value, 'depth', links)  12 us
    pallas_call x1, Pallas kernels, local_step(): pl.pallas_call(local_kernel, out_shape=(jax.ShapeDtypeStruct((PLANES, CH,...  7.11 us
    all_to_all x2, waiting for transfers between devices, plane_exchange(): return lax.all_to_all(slots, 'trainer', 0, 0, axis_index_groups=groups)  6.5 us
    ppermute x5, waiting for transfers between devices, move(): return lax.ppermute(value, axis, [(i, target_of(i)) for i in range(count)])  4.66 us
  transfers between devices with their start and end apart: 12, of which 7 were waited for; matrix products, arithmetic and copies ran while one was open for 0% of the time, Pallas kernels for 7%

profile of v8, /device:TPU:1, one launch (start us, length us, event | category | flops | bytes accessed | tf_op | source)
XLA Modules:
  0.0 130.3 jit_solution(11780912523626617606)
XLA Ops:
  0.6 1.9 %pack_slots.1 = (bf16[16,162,128]{2,1,0:T(8,128)(2,1)}, bf16[162,128]{1,0:T(8,128)(2,1)}, f32[2,162,128]{2,1,0:T(8,128)}) custom-call(f32[1,20736]{1,0:T(1,128)} %weight_ref.1, f32[1,20736]{1,0:T(1,128)} %moment_ref.1), custom_call_target="tpu_custom_call" | custom-call | flops 100000 | bytes 1000000 | tf_op jit(solution)/shard_map/pack_slots/pallas_call | solution.py:295
  2.5 0.0 copy-start.2
  2.5 0.0 copy-start.5
  2.5 7.7 %all-to-all-start = ((bf16[16,162,128]{2,1,0:T(8,128)(2,1)}), bf16[16,162,128]{2,1,0:T(8,128)(2,1)S(1)}, u32[]{:S(2)}, u32[]{:S(2)}) async-start(bf16[16,162,128]{2,1,0:T(8,128)(2,1)} %get-tuple-element.26), calls=%async_computation | async-start | bytes 1376256 | tf_op jit(solution)/shard_map/all_to_all | solution.py:280
  10.2 0.0 copy-done.2
  10.2 4.8 %collective-permute-start.1 = (bf16[4,64,256]{2,1,0:T(8,128)(2,1)S(1)}, bf16[4,64,256]{2,1,0:T(8,128)(2,1)S(1)}, u32[]{:S(2)}, u32[]{:S(2)}) collective-permute-start(bf16[4,64,256]{2,1,0:T(8,128)(2,1)S(1)} %bitcast.22), channel_id=1, source_target_pairs={{1,0},{2,1},{3,2},{4,3},{5,4},{6,5},{7,6},{8,7},{9,8},{10,9},{11,1... | collective-permute-start | bytes 393224 | tf_op jit(solution)/shard_map/ppermute | solution.py:436
  15.0 1.9 %collective-permute-start = (bf16[4,64,256]{2,1,0:T(8,128)(2,1)S(1)}, bf16[4,64,256]{2,1,0:T(8,128)(2,1)S(1)}, u32[]{:S(2)}, u32[]{:S(2)}) collective-permute-start(bf16[4,64,256]{2,1,0:T(8,128)(2,1)S(1)} %bitcast.23), channel_id=1, source_target_pairs={{0,1},{1,2},{2,3},{3,4},{4,5},{5,6},{6,7},{7,8},{8,9},{9,10},{10,1... | collective-permute-start | bytes 393224 | tf_op jit(solution)/shard_map/ppermute | solution.py:436
  16.9 0.0 copy-done.5
  16.9 0.1 copy.15
  17.1 0.0 copy-start.6
  17.1 0.4 collective-permute-done.1.high
  17.6 1.3 %collective-permute-done.low = bf16[4,64,256]{2,1,0:T(8,128)(2,1)S(1)} collective-permute-done((bf16[4,64,256]{2,1,0:T(8,128)(2,1)S(1)}, bf16[4,64,256]{2,1,0:T(8,128)(2,1)S(1)}, u32[]{:S(2)}, u32[]{:S(2)}) %collective-permute-start) | collective-permute-done | bytes 131104 | tf_op jit(solution)/shard_map/ppermute | solution.py:436
  18.9 1.9 %all-to-all-done.heard = bf16[16,162,128]{2,1,0:T(8,128)(2,1)S(1)} async-done(((bf16[16,162,128]{2,1,0:T(8,128)(2,1)}), bf16[16,162,128]{2,1,0:T(8,128)(2,1)S(1)}, u32[]{:S(2)}, u32[]{:S(2)}) %all-to-all-start) | async-done | bytes 663584 | tf_op jit(solution)/shard_map/all_to_all | solution.py:280
  20.8 0.0 copy-done.6
  20.8 0.1 broadcast_in_dim.11.score_ref
  20.9 0.0 copy-start.3
  20.9 0.0 copy-start.4
  20.9 0.6 copy-done.3
  21.5 0.0 copy-done.4
  21.5 1.4 %pick_slots.1 = (bf16[4,162,128]{2,1,0:T(8,128)(2,1)}, s32[4]{0:T(128)S(1)}) custom-call(s32[32]{0:T(128)S(1)} %copy-done.3, s32[32]{0:T(128)S(1)} %copy-done.4, bf16[16,162,128]{2,1,0:T(8,128)(2,1)S(1)} %all-to-all-done.heard), custom_call_target="tpu_custom_call" | custom-call | flops 100000 | bytes 300000 | tf_op jit(solution)/shard_map/pick_slots/pallas_call | solution.py:332
  22.9 0.0 copy-start.1
  23.0 16.1 %all-to-all-start.1 = ((bf16[4,162,128]{2,1,0:T(8,128)(2,1)}), bf16[4,162,128]{2,1,0:T(8,128)(2,1)S(1)}, u32[]{:S(2)}, u32[]{:S(2)}) async-start(bf16[4,162,128]{2,1,0:T(8,128)(2,1)} %get-tuple-element.28), calls=%async_computation.1 | async-start | bytes 344064 | tf_op jit(solution)/shard_map/all_to_all | solution.py:422
  39.1 0.0 copy-done.1
  39.1 12.1 %collective-permute-start.5 = (bf16[162,128]{1,0:T(8,128)(2,1)S(1)}, bf16[162,128]{1,0:T(8,128)(2,1)S(1)}, u32[]{:S(2)}, u32[]{:S(2)}) collective-permute-start(bf16[162,128]{1,0:T(8,128)(2,1)S(1)} %copy-done.1), channel_id=1, source_target_pairs={{0,256},{16,272},{32,288},{48,304},{64,320},{80,336},{96,352},{112... | collective-permute-start | bytes 124424 | tf_op jit(solution)/shard_map/ppermute | solution.py:275
  51.3 0.1 all-to-all-done.1
  51.4 4.5 %collective-permute-start.2 = (bf16[2,162,128]{2,1,0:T(8,128)(2,1)S(1)}, bf16[2,162,128]{2,1,0:T(8,128)(2,1)S(1)}, u32[]{:S(2)}, u32[]{:S(2)}) collective-permute-start(bf16[2,162,128]{2,1,0:T(8,128)(2,1)S(1)} %constant_dynamic-slice_fusion.held), channel_id=1, source_target_pairs={{0,4},{1,5},{2,6},{3,7},{4,0},{5,1},{6,2},{7,3},{8,12},{9,13},{10,... | collective-permute-start | bytes 248840 | tf_op jit(solution)/shard_map/ppermute | solution.py:275
  55.9 1.3 collective-permute-start.4
  57.2 4.0 %collective-permute-start.3 = (bf16[1,64,256]{2,1,0:T(8,128)(2,1)S(1)}, bf16[1,64,256]{2,1,0:T(8,128)(2,1)S(1)}, u32[]{:S(2)}, u32[]{:S(2)}) collective-permute-start(bf16[1,64,256]{2,1,0:T(8,128)(2,1)S(1)} %get-tuple-element.50), channel_id=1, source_target_pairs={{0,2},{1,3},{2,4},{3,5},{4,6},{5,7},{6,8},{7,9},{8,10},{9,11},{10,... | collective-permute-start | bytes 98312 | tf_op jit(solution)/shard_map/ppermute | solution.py:436
  61.2 0.0 collective-permute-done.5.across
  61.2 1.5 %moment_slots.1 = bf16[16,162,128]{2,1,0:T(8,128)(2,1)} custom-call(s32[32]{0:T(128)S(1)} %copy-done.3, bf16[162,128]{1,0:T(8,128)(2,1)S(1)} %copy-done.1, bf16[162,128]{1,0:T(8,128)(2,1)S(1)} %collective-permute-done.5.across), custom_call_target="tpu_custom_call" | custom-call | flops 100000 | bytes 800000 | tf_op jit(solution)/shard_map/moment_slots/pallas_call | solution.py:360
  62.7 0.0 collective-permute-done.2
  62.7 0.0 collective-permute-done.4.far_high
  62.7 0.0 collective-permute-done.3.far_low
  62.8 3.1 %collective-permute-start.6 = (bf16[4,162,128]{2,1,0:T(8,128)(2,1)S(1)}, bf16[4,162,128]{2,1,0:T(8,128)(2,1)S(1)}, u32[]{:S(2)}, u32[]{:S(2)}) collective-permute-start(bf16[4,162,128]{2,1,0:T(8,128)(2,1)S(1)} %pad_maximum_fusion), channel_id=1, source_target_pairs={{0,2},{1,3},{2,0},{3,1},{4,6},{5,7},{6,4},{7,5},{8,10},{9,11},{10,... | collective-permute-start | bytes 497672 | tf_op jit(solution)/shard_map/ppermute | solution.py:275
  65.9 3.4 %collective-permute-done.6 = bf16[4,162,128]{2,1,0:T(8,128)(2,1)S(1)} collective-permute-done((bf16[4,162,128]{2,1,0:T(8,128)(2,1)S(1)}, bf16[4,162,128]{2,1,0:T(8,128)(2,1)S(1)}, u32[]{:S(2)}, u32[]{:S(2)}) %collective-permute-start.6) | collective-permute-done | bytes 165920 | tf_op jit(solution)/shard_map/ppermute | solution.py:275
  69.3 10.8 %collective-permute-start.7 = (bf16[8,162,128]{2,1,0:T(8,128)(2,1)S(1)}, bf16[8,162,128]{2,1,0:T(8,128)(2,1)S(1)}, u32[]{:S(2)}, u32[]{:S(2)}) collective-permute-start(bf16[8,162,128]{2,1,0:T(8,128)(2,1)S(1)} %constant_dynamic-update-slice_fusion.held_ref), channel_id=1, source_target_pairs={{0,1},{1,0},{2,3},{3,2},{4,5},{5,4},{6,7},{7,6},{8,9},{9,8},{10,11... | collective-permute-start | bytes 995336 | tf_op jit(solution)/shard_map/ppermute | solution.py:275
  80.1 5.4 %all-to-all-start.2 = ((bf16[16,162,128]{2,1,0:T(8,128)(2,1)}), bf16[16,162,128]{2,1,0:T(8,128)(2,1)S(1)}, u32[]{:S(2)}, u32[]{:S(2)}) async-start(bf16[16,162,128]{2,1,0:T(8,128)(2,1)} %moment_slots.1), calls=%async_computation.2 | async-start | bytes 1376256 | tf_op jit(solution)/shard_map/all_to_all | solution.py:280
  85.5 0.1 copy.16.critic_ref
  85.6 0.0 collective-permute-done.7.got_ref
  85.6 7.1 %local_step.1 = (bf16[4,64,256]{2,1,0:T(8,128)(2,1)}, f32[8,162,128]{2,1,0:T(8,128)S(1)}, bf16[8,162,128]{2,1,0:T(8,128)(2,1)S(1)}) custom-call(s32[1]{0:T(128)} %bitcast.slab_ref, bf16[1,64,256]{2,1,0:T(8,128)(2,1)S(1)} %collective-permute-done.3.far_low, bf16[4,64,256]{2,1,0:T(8,128)(2,1)S(1)} %collective-permute-done.low, ...), custom_call_target="tpu_custom_call" | custom-call | flops 6000000000 | bytes 4000000 | tf_op jit(solution)/shard_map/local_step/pallas_call | solution.py:240
  92.7 4.6 %all-to-all-done.2.moments = bf16[16,162,128]{2,1,0:T(8,128)(2,1)S(1)} async-done(((bf16[16,162,128]{2,1,0:T(8,128)(2,1)}), bf16[16,162,128]{2,1,0:T(8,128)(2,1)S(1)}, u32[]{:S(2)}, u32[]{:S(2)}) %all-to-all-start.2) | async-done | bytes 663584 | tf_op jit(solution)/shard_map/all_to_all | solution.py:280
  97.3 4.5 %collective-permute-start.8 = (bf16[8,162,128]{2,1,0:T(8,128)(2,1)S(1)}, bf16[8,162,128]{2,1,0:T(8,128)(2,1)S(1)}, u32[]{:S(2)}, u32[]{:S(2)}) collective-permute-start(bf16[8,162,128]{2,1,0:T(8,128)(2,1)S(1)} %get-tuple-element.46), channel_id=1, source_target_pairs={{0,1},{1,0},{2,3},{3,2},{4,5},{5,4},{6,7},{7,6},{8,9},{9,8},{10,11... | collective-permute-start | bytes 995336 | tf_op jit(solution)/shard_map/ppermute | solution.py:275
  101.8 1.3 collective-permute-done.8
  103.0 0.1 add_convert_fusion
  103.1 0.0 copy-start
  103.1 25.8 %all_to_all.20.heard = bf16[8,162,128]{2,1,0:T(8,128)(2,1)S(1)} all-to-all(bf16[8,162,128]{2,1,0:T(8,128)(2,1)S(1)} %add_convert_fusion), channel_id=1, replica_groups={{0,2,4,6,8,10,12,14},{1,3,5,7,9,11,13,15},{16,18,20,22,24,26,28,30},{17..., dimensions={0} | all-to-all | bytes 663552 | tf_op jit(solution)/shard_map/all_to_all | solution.py:428
  128.9 0.0 copy-done
  128.9 1.5 %update.1 = (f32[1,20736]{1,0:T(1,128)}, f32[1,20736]{1,0:T(1,128)}) custom-call(s32[4]{0:T(128)S(1)} %get-tuple-element.29.info, f32[2,162,128]{2,1,0:T(8,128)S(1)} %copy-done, bf16[2,162,128]{2,1,0:T(8,128)(2,1)S(1)} %constant_dynamic-slice_fusion.held, bf16[16,162,128]{2,1,0:T(8,128)(2,1)S(1)} %all-to-all-done.2.moments, ...), custom_call_target="tpu_custom_call" | custom-call | flops 500000 | bytes 1000000 | tf_op jit(solution)/shard_map/update/pallas_call | solution.py:393
  (7 shorter events, 0.1 us)
Async XLA Ops:
  2.5 7.7 %copy-start.2 = (bf16[1,4,64,256]{3,2,1,0:T(8,128)(2,1)S(1)}, bf16[1,4,64,256]{3,2,1,0:T(8,128)(2,1)}, u32[]{:S(2)}) copy-start(bf16[1,4,64,256]{3,2,1,0:T(8,128)(2,1)} %param.7) | copy-start | bytes 393220
  2.5 14.4 %copy-start.5 = (bf16[1,8,128,64]{2,3,1,0:T(8,128)(2,1)S(1)}, bf16[1,8,128,64]{2,3,1,0:T(8,128)(2,1)}, u32[]{:S(2)}) copy-start(bf16[1,8,128,64]{2,3,1,0:T(8,128)(2,1)} %param.10) | copy-start | bytes 393220
  2.5 18.3 %all-to-all-start = ((bf16[16,162,128]{2,1,0:T(8,128)(2,1)}), bf16[16,162,128]{2,1,0:T(8,128)(2,1)S(1)}, u32[]{:S(2)}, u32[]{:S(2)}) async-start(bf16[16,162,128]{2,1,0:T(8,128)(2,1)} %get-tuple-element.26), calls=%async_computation | async-start | bytes 1376256 | tf_op jit(solution)/shard_map/all_to_all | solution.py:280
  10.2 7.3 %collective-permute-start.1 = (bf16[4,64,256]{2,1,0:T(8,128)(2,1)S(1)}, bf16[4,64,256]{2,1,0:T(8,128)(2,1)S(1)}, u32[]{:S(2)}, u32[]{:S(2)}) collective-permute-start(bf16[4,64,256]{2,1,0:T(8,128)(2,1)S(1)} %bitcast.22), channel_id=1, source_target_pairs={{1,0},{2,1},{3,2},{4,3},{5,4},{6,5},{7,6},{8,7},{9,8},{10,9},{11,1... | collective-permute-start | bytes 393224 | tf_op jit(solution)/shard_map/ppermute | solution.py:436
  15.0 3.9 %collective-permute-start = (bf16[4,64,256]{2,1,0:T(8,128)(2,1)S(1)}, bf16[4,64,256]{2,1,0:T(8,128)(2,1)S(1)}, u32[]{:S(2)}, u32[]{:S(2)}) collective-permute-start(bf16[4,64,256]{2,1,0:T(8,128)(2,1)S(1)} %bitcast.23), channel_id=1, source_target_pairs={{0,1},{1,2},{2,3},{3,4},{4,5},{5,6},{6,7},{7,8},{8,9},{9,10},{10,1... | collective-permute-start | bytes 393224 | tf_op jit(solution)/shard_map/ppermute | solution.py:436
  17.1 3.6 %copy-start.6 = (f32[1,128]{1,0:T(1,128)S(1)}, f32[1,128]{1,0:T(1,128)}, u32[]{:S(2)}) copy-start(f32[1,128]{1,0:T(1,128)} %param.11) | copy-start | bytes 1540
  20.9 0.7 copy-start.3
  20.9 0.7 copy-start.4
  22.9 16.1 %copy-start.1 = (bf16[162,128]{1,0:T(8,128)(2,1)S(1)}, bf16[162,128]{1,0:T(8,128)(2,1)}, u32[]{:S(2)}) copy-start(bf16[162,128]{1,0:T(8,128)(2,1)} %get-tuple-element.30.own) | copy-start | bytes 124420
  23.0 28.4 %all-to-all-start.1 = ((bf16[4,162,128]{2,1,0:T(8,128)(2,1)}), bf16[4,162,128]{2,1,0:T(8,128)(2,1)S(1)}, u32[]{:S(2)}, u32[]{:S(2)}) async-start(bf16[4,162,128]{2,1,0:T(8,128)(2,1)} %get-tuple-element.28), calls=%async_computation.1 | async-start | bytes 344064 | tf_op jit(solution)/shard_map/all_to_all | solution.py:422
  39.1 22.1 %collective-permute-start.5 = (bf16[162,128]{1,0:T(8,128)(2,1)S(1)}, bf16[162,128]{1,0:T(8,128)(2,1)S(1)}, u32[]{:S(2)}, u32[]{:S(2)}) collective-permute-start(bf16[162,128]{1,0:T(8,128)(2,1)S(1)} %copy-done.1), channel_id=1, source_target_pairs={{0,256},{16,272},{32,288},{48,304},{64,320},{80,336},{96,352},{112... | collective-permute-start | bytes 124424 | tf_op jit(solution)/shard_map/ppermute | solution.py:275
  51.4 11.3 %collective-permute-start.2 = (bf16[2,162,128]{2,1,0:T(8,128)(2,1)S(1)}, bf16[2,162,128]{2,1,0:T(8,128)(2,1)S(1)}, u32[]{:S(2)}, u32[]{:S(2)}) collective-permute-start(bf16[2,162,128]{2,1,0:T(8,128)(2,1)S(1)} %constant_dynamic-slice_fusion.held), channel_id=1, source_target_pairs={{0,4},{1,5},{2,6},{3,7},{4,0},{5,1},{6,2},{7,3},{8,12},{9,13},{10,... | collective-permute-start | bytes 248840 | tf_op jit(solution)/shard_map/ppermute | solution.py:275
  55.9 6.8 %collective-permute-start.4 = (bf16[1,64,256]{2,1,0:T(8,128)(2,1)S(1)}, bf16[1,64,256]{2,1,0:T(8,128)(2,1)S(1)}, u32[]{:S(2)}, u32[]{:S(2)}) collective-permute-start(bf16[1,64,256]{2,1,0:T(8,128)(2,1)S(1)} %get-tuple-element.49), channel_id=1, source_target_pairs={{2,0},{3,1},{4,2},{5,3},{6,4},{7,5},{8,6},{9,7},{10,8},{11,9},{12,... | collective-permute-start | bytes 98312 | tf_op jit(solution)/shard_map/ppermute | solution.py:436
  57.2 5.6 %collective-permute-start.3 = (bf16[1,64,256]{2,1,0:T(8,128)(2,1)S(1)}, bf16[1,64,256]{2,1,0:T(8,128)(2,1)S(1)}, u32[]{:S(2)}, u32[]{:S(2)}) collective-permute-start(bf16[1,64,256]{2,1,0:T(8,128)(2,1)S(1)} %get-tuple-element.50), channel_id=1, source_target_pairs={{0,2},{1,3},{2,4},{3,5},{4,6},{5,7},{6,8},{7,9},{8,10},{9,11},{10,... | collective-permute-start | bytes 98312 | tf_op jit(solution)/shard_map/ppermute | solution.py:436
  62.8 6.5 %collective-permute-start.6 = (bf16[4,162,128]{2,1,0:T(8,128)(2,1)S(1)}, bf16[4,162,128]{2,1,0:T(8,128)(2,1)S(1)}, u32[]{:S(2)}, u32[]{:S(2)}) collective-permute-start(bf16[4,162,128]{2,1,0:T(8,128)(2,1)S(1)} %pad_maximum_fusion), channel_id=1, source_target_pairs={{0,2},{1,3},{2,0},{3,1},{4,6},{5,7},{6,4},{7,5},{8,10},{9,11},{10,... | collective-permute-start | bytes 497672 | tf_op jit(solution)/shard_map/ppermute | solution.py:275
  69.3 16.3 %collective-permute-start.7 = (bf16[8,162,128]{2,1,0:T(8,128)(2,1)S(1)}, bf16[8,162,128]{2,1,0:T(8,128)(2,1)S(1)}, u32[]{:S(2)}, u32[]{:S(2)}) collective-permute-start(bf16[8,162,128]{2,1,0:T(8,128)(2,1)S(1)} %constant_dynamic-update-slice_fusion.held_ref), channel_id=1, source_target_pairs={{0,1},{1,0},{2,3},{3,2},{4,5},{5,4},{6,7},{7,6},{8,9},{9,8},{10,11... | collective-permute-start | bytes 995336 | tf_op jit(solution)/shard_map/ppermute | solution.py:275
  80.1 17.2 %all-to-all-start.2 = ((bf16[16,162,128]{2,1,0:T(8,128)(2,1)}), bf16[16,162,128]{2,1,0:T(8,128)(2,1)S(1)}, u32[]{:S(2)}, u32[]{:S(2)}) async-start(bf16[16,162,128]{2,1,0:T(8,128)(2,1)} %moment_slots.1), calls=%async_computation.2 | async-start | bytes 1376256 | tf_op jit(solution)/shard_map/all_to_all | solution.py:280
  97.3 5.7 %collective-permute-start.8 = (bf16[8,162,128]{2,1,0:T(8,128)(2,1)S(1)}, bf16[8,162,128]{2,1,0:T(8,128)(2,1)S(1)}, u32[]{:S(2)}, u32[]{:S(2)}) collective-permute-start(bf16[8,162,128]{2,1,0:T(8,128)(2,1)S(1)} %get-tuple-element.46), channel_id=1, source_target_pairs={{0,1},{1,0},{2,3},{3,2},{4,5},{5,4},{6,7},{7,6},{8,9},{9,8},{10,11... | collective-permute-start | bytes 995336 | tf_op jit(solution)/shard_map/ppermute | solution.py:275
  103.1 25.8 %copy-start = (f32[2,162,128]{2,1,0:T(8,128)S(1)}, f32[2,162,128]{2,1,0:T(8,128)}, u32[]{:S(2)}) copy-start(f32[2,162,128]{2,1,0:T(8,128)} %get-tuple-element.40.rows) | copy-start | bytes 497668

commit v9 on v7

--- a/solution.py
+++ b/solution.py
@@ -38,7 +38,6 @@
     high,
     far_high,
     held_ref,
-    got_ref,
     critic_ref,
     critic_back_ref,
     score_ref,
@@ -89,14 +88,8 @@
         store_window(win0, index, value)
 
     for block in range(SLABS):
-        apart = block ^ slab
-        slot = ((apart >> 1) & 1) * 4 + ((apart >> 2) & 1) * 2 + block // 8
-        piece = jnp.where(
-            (apart & 1) == 1,
-            got_ref[slot].astype(jnp.float32),
-            held_ref[slot].astype(jnp.float32),
-        )
-        raw[block * ROWS : (block + 1) * ROWS, :] = piece
+        slot = ((block >> 2) ^ (slab >> 2)) % 2 * 2 + block // 8
+        raw[block * ROWS : (block + 1) * ROWS, :] = held_ref[block % 4, slot].astype(jnp.float32)
 
     for layer in range(3):
         rows = raw[layer * K_ROWS : (layer + 1) * K_ROWS, :]
@@ -235,7 +228,7 @@
             keep_ref[block // 2] = piece
 
 
-def local_step(slab, pieces, held, got, critic, critic_back, score):
+def local_step(slab, pieces, held, critic, critic_back, score):
     bf16, f32 = jnp.bfloat16, jnp.float32
     vmem = pl.BlockSpec(memory_space=pltpu.VMEM)
     return pl.pallas_call(
@@ -245,7 +238,7 @@
             jax.ShapeDtypeStruct((SLABS // 2, ROWS, ROW), f32),
             jax.ShapeDtypeStruct((SLABS // 2, ROWS, ROW), bf16),
         ),
-        in_specs=[pl.BlockSpec(memory_space=pltpu.SMEM)] + [vmem] * 10,
+        in_specs=[pl.BlockSpec(memory_space=pltpu.SMEM)] + [vmem] * 9,
         out_specs=(vmem, vmem, vmem),
         scratch_shapes=[
             pltpu.VMEM((FLAT_ROWS, ROW), f32),
@@ -268,7 +261,7 @@
             flops=6_000_000_000, bytes_accessed=4_000_000, transcendentals=1_000_000
         ),
         name="local_step",
-    )(slab, *pieces, held, got, critic, critic_back, score)
+    )(slab, *pieces, held, critic, critic_back, score)
 
 
 def move(value, axis, target_of):
@@ -303,7 +296,6 @@
         in_specs=[vmem, vmem],
         out_specs=(vmem, vmem),
         cost_estimate=pl.CostEstimate(flops=100_000, bytes_accessed=1_500_000, transcendentals=0),
-        compiler_params=pltpu.CompilerParams(vmem_limit_bytes=8 << 20),
         name="pack_slots",
     )(weight, moment)
 
@@ -447,10 +439,10 @@
     held = lax.dynamic_slice_in_dim(got, info[0], 2, 0)
     both = held
     held = jnp.concatenate([held, move(held, "depth", lambda i: i ^ 4)])
-    held = jnp.concatenate([held, move(held, "depth", lambda i: i ^ 2)])
-    near = move(held, "depth", lambda i: i ^ 1)
+    near = [list(range(first, first + 4)) for first in range(0, 16, 4)]
+    held = lax.all_gather(held, "depth", axis_index_groups=near)
     generated, keep, send = local_step(
-        slab.reshape(1), pieces, held, near, critic, critic_back, score
+        slab.reshape(1), pieces, held, critic, critic_back, score
     )
     keep, send, across = together((keep, send, across))
     new_weight, new_momentum = update(

time: 128 us -> 120 us (0.938)
  the two profiles are of different devices: /device:TPU:8 before, /device:TPU:1 now
where the time goes in v9:
time: 120 us
  starting transfers between devices  44.4 us (37%)
  blocking collectives  42.3 us (35%)
  waiting for transfers between devices  19.7 us (16%)
  Pallas kernels  12 us (10%)
    all_to_all x1, blocking collectives, exchange_depth(): lax.all_to_all(mine.astype(jnp.bfloat16), 'depth', 0, 0, axis_index_group...  25.5 us
    all_gather x1, blocking collectives, one_step(): held = lax.all_gather(held, 'depth', axis_index_groups=near)  16.8 us
    all_to_all x1, starting transfers between devices, far_exchange(): lax.all_to_all(slots, ('trainer', 'depth'), 0, 0, axis_index_groups=groups)  16.2 us
    all_to_all x1, waiting for transfers between devices, far_exchange(): lax.all_to_all(slots, ('trainer', 'depth'), 0, 0, axis_index_groups=groups)  12.2 us
    ppermute x4, starting transfers between devices, shifted(): return lax.ppermute(value, 'depth', links)  11.1 us
    ppermute x3, starting transfers between devices, move(): return lax.ppermute(value, axis, [(i, target_of(i)) for i in range(count)])  9.3 us
    all_to_all x1, starting transfers between devices, plane_exchange(): return lax.all_to_all(slots, 'trainer', 0, 0, axis_index_groups=groups)  7.72 us
    pallas_call x1, Pallas kernels, local_step(): pl.pallas_call(local_kernel, out_shape=(jax.ShapeDtypeStruct((PLANES, CH,...  7 us
  transfers between devices with their start and end apart: 9, of which 4 were waited for; matrix products, arithmetic and copies ran while one was open for 0% of the time, Pallas kernels for 6%

profile of v9, /device:TPU:1, one launch (start us, length us, event | category | flops | bytes accessed | tf_op | source)
XLA Modules:
  0.0 119.8 jit_solution(156015096266632588)
XLA Ops:
  0.6 2.1 %pack_slots.1 = (bf16[16,336,128]{2,1,0:T(8,128)(2,1)}, f32[336,128]{1,0:T(8,128)}) custom-call(f32[1,20736]{1,0:T(1,128)} %weight_ref.1, f32[1,20736]{1,0:T(1,128)} %moment_ref.1), custom_call_target="tpu_custom_call" | custom-call | flops 100000 | bytes 1500000 | tf_op jit(solution)/shard_map/pack_slots/pallas_call | solution.py:290
  2.8 0.0 copy-start.1
  2.8 0.0 copy-start.4
  2.8 0.0 copy-start.5
  2.8 0.0 copy-start.2
  2.8 0.0 copy-start.3
  2.8 7.7 %all-to-all-start = ((bf16[16,336,128]{2,1,0:T(8,128)(2,1)}), bf16[16,336,128]{2,1,0:T(8,128)(2,1)S(1)}, u32[]{:S(2)}, u32[]{:S(2)}) async-start(bf16[16,336,128]{2,1,0:T(8,128)(2,1)} %get-tuple-element.26), calls=%async_computation | async-start | bytes 2752512 | tf_op jit(solution)/shard_map/all_to_all | solution.py:274
  10.5 0.0 copy-done.1
  10.5 4.4 %collective-permute-start.1 = (bf16[4,64,256]{2,1,0:T(8,128)(2,1)S(1)}, bf16[4,64,256]{2,1,0:T(8,128)(2,1)S(1)}, u32[]{:S(2)}, u32[]{:S(2)}) collective-permute-start(bf16[4,64,256]{2,1,0:T(8,128)(2,1)S(1)} %bitcast.24), channel_id=1, source_target_pairs={{0,1},{1,2},{2,3},{3,4},{4,5},{5,6},{6,7},{7,8},{8,9},{9,10},{10,1... | collective-permute-start | bytes 393224 | tf_op jit(solution)/shard_map/ppermute | solution.py:408
  14.9 1.9 %collective-permute-start.2 = (bf16[4,64,256]{2,1,0:T(8,128)(2,1)S(1)}, bf16[4,64,256]{2,1,0:T(8,128)(2,1)S(1)}, u32[]{:S(2)}, u32[]{:S(2)}) collective-permute-start(bf16[4,64,256]{2,1,0:T(8,128)(2,1)S(1)} %bitcast.25), channel_id=1, source_target_pairs={{1,0},{2,1},{3,2},{4,3},{5,4},{6,5},{7,6},{8,7},{9,8},{10,9},{11,1... | collective-permute-start | bytes 393224 | tf_op jit(solution)/shard_map/ppermute | solution.py:408
  16.9 3.5 %collective-permute-start = (bf16[1,64,256]{2,1,0:T(8,128)(2,1)S(1)}, bf16[1,64,256]{2,1,0:T(8,128)(2,1)S(1)}, u32[]{:S(2)}, u32[]{:S(2)}) collective-permute-start(bf16[1,64,256]{2,1,0:T(8,128)(2,1)S(1)} %get-tuple-element.50), channel_id=1, source_target_pairs={{0,2},{1,3},{2,4},{3,5},{4,6},{5,7},{6,8},{7,9},{8,10},{9,11},{10,... | collective-permute-start | bytes 98312 | tf_op jit(solution)/shard_map/ppermute | solution.py:408
  20.4 1.3 %collective-permute-start.3 = (bf16[1,64,256]{2,1,0:T(8,128)(2,1)S(1)}, bf16[1,64,256]{2,1,0:T(8,128)(2,1)S(1)}, u32[]{:S(2)}, u32[]{:S(2)}) collective-permute-start(bf16[1,64,256]{2,1,0:T(8,128)(2,1)S(1)} %get-tuple-element.49), channel_id=1, source_target_pairs={{2,0},{3,1},{4,2},{5,3},{6,4},{7,5},{8,6},{9,7},{10,8},{11,9},{12,... | collective-permute-start | bytes 98312 | tf_op jit(solution)/shard_map/ppermute | solution.py:408
  21.7 0.0 copy-done.4
  21.7 0.1 copy.18
  21.9 0.0 collective-permute-done.far_low
  21.9 3.6 %collective-permute-done.3.far_high = bf16[1,64,256]{2,1,0:T(8,128)(2,1)S(1)} collective-permute-done((bf16[1,64,256]{2,1,0:T(8,128)(2,1)S(1)}, bf16[1,64,256]{2,1,0:T(8,128)(2,1)S(1)}, u32[]{:S(2)}, u32[]{:S(2)}) %collective-permute-start.3) | collective-permute-done | bytes 32800 | tf_op jit(solution)/shard_map/ppermute | solution.py:408
  25.6 0.0 collective-permute-done.1.low
  25.6 0.0 collective-permute-done.2.high
  25.6 2.4 %all-to-all-done.heard = bf16[16,336,128]{2,1,0:T(8,128)(2,1)S(1)} async-done(((bf16[16,336,128]{2,1,0:T(8,128)(2,1)}), bf16[16,336,128]{2,1,0:T(8,128)(2,1)S(1)}, u32[]{:S(2)}, u32[]{:S(2)}) %all-to-all-start) | async-done | bytes 1376288 | tf_op jit(solution)/shard_map/all_to_all | solution.py:274
  28.0 0.0 copy-done.5
  28.0 0.1 broadcast_in_dim.11.score_ref
  28.1 0.0 copy-done.2
  28.1 0.0 copy-done.3
  28.1 1.5 %pick_slots.1 = (bf16[4,162,128]{2,1,0:T(8,128)(2,1)}, bf16[162,128]{1,0:T(8,128)(2,1)S(1)}, bf16[162,128]{1,0:T(8,128)(2,1)S(1)}, s32[4]{0:T(128)S(1)}) custom-call(s32[32]{0:T(128)S(1)} %copy-done.2, s32[32]{0:T(128)S(1)} %copy-done.3, bf16[16,336,128]{2,1,0:T(8,128)(2,1)S(1)} %all-to-all-done.heard), custom_call_target="tpu_custom_call" | custom-call | flops 100000 | bytes 400000 | tf_op jit(solution)/shard_map/pick_slots/pallas_call | solution.py:366
  29.6 16.2 %all-to-all-start.1 = ((bf16[4,162,128]{2,1,0:T(8,128)(2,1)}), bf16[4,162,128]{2,1,0:T(8,128)(2,1)S(1)}, u32[]{:S(2)}, u32[]{:S(2)}) async-start(bf16[4,162,128]{2,1,0:T(8,128)(2,1)} %get-tuple-element.33), calls=%async_computation.1 | async-start | bytes 344064 | tf_op jit(solution)/shard_map/all_to_all | solution.py:394
  45.9 12.2 %all-to-all-done.1 = bf16[4,162,128]{2,1,0:T(8,128)(2,1)S(1)} async-done(((bf16[4,162,128]{2,1,0:T(8,128)(2,1)}), bf16[4,162,128]{2,1,0:T(8,128)(2,1)S(1)}, u32[]{:S(2)}, u32[]{:S(2)}) %all-to-all-start.1) | async-done | bytes 165920 | tf_op jit(solution)/shard_map/all_to_all | solution.py:394
  58.1 4.9 %collective-permute-start.4 = (bf16[2,162,128]{2,1,0:T(8,128)(2,1)S(1)}, bf16[2,162,128]{2,1,0:T(8,128)(2,1)S(1)}, u32[]{:S(2)}, u32[]{:S(2)}) collective-permute-start(bf16[2,162,128]{2,1,0:T(8,128)(2,1)S(1)} %constant_dynamic-slice_fusion.held), channel_id=1, source_target_pairs={{0,4},{1,5},{2,6},{3,7},{4,0},{5,1},{6,2},{7,3},{8,12},{9,13},{10,... | collective-permute-start | bytes 248840 | tf_op jit(solution)/shard_map/ppermute | solution.py:269
  63.1 0.1 copy.19.critic_ref
  63.2 2.2 %collective-permute-start.5 = (bf16[162,128]{1,0:T(8,128)(2,1)S(1)}, bf16[162,128]{1,0:T(8,128)(2,1)S(1)}, u32[]{:S(2)}, u32[]{:S(2)}) collective-permute-start(bf16[162,128]{1,0:T(8,128)(2,1)S(1)} %get-tuple-element.43), channel_id=1, source_target_pairs={{0,256},{16,272},{32,288},{48,304},{64,320},{80,336},{96,352},{112... | collective-permute-start | bytes 124424 | tf_op jit(solution)/shard_map/ppermute | solution.py:269
  65.4 0.0 collective-permute-done.4
  65.4 16.8 %all-gather = bf16[16,162,128]{2,1,0:T(8,128)(2,1)S(1)} all-gather(bf16[4,162,128]{2,1,0:T(8,128)(2,1)S(1)} %pad_maximum_fusion), channel_id=2, replica_groups={{0,1,2,3},{4,5,6,7},{8,9,10,11},{12,13,14,15},{16,17,18,19},{20,21,22,2..., dimensions={0}, use_global_device_ids=true | all-gather | bytes 829440 | tf_op jit(solution)/shard_map/all_gather | solution.py:443
  82.2 7.0 %local_step.1 = (bf16[4,64,256]{2,1,0:T(8,128)(2,1)}, f32[8,162,128]{2,1,0:T(8,128)S(1)}, bf16[8,162,128]{2,1,0:T(8,128)(2,1)S(1)}) custom-call(s32[1]{0:T(128)} %bitcast.slab_ref, bf16[1,64,256]{2,1,0:T(8,128)(2,1)S(1)} %collective-permute-done.far_low, bf16[4,64,256]{2,1,0:T(8,128)(2,1)S(1)} %collective-permute-done.1.low, ...), custom_call_target="tpu_custom_call" | custom-call | flops 6000000000 | bytes 4000000 | tf_op jit(solution)/shard_map/local_step/pallas_call | solution.py:234
  89.2 0.0 copy-start
  89.2 0.0 collective-permute-done.5.across
  89.2 2.2 %collective-permute-start.6 = (bf16[8,162,128]{2,1,0:T(8,128)(2,1)S(1)}, bf16[8,162,128]{2,1,0:T(8,128)(2,1)S(1)}, u32[]{:S(2)}, u32[]{:S(2)}) collective-permute-start(bf16[8,162,128]{2,1,0:T(8,128)(2,1)S(1)} %get-tuple-element.46), channel_id=1, source_target_pairs={{0,1},{1,0},{2,3},{3,2},{4,5},{5,4},{6,7},{7,6},{8,9},{9,8},{10,11... | collective-permute-start | bytes 995336 | tf_op jit(solution)/shard_map/ppermute | solution.py:269
  91.4 1.5 %collective-permute-done.6 = bf16[8,162,128]{2,1,0:T(8,128)(2,1)S(1)} collective-permute-done((bf16[8,162,128]{2,1,0:T(8,128)(2,1)S(1)}, bf16[8,162,128]{2,1,0:T(8,128)(2,1)S(1)}, u32[]{:S(2)}, u32[]{:S(2)}) %collective-permute-start.6) | collective-permute-done | bytes 331808 | tf_op jit(solution)/shard_map/ppermute | solution.py:269
  92.9 0.1 add_convert_fusion
  92.9 25.5 %all_to_all.15.heard = bf16[8,162,128]{2,1,0:T(8,128)(2,1)S(1)} all-to-all(bf16[8,162,128]{2,1,0:T(8,128)(2,1)S(1)} %add_convert_fusion), channel_id=1, replica_groups={{0,2,4,6,8,10,12,14},{1,3,5,7,9,11,13,15},{16,18,20,22,24,26,28,30},{17..., dimensions={0} | all-to-all | bytes 663552 | tf_op jit(solution)/shard_map/all_to_all | solution.py:400
  118.4 0.0 copy-done
  118.4 1.4 %update.1 = (f32[1,20736]{1,0:T(1,128)}, f32[1,20736]{1,0:T(1,128)}) custom-call(s32[4]{0:T(128)S(1)} %get-tuple-element.34.info, f32[336,128]{1,0:T(8,128)S(1)} %copy-done, bf16[2,162,128]{2,1,0:T(8,128)(2,1)S(1)} %constant_dynamic-slice_fusion.held, bf16[162,128]{1,0:T(8,128)(2,1)S(1)} %get-tuple-element.40.moment_own, ...), custom_call_target="tpu_custom_call" | custom-call | flops 500000 | bytes 1000000 | tf_op jit(solution)/shard_map/update/pallas_call | solution.py:326
  (5 shorter events, 0.1 us)
Async XLA Ops:
  2.8 7.8 %copy-start.1 = (bf16[1,4,64,256]{3,2,1,0:T(8,128)(2,1)S(1)}, bf16[1,4,64,256]{3,2,1,0:T(8,128)(2,1)}, u32[]{:S(2)}) copy-start(bf16[1,4,64,256]{3,2,1,0:T(8,128)(2,1)} %param.7) | copy-start | bytes 393220
  2.8 19.0 %copy-start.4 = (bf16[1,8,128,64]{2,3,1,0:T(8,128)(2,1)S(1)}, bf16[1,8,128,64]{2,3,1,0:T(8,128)(2,1)}, u32[]{:S(2)}) copy-start(bf16[1,8,128,64]{2,3,1,0:T(8,128)(2,1)} %param.10) | copy-start | bytes 393220
  2.8 25.2 %copy-start.5 = (f32[1,128]{1,0:T(1,128)S(1)}, f32[1,128]{1,0:T(1,128)}, u32[]{:S(2)}) copy-start(f32[1,128]{1,0:T(1,128)} %param.11) | copy-start | bytes 1540
  2.8 25.3 %copy-start.2 = (s32[32]{0:T(128)S(1)}, s32[32]{0:T(128)}, u32[]{:S(2)}) copy-start(s32[32]{0:T(128)} %pairing.1) | copy-start | bytes 388
  2.8 25.3 %copy-start.3 = (s32[32]{0:T(128)S(1)}, s32[32]{0:T(128)}, u32[]{:S(2)}) copy-start(s32[32]{0:T(128)} %flags.1) | copy-start | bytes 388
  2.8 25.2 %all-to-all-start = ((bf16[16,336,128]{2,1,0:T(8,128)(2,1)}), bf16[16,336,128]{2,1,0:T(8,128)(2,1)S(1)}, u32[]{:S(2)}, u32[]{:S(2)}) async-start(bf16[16,336,128]{2,1,0:T(8,128)(2,1)} %get-tuple-element.26), calls=%async_computation | async-start | bytes 2752512 | tf_op jit(solution)/shard_map/all_to_all | solution.py:274
  10.5 15.0 %collective-permute-start.1 = (bf16[4,64,256]{2,1,0:T(8,128)(2,1)S(1)}, bf16[4,64,256]{2,1,0:T(8,128)(2,1)S(1)}, u32[]{:S(2)}, u32[]{:S(2)}) collective-permute-start(bf16[4,64,256]{2,1,0:T(8,128)(2,1)S(1)} %bitcast.24), channel_id=1, source_target_pairs={{0,1},{1,2},{2,3},{3,4},{4,5},{5,6},{6,7},{7,8},{8,9},{9,10},{10,1... | collective-permute-start | bytes 393224 | tf_op jit(solution)/shard_map/ppermute | solution.py:408
  14.9 10.6 %collective-permute-start.2 = (bf16[4,64,256]{2,1,0:T(8,128)(2,1)S(1)}, bf16[4,64,256]{2,1,0:T(8,128)(2,1)S(1)}, u32[]{:S(2)}, u32[]{:S(2)}) collective-permute-start(bf16[4,64,256]{2,1,0:T(8,128)(2,1)S(1)} %bitcast.25), channel_id=1, source_target_pairs={{1,0},{2,1},{3,2},{4,3},{5,4},{6,5},{7,6},{8,7},{9,8},{10,9},{11,1... | collective-permute-start | bytes 393224 | tf_op jit(solution)/shard_map/ppermute | solution.py:408
  16.9 5.1 %collective-permute-start = (bf16[1,64,256]{2,1,0:T(8,128)(2,1)S(1)}, bf16[1,64,256]{2,1,0:T(8,128)(2,1)S(1)}, u32[]{:S(2)}, u32[]{:S(2)}) collective-permute-start(bf16[1,64,256]{2,1,0:T(8,128)(2,1)S(1)} %get-tuple-element.50), channel_id=1, source_target_pairs={{0,2},{1,3},{2,4},{3,5},{4,6},{5,7},{6,8},{7,9},{8,10},{9,11},{10,... | collective-permute-start | bytes 98312 | tf_op jit(solution)/shard_map/ppermute | solution.py:408
  20.4 5.1 %collective-permute-start.3 = (bf16[1,64,256]{2,1,0:T(8,128)(2,1)S(1)}, bf16[1,64,256]{2,1,0:T(8,128)(2,1)S(1)}, u32[]{:S(2)}, u32[]{:S(2)}) collective-permute-start(bf16[1,64,256]{2,1,0:T(8,128)(2,1)S(1)} %get-tuple-element.49), channel_id=1, source_target_pairs={{2,0},{3,1},{4,2},{5,3},{6,4},{7,5},{8,6},{9,7},{10,8},{11,9},{12,... | collective-permute-start | bytes 98312 | tf_op jit(solution)/shard_map/ppermute | solution.py:408
  29.6 28.5 %all-to-all-start.1 = ((bf16[4,162,128]{2,1,0:T(8,128)(2,1)}), bf16[4,162,128]{2,1,0:T(8,128)(2,1)S(1)}, u32[]{:S(2)}, u32[]{:S(2)}) async-start(bf16[4,162,128]{2,1,0:T(8,128)(2,1)} %get-tuple-element.33), calls=%async_computation.1 | async-start | bytes 344064 | tf_op jit(solution)/shard_map/all_to_all | solution.py:394
  58.1 7.2 %collective-permute-start.4 = (bf16[2,162,128]{2,1,0:T(8,128)(2,1)S(1)}, bf16[2,162,128]{2,1,0:T(8,128)(2,1)S(1)}, u32[]{:S(2)}, u32[]{:S(2)}) collective-permute-start(bf16[2,162,128]{2,1,0:T(8,128)(2,1)S(1)} %constant_dynamic-slice_fusion.held), channel_id=1, source_target_pairs={{0,4},{1,5},{2,6},{3,7},{4,0},{5,1},{6,2},{7,3},{8,12},{9,13},{10,... | collective-permute-start | bytes 248840 | tf_op jit(solution)/shard_map/ppermute | solution.py:269
  63.2 26.0 %collective-permute-start.5 = (bf16[162,128]{1,0:T(8,128)(2,1)S(1)}, bf16[162,128]{1,0:T(8,128)(2,1)S(1)}, u32[]{:S(2)}, u32[]{:S(2)}) collective-permute-start(bf16[162,128]{1,0:T(8,128)(2,1)S(1)} %get-tuple-element.43), channel_id=1, source_target_pairs={{0,256},{16,272},{32,288},{48,304},{64,320},{80,336},{96,352},{112... | collective-permute-start | bytes 124424 | tf_op jit(solution)/shard_map/ppermute | solution.py:269
  89.2 29.3 %copy-start = (f32[336,128]{1,0:T(8,128)S(1)}, f32[336,128]{1,0:T(8,128)}, u32[]{:S(2)}) copy-start(f32[336,128]{1,0:T(8,128)} %get-tuple-element.39.rows) | copy-start | bytes 516100
  89.2 3.7 %collective-permute-start.6 = (bf16[8,162,128]{2,1,0:T(8,128)(2,1)S(1)}, bf16[8,162,128]{2,1,0:T(8,128)(2,1)S(1)}, u32[]{:S(2)}, u32[]{:S(2)}) collective-permute-start(bf16[8,162,128]{2,1,0:T(8,128)(2,1)S(1)} %get-tuple-element.46), channel_id=1, source_target_pairs={{0,1},{1,0},{2,3},{3,2},{4,5},{5,4},{6,7},{7,6},{8,9},{9,8},{10,11... | collective-permute-start | bytes 995336 | tf_op jit(solution)/shard_map/ppermute | solution.py:269

commit v10 on v9

--- a/solution.py
+++ b/solution.py
@@ -88,8 +88,8 @@
         store_window(win0, index, value)
 
     for block in range(SLABS):
-        slot = ((block >> 2) ^ (slab >> 2)) % 2 * 2 + block // 8
-        raw[block * ROWS : (block + 1) * ROWS, :] = held_ref[block % 4, slot].astype(jnp.float32)
+        piece = held_ref[block % 8, block // 8]
+        raw[block * ROWS : (block + 1) * ROWS, :] = piece.astype(jnp.float32)
 
     for layer in range(3):
         rows = raw[layer * K_ROWS : (layer + 1) * K_ROWS, :]
@@ -438,8 +438,7 @@
     across = move(moment_other, "trainer", lambda i: i ^ 16)
     held = lax.dynamic_slice_in_dim(got, info[0], 2, 0)
     both = held
-    held = jnp.concatenate([held, move(held, "depth", lambda i: i ^ 4)])
-    near = [list(range(first, first + 4)) for first in range(0, 16, 4)]
+    near = [list(range(first, first + 8)) for first in range(0, 16, 8)]
     held = lax.all_gather(held, "depth", axis_index_groups=near)
     generated, keep, send = local_step(
         slab.reshape(1), pieces, held, critic, critic_back, score

time: 120 us -> 116 us (0.967)
  waiting for transfers between devices: 19.7 us -> 7.54 us
  starting transfers between devices: 44.4 us -> 49.4 us
  blocking collectives: 42.3 us -> 45.7 us
    all_to_all x1, waiting for transfers between devices: 12.2 us -> 0.01 us  [far_exchange(): lax.all_to_all(slots, ('trainer', 'depth'), 0, 0, axis_index_groups=groups)]
    all_gather x1, blocking collectives: 16.8 us -> 23.3 us  [one_step(): held = lax.all_gather(held, 'depth', axis_index_groups=near)]
    ppermute x3 -> x2, starting transfers between devices: 9.3 us -> 14.3 us  [move(): return lax.ppermute(value, axis, [(i, target_of(i)) for i in range(count)])]
    all_to_all x1, blocking collectives: 25.5 us -> 22.4 us  [exchange_depth(): lax.all_to_all(mine.astype(jnp.bfloat16), 'depth', 0, 0, axis_index_group...]
  transfers between devices with their start and end apart: 9 -> 8, of which waited for: 4 -> 3; matrix products, arithmetic and copies ran while one was open for 0% -> 0% of each run, Pallas kernels for 6% -> 6%
where the time goes in v10:
time: 116 us
  starting transfers between devices  49.4 us (43%)
  blocking collectives  45.7 us (39%)
  Pallas kernels  12 us (10%)
  waiting for transfers between devices  7.54 us (6%)
    all_gather x1, blocking collectives, one_step(): held = lax.all_gather(held, 'depth', axis_index_groups=near)  23.3 us
    all_to_all x1, blocking collectives, exchange_depth(): lax.all_to_all(mine.astype(jnp.bfloat16), 'depth', 0, 0, axis_index_group...  22.4 us
    all_to_all x1, starting transfers between devices, far_exchange(): lax.all_to_all(slots, ('trainer', 'depth'), 0, 0, axis_index_groups=groups)  16.2 us
    ppermute x2, starting transfers between devices, move(): return lax.ppermute(value, axis, [(i, target_of(i)) for i in range(count)])  14.3 us
    ppermute x4, starting transfers between devices, shifted(): return lax.ppermute(value, 'depth', links)  11.1 us
    all_to_all x1, starting transfers between devices, plane_exchange(): return lax.all_to_all(slots, 'trainer', 0, 0, axis_index_groups=groups)  7.72 us
    pallas_call x1, Pallas kernels, local_step(): pl.pallas_call(local_kernel, out_shape=(jax.ShapeDtypeStruct((PLANES, CH,...  6.93 us
    ppermute x4, waiting for transfers between devices, shifted(): return lax.ppermute(value, 'depth', links)  3.64 us
  transfers between devices with their start and end apart: 8, of which 3 were waited for; matrix products, arithmetic and copies ran while one was open for 0% of the time, Pallas kernels for 6%

profile of v10, /device:TPU:1, one launch (start us, length us, event | category | flops | bytes accessed | tf_op | source)
XLA Modules:
  0.0 116.0 jit_solution(13959524501633247195)
XLA Ops:
  0.6 2.1 %pack_slots.1 = (bf16[16,336,128]{2,1,0:T(8,128)(2,1)}, f32[336,128]{1,0:T(8,128)}) custom-call(f32[1,20736]{1,0:T(1,128)} %weight_ref.1, f32[1,20736]{1,0:T(1,128)} %moment_ref.1), custom_call_target="tpu_custom_call" | custom-call | flops 100000 | bytes 1500000 | tf_op jit(solution)/shard_map/pack_slots/pallas_call | solution.py:290
  2.8 0.0 copy-start.1
  2.8 0.0 copy-start.4
  2.8 0.0 copy-start.5
  2.8 0.0 copy-start.2
  2.8 0.0 copy-start.3
  2.8 7.7 %all-to-all-start = ((bf16[16,336,128]{2,1,0:T(8,128)(2,1)}), bf16[16,336,128]{2,1,0:T(8,128)(2,1)S(1)}, u32[]{:S(2)}, u32[]{:S(2)}) async-start(bf16[16,336,128]{2,1,0:T(8,128)(2,1)} %get-tuple-element.26), calls=%async_computation | async-start | bytes 2752512 | tf_op jit(solution)/shard_map/all_to_all | solution.py:274
  10.5 0.0 copy-done.1
  10.5 4.4 %collective-permute-start.1 = (bf16[4,64,256]{2,1,0:T(8,128)(2,1)S(1)}, bf16[4,64,256]{2,1,0:T(8,128)(2,1)S(1)}, u32[]{:S(2)}, u32[]{:S(2)}) collective-permute-start(bf16[4,64,256]{2,1,0:T(8,128)(2,1)S(1)} %bitcast.24), channel_id=1, source_target_pairs={{0,1},{1,2},{2,3},{3,4},{4,5},{5,6},{6,7},{7,8},{8,9},{9,10},{10,1... | collective-permute-start | bytes 393224 | tf_op jit(solution)/shard_map/ppermute | solution.py:408
  14.9 1.9 %collective-permute-start.2 = (bf16[4,64,256]{2,1,0:T(8,128)(2,1)S(1)}, bf16[4,64,256]{2,1,0:T(8,128)(2,1)S(1)}, u32[]{:S(2)}, u32[]{:S(2)}) collective-permute-start(bf16[4,64,256]{2,1,0:T(8,128)(2,1)S(1)} %bitcast.25), channel_id=1, source_target_pairs={{1,0},{2,1},{3,2},{4,3},{5,4},{6,5},{7,6},{8,7},{9,8},{10,9},{11,1... | collective-permute-start | bytes 393224 | tf_op jit(solution)/shard_map/ppermute | solution.py:408
  16.9 3.5 %collective-permute-start = (bf16[1,64,256]{2,1,0:T(8,128)(2,1)S(1)}, bf16[1,64,256]{2,1,0:T(8,128)(2,1)S(1)}, u32[]{:S(2)}, u32[]{:S(2)}) collective-permute-start(bf16[1,64,256]{2,1,0:T(8,128)(2,1)S(1)} %get-tuple-element.50), channel_id=1, source_target_pairs={{0,2},{1,3},{2,4},{3,5},{4,6},{5,7},{6,8},{7,9},{8,10},{9,11},{10,... | collective-permute-start | bytes 98312 | tf_op jit(solution)/shard_map/ppermute | solution.py:408
  20.4 1.3 %collective-permute-start.3 = (bf16[1,64,256]{2,1,0:T(8,128)(2,1)S(1)}, bf16[1,64,256]{2,1,0:T(8,128)(2,1)S(1)}, u32[]{:S(2)}, u32[]{:S(2)}) collective-permute-start(bf16[1,64,256]{2,1,0:T(8,128)(2,1)S(1)} %get-tuple-element.49), channel_id=1, source_target_pairs={{2,0},{3,1},{4,2},{5,3},{6,4},{7,5},{8,6},{9,7},{10,8},{11,9},{12,... | collective-permute-start | bytes 98312 | tf_op jit(solution)/shard_map/ppermute | solution.py:408
  21.7 0.0 copy-done.4
  21.7 0.1 copy.18
  21.9 0.0 collective-permute-done.far_low
  21.9 3.6 %collective-permute-done.3.far_high = bf16[1,64,256]{2,1,0:T(8,128)(2,1)S(1)} collective-permute-done((bf16[1,64,256]{2,1,0:T(8,128)(2,1)S(1)}, bf16[1,64,256]{2,1,0:T(8,128)(2,1)S(1)}, u32[]{:S(2)}, u32[]{:S(2)}) %collective-permute-start.3) | collective-permute-done | bytes 32800 | tf_op jit(solution)/shard_map/ppermute | solution.py:408
  25.6 0.0 collective-permute-done.1.low
  25.6 0.0 collective-permute-done.2.high
  25.6 2.4 %all-to-all-done.heard = bf16[16,336,128]{2,1,0:T(8,128)(2,1)S(1)} async-done(((bf16[16,336,128]{2,1,0:T(8,128)(2,1)}), bf16[16,336,128]{2,1,0:T(8,128)(2,1)S(1)}, u32[]{:S(2)}, u32[]{:S(2)}) %all-to-all-start) | async-done | bytes 1376288 | tf_op jit(solution)/shard_map/all_to_all | solution.py:274
  28.0 0.0 copy-done.5
  28.0 0.1 broadcast_in_dim.11.score_ref
  28.1 0.0 copy-done.2
  28.1 0.0 copy-done.3
  28.1 1.5 %pick_slots.1 = (bf16[4,162,128]{2,1,0:T(8,128)(2,1)}, bf16[162,128]{1,0:T(8,128)(2,1)S(1)}, bf16[162,128]{1,0:T(8,128)(2,1)S(1)}, s32[4]{0:T(128)S(1)}) custom-call(s32[32]{0:T(128)S(1)} %copy-done.2, s32[32]{0:T(128)S(1)} %copy-done.3, bf16[16,336,128]{2,1,0:T(8,128)(2,1)S(1)} %all-to-all-done.heard), custom_call_target="tpu_custom_call" | custom-call | flops 100000 | bytes 400000 | tf_op jit(solution)/shard_map/pick_slots/pallas_call | solution.py:366
  29.6 16.2 %all-to-all-start.1 = ((bf16[4,162,128]{2,1,0:T(8,128)(2,1)}), bf16[4,162,128]{2,1,0:T(8,128)(2,1)S(1)}, u32[]{:S(2)}, u32[]{:S(2)}) async-start(bf16[4,162,128]{2,1,0:T(8,128)(2,1)} %get-tuple-element.33), calls=%async_computation.1 | async-start | bytes 344064 | tf_op jit(solution)/shard_map/all_to_all | solution.py:394
  45.9 0.1 copy.19.critic_ref
  46.0 12.1 %collective-permute-start.4 = (bf16[162,128]{1,0:T(8,128)(2,1)S(1)}, bf16[162,128]{1,0:T(8,128)(2,1)S(1)}, u32[]{:S(2)}, u32[]{:S(2)}) collective-permute-start(bf16[162,128]{1,0:T(8,128)(2,1)S(1)} %get-tuple-element.43), channel_id=1, source_target_pairs={{0,256},{16,272},{32,288},{48,304},{64,320},{80,336},{96,352},{112... | collective-permute-start | bytes 124424 | tf_op jit(solution)/shard_map/ppermute | solution.py:269
  58.2 0.0 all-to-all-done.1
  58.2 23.3 %all-gather = bf16[16,162,128]{2,1,0:T(8,128)(2,1)S(1)} all-gather(bf16[2,162,128]{2,1,0:T(8,128)(2,1)S(1)} %constant_dynamic-slice_fusion.held), channel_id=2, replica_groups={{0,1,2,3,4,5,6,7},{8,9,10,11,12,13,14,15},{16,17,18,19,20,21,22,23},{24..., dimensions={0}, use_global_device_ids=true | all-gather | bytes 746496 | tf_op jit(solution)/shard_map/all_gather | solution.py:442
  81.5 6.9 %local_step.1 = (bf16[4,64,256]{2,1,0:T(8,128)(2,1)}, f32[8,162,128]{2,1,0:T(8,128)S(1)}, bf16[8,162,128]{2,1,0:T(8,128)(2,1)S(1)}) custom-call(s32[1]{0:T(128)} %bitcast.slab_ref, bf16[1,64,256]{2,1,0:T(8,128)(2,1)S(1)} %collective-permute-done.far_low, bf16[4,64,256]{2,1,0:T(8,128)(2,1)S(1)} %collective-permute-done.1.low, ...), custom_call_target="tpu_custom_call" | custom-call | flops 6000000000 | bytes 4000000 | tf_op jit(solution)/shard_map/local_step/pallas_call | solution.py:234
  88.4 0.0 copy-start
  88.4 0.0 collective-permute-done.4.across
  88.4 2.2 %collective-permute-start.5 = (bf16[8,162,128]{2,1,0:T(8,128)(2,1)S(1)}, bf16[8,162,128]{2,1,0:T(8,128)(2,1)S(1)}, u32[]{:S(2)}, u32[]{:S(2)}) collective-permute-start(bf16[8,162,128]{2,1,0:T(8,128)(2,1)S(1)} %get-tuple-element.46), channel_id=1, source_target_pairs={{0,1},{1,0},{2,3},{3,2},{4,5},{5,4},{6,7},{7,6},{8,9},{9,8},{10,11... | collective-permute-start | bytes 995336 | tf_op jit(solution)/shard_map/ppermute | solution.py:269
  90.6 1.5 %collective-permute-done.5 = bf16[8,162,128]{2,1,0:T(8,128)(2,1)S(1)} collective-permute-done((bf16[8,162,128]{2,1,0:T(8,128)(2,1)S(1)}, bf16[8,162,128]{2,1,0:T(8,128)(2,1)S(1)}, u32[]{:S(2)}, u32[]{:S(2)}) %collective-permute-start.5) | collective-permute-done | bytes 331808 | tf_op jit(solution)/shard_map/ppermute | solution.py:269
  92.1 0.1 add_convert_fusion
  92.2 22.4 %all_to_all.15.heard = bf16[8,162,128]{2,1,0:T(8,128)(2,1)S(1)} all-to-all(bf16[8,162,128]{2,1,0:T(8,128)(2,1)S(1)} %add_convert_fusion), channel_id=1, replica_groups={{0,2,4,6,8,10,12,14},{1,3,5,7,9,11,13,15},{16,18,20,22,24,26,28,30},{17..., dimensions={0} | all-to-all | bytes 663552 | tf_op jit(solution)/shard_map/all_to_all | solution.py:400
  114.6 0.0 copy-done
  114.6 1.4 %update.1 = (f32[1,20736]{1,0:T(1,128)}, f32[1,20736]{1,0:T(1,128)}) custom-call(s32[4]{0:T(128)S(1)} %get-tuple-element.34.info, f32[336,128]{1,0:T(8,128)S(1)} %copy-done, bf16[2,162,128]{2,1,0:T(8,128)(2,1)S(1)} %constant_dynamic-slice_fusion.held, bf16[162,128]{1,0:T(8,128)(2,1)S(1)} %get-tuple-element.40.moment_own, ...), custom_call_target="tpu_custom_call" | custom-call | flops 500000 | bytes 1000000 | tf_op jit(solution)/shard_map/update/pallas_call | solution.py:326
  (4 shorter events, 0.1 us)
Async XLA Ops:
  2.8 7.8 %copy-start.1 = (bf16[1,4,64,256]{3,2,1,0:T(8,128)(2,1)S(1)}, bf16[1,4,64,256]{3,2,1,0:T(8,128)(2,1)}, u32[]{:S(2)}) copy-start(bf16[1,4,64,256]{3,2,1,0:T(8,128)(2,1)} %param.7) | copy-start | bytes 393220
  2.8 19.0 %copy-start.4 = (bf16[1,8,128,64]{2,3,1,0:T(8,128)(2,1)S(1)}, bf16[1,8,128,64]{2,3,1,0:T(8,128)(2,1)}, u32[]{:S(2)}) copy-start(bf16[1,8,128,64]{2,3,1,0:T(8,128)(2,1)} %param.10) | copy-start | bytes 393220
  2.8 25.2 %copy-start.5 = (f32[1,128]{1,0:T(1,128)S(1)}, f32[1,128]{1,0:T(1,128)}, u32[]{:S(2)}) copy-start(f32[1,128]{1,0:T(1,128)} %param.11) | copy-start | bytes 1540
  2.8 25.3 %copy-start.2 = (s32[32]{0:T(128)S(1)}, s32[32]{0:T(128)}, u32[]{:S(2)}) copy-start(s32[32]{0:T(128)} %pairing.1) | copy-start | bytes 388
  2.8 25.3 %copy-start.3 = (s32[32]{0:T(128)S(1)}, s32[32]{0:T(128)}, u32[]{:S(2)}) copy-start(s32[32]{0:T(128)} %flags.1) | copy-start | bytes 388
  2.8 25.2 %all-to-all-start = ((bf16[16,336,128]{2,1,0:T(8,128)(2,1)}), bf16[16,336,128]{2,1,0:T(8,128)(2,1)S(1)}, u32[]{:S(2)}, u32[]{:S(2)}) async-start(bf16[16,336,128]{2,1,0:T(8,128)(2,1)} %get-tuple-element.26), calls=%async_computation | async-start | bytes 2752512 | tf_op jit(solution)/shard_map/all_to_all | solution.py:274
  10.5 15.0 %collective-permute-start.1 = (bf16[4,64,256]{2,1,0:T(8,128)(2,1)S(1)}, bf16[4,64,256]{2,1,0:T(8,128)(2,1)S(1)}, u32[]{:S(2)}, u32[]{:S(2)}) collective-permute-start(bf16[4,64,256]{2,1,0:T(8,128)(2,1)S(1)} %bitcast.24), channel_id=1, source_target_pairs={{0,1},{1,2},{2,3},{3,4},{4,5},{5,6},{6,7},{7,8},{8,9},{9,10},{10,1... | collective-permute-start | bytes 393224 | tf_op jit(solution)/shard_map/ppermute | solution.py:408
  14.9 10.6 %collective-permute-start.2 = (bf16[4,64,256]{2,1,0:T(8,128)(2,1)S(1)}, bf16[4,64,256]{2,1,0:T(8,128)(2,1)S(1)}, u32[]{:S(2)}, u32[]{:S(2)}) collective-permute-start(bf16[4,64,256]{2,1,0:T(8,128)(2,1)S(1)} %bitcast.25), channel_id=1, source_target_pairs={{1,0},{2,1},{3,2},{4,3},{5,4},{6,5},{7,6},{8,7},{9,8},{10,9},{11,1... | collective-permute-start | bytes 393224 | tf_op jit(solution)/shard_map/ppermute | solution.py:408
  16.9 5.1 %collective-permute-start = (bf16[1,64,256]{2,1,0:T(8,128)(2,1)S(1)}, bf16[1,64,256]{2,1,0:T(8,128)(2,1)S(1)}, u32[]{:S(2)}, u32[]{:S(2)}) collective-permute-start(bf16[1,64,256]{2,1,0:T(8,128)(2,1)S(1)} %get-tuple-element.50), channel_id=1, source_target_pairs={{0,2},{1,3},{2,4},{3,5},{4,6},{5,7},{6,8},{7,9},{8,10},{9,11},{10,... | collective-permute-start | bytes 98312 | tf_op jit(solution)/shard_map/ppermute | solution.py:408
  20.4 5.1 %collective-permute-start.3 = (bf16[1,64,256]{2,1,0:T(8,128)(2,1)S(1)}, bf16[1,64,256]{2,1,0:T(8,128)(2,1)S(1)}, u32[]{:S(2)}, u32[]{:S(2)}) collective-permute-start(bf16[1,64,256]{2,1,0:T(8,128)(2,1)S(1)} %get-tuple-element.49), channel_id=1, source_target_pairs={{2,0},{3,1},{4,2},{5,3},{6,4},{7,5},{8,6},{9,7},{10,8},{11,9},{12,... | collective-permute-start | bytes 98312 | tf_op jit(solution)/shard_map/ppermute | solution.py:408
  29.6 28.5 %all-to-all-start.1 = ((bf16[4,162,128]{2,1,0:T(8,128)(2,1)}), bf16[4,162,128]{2,1,0:T(8,128)(2,1)S(1)}, u32[]{:S(2)}, u32[]{:S(2)}) async-start(bf16[4,162,128]{2,1,0:T(8,128)(2,1)} %get-tuple-element.33), calls=%async_computation.1 | async-start | bytes 344064 | tf_op jit(solution)/shard_map/all_to_all | solution.py:394
  46.0 42.4 %collective-permute-start.4 = (bf16[162,128]{1,0:T(8,128)(2,1)S(1)}, bf16[162,128]{1,0:T(8,128)(2,1)S(1)}, u32[]{:S(2)}, u32[]{:S(2)}) collective-permute-start(bf16[162,128]{1,0:T(8,128)(2,1)S(1)} %get-tuple-element.43), channel_id=1, source_target_pairs={{0,256},{16,272},{32,288},{48,304},{64,320},{80,336},{96,352},{112... | collective-permute-start | bytes 124424 | tf_op jit(solution)/shard_map/ppermute | solution.py:269
  88.4 26.2 %copy-start = (f32[336,128]{1,0:T(8,128)S(1)}, f32[336,128]{1,0:T(8,128)}, u32[]{:S(2)}) copy-start(f32[336,128]{1,0:T(8,128)} %get-tuple-element.39.rows) | copy-start | bytes 516100
  88.4 3.7 %collective-permute-start.5 = (bf16[8,162,128]{2,1,0:T(8,128)(2,1)S(1)}, bf16[8,162,128]{2,1,0:T(8,128)(2,1)S(1)}, u32[]{:S(2)}, u32[]{:S(2)}) collective-permute-start(bf16[8,162,128]{2,1,0:T(8,128)(2,1)S(1)} %get-tuple-element.46), channel_id=1, source_target_pairs={{0,1},{1,0},{2,3},{3,2},{4,5},{5,4},{6,7},{7,6},{8,9},{9,8},{10,11... | collective-permute-start | bytes 995336 | tf_op jit(solution)/shard_map/ppermute | solution.py:269
